TPU v7x, 32 devices: a whole 2x2x4 slice. The times are simulated.
32 devices in a mesh: gx: 2 (over core), gy: 4 (over y, x), gz: 4 (over z).
Axes of the slice: x: 2, y: 2, z: 4, core: 2. Of those that a mesh axis runs over, the one named last changes fastest.
Arguments:
- particles: float32 [128, 8, 128], P(('gx', 'gy', 'gz')), as said below
- local_pairs: int32 [128, 2], P(('gx', 'gy', 'gz')), may hold values from 0 to 3, as said below
- cross_pairs: int32 [64, 2], P(('gx', 'gy', 'gz')), may hold values from 0 to 3
- drag_cell: int32 [128, 128], P(('gx', 'gy', 'gz')), may hold values from 0 to 65535
- drag_share: float32 [128, 128], P(('gx', 'gy', 'gz')), may hold values from 0 to 1
- fluid: float32 [3, 16, 256, 512], P(None, 'gx', 'gy', 'gz'), may hold values from -6 to 6
Outputs:
- particle_force: float32 [128, 3, 128], P(('gx', 'gy', 'gz'))
- fluid_next: float32 [3, 16, 256, 512], P(None, 'gx', 'gy', 'gz')
Inputs may be any that keep to these rules, and one draw needn't show every extreme that they name: `particles`: positions lie in 0 to 4 along each direction, radii in 0.3 to 0.6, elastic moduli in 0.5 to 2. `local_pairs`: each row names two different local blocks of its device; a pair may be listed more than once. `cross_pairs`: row entries: a local block of the listing device, then a local block of the device above it along the bed height; lists of devices at the top of gx have no partner and contribute nothing. `drag_cell`: index height * 64 * 128 + first lateral * 128 + second lateral within the owning device's cells.
All inputs are finite; a program needn't handle non-finite values.
Results may differ from a plain program's by a relative error of at most 0.00002.
Values sent between devices are 32-bit elements; how exact they have to be, the bound alone decides.
No kernel may reach another device: no remote copies, remote signals or barrier semaphores. Data moves between devices by JAX's collectives and lax.ppermute only.
A program may use at most 256 MiB of HBM per device.

v0:
```python
import math

import jax
import jax.numpy as jnp
from jax import lax
from jax.sharding import PartitionSpec as P

soft_core = 0.01
damp_normal = 0.3
damp_tangent = 0.2
drag_coef = 1.5
diffuse = 0.1
source_gain = 0.5


def with_halo(block, sides, width):
    for axis, dim in sides:
        count = lax.axis_size(axis)
        forward = [(i, i + 1) for i in range(count - 1)]
        backward = [(target, source) for source, target in forward]
        low = lax.ppermute(
            lax.slice_in_dim(block, block.shape[dim] - width, None, axis=dim), axis, forward
        )
        high = lax.ppermute(lax.slice_in_dim(block, 0, width, axis=dim), axis, backward)
        block = jnp.concatenate([low, block, high], axis=dim)
    return block


def shifted(block, axis, distance):
    devices = range(lax.axis_size(axis))
    route = [(i - distance, i) for i in devices if i - distance in devices]
    return lax.ppermute(block, axis, route)


def pair_force(left, right):
    offset = left[0:3][:, :, None] - right[0:3][:, None, :]
    distance = jnp.sqrt(jnp.sum(offset * offset, axis=0) + soft_core)
    normal = offset / distance
    radius_left = left[6][:, None]
    radius_right = right[6][None, :]
    modulus_left = left[7][:, None]
    modulus_right = right[7][None, :]
    intersection = jnp.maximum(radius_left + radius_right - distance, 0.0)
    radius_eff = radius_left * radius_right / (radius_left + radius_right)
    modulus_eff = modulus_left * modulus_right / (modulus_left + modulus_right)
    stiffness = 2.0 * modulus_eff * jnp.sqrt(radius_eff * intersection)
    relative = left[3:6][:, :, None] - right[3:6][:, None, :]
    normal_speed = jnp.sum(relative * normal, axis=0)
    tangent = relative - normal_speed * normal
    pairwise = (
        stiffness * (intersection * (2.0 / 3.0) - damp_normal * normal_speed) * normal
        - damp_tangent * stiffness * tangent
    )
    return (jnp.sum(pairwise, axis=2), -jnp.sum(pairwise, axis=1))


def grouped(operands):
    count = operands[0].shape[0]
    group_size = math.gcd(8, count)
    shaped = tuple(
        (item.reshape((count // group_size, group_size) + item.shape[1:]) for item in operands)
    )
    result = lax.map(lambda group: jax.vmap(pair_force)(*group), shaped)
    return tuple((item.reshape((count,) + item.shape[2:]) for item in result))


def block_forces(own, above, local_list, cross_list):
    self_force = grouped((own, own))[0]
    first = local_list[:, 0]
    second = local_list[:, 1]
    near_force, near_react = grouped((own[first], own[second]))
    force = self_force.at[first].add(near_force).at[second].add(near_react)
    mine = cross_list[:, 0]
    theirs = cross_list[:, 1]
    cross_force, cross_react = grouped((own[mine], above[theirs]))
    force = force.at[mine].add(cross_force)
    reaction = jnp.zeros_like(force).at[theirs].add(cross_react)
    return (force, reaction)


def body(particles, local_pairs, cross_pairs, drag_cell, drag_share, fluid):
    depth = fluid.shape[1]
    across_count = fluid.shape[2]
    along_count = fluid.shape[3]
    layer = across_count * along_count
    padded = with_halo(fluid, (("gx", 1), ("gy", 2), ("gz", 3)), 1)
    height = drag_cell // layer
    across = drag_cell // along_count % across_count
    along = drag_cell % along_count
    lower_index = ((height + 1) * (across_count + 2) + across + 1) * (along_count + 2) + along + 1
    upper_index = lower_index + (across_count + 2) * (along_count + 2)
    flat = padded.reshape(3, -1)
    interp = (1.0 - drag_share) * flat[:, lower_index] + drag_share * flat[:, upper_index]
    drag = (
        drag_coef
        * particles[:, 6, :][:, None, :]
        * (jnp.transpose(interp, (1, 0, 2)) - particles[:, 3:6, :])
    )
    terms = -jnp.transpose(drag, (1, 0, 2))
    deposit = jnp.zeros((3, (depth + 1) * layer), jnp.float32)
    deposit = deposit.at[:, drag_cell].add((1.0 - drag_share) * terms)
    deposit = deposit.at[:, drag_cell + layer].add(drag_share * terms)
    rim = deposit[:, depth * layer :].reshape(3, across_count, along_count)
    above = shifted(particles, "gx", -1)
    force, reaction = block_forces(particles, above, local_pairs, cross_pairs)
    returned, rim_below = shifted((reaction, rim), "gx", 1)
    force = force + returned
    source = deposit[:, : depth * layer].reshape(3, depth, across_count, along_count)
    source = source.at[:, 0].add(rim_below)
    beside = padded[:, 2:, 1:-1, 1:-1] + padded[:, :-2, 1:-1, 1:-1]
    beside = beside + padded[:, 1:-1, 2:, 1:-1] + padded[:, 1:-1, :-2, 1:-1]
    beside = beside + padded[:, 1:-1, 1:-1, 2:] + padded[:, 1:-1, 1:-1, :-2]
    fluid_next = fluid + diffuse * (beside - 6.0 * fluid) + source_gain * source
    return (force + drag, fluid_next)


def solution(mesh):
    in_specs = (
        P(("gx", "gy", "gz"), None, None),
        P(("gx", "gy", "gz"), None),
        P(("gx", "gy", "gz"), None),
        P(("gx", "gy", "gz"), None),
        P(("gx", "gy", "gz"), None),
        P(None, "gx", "gy", "gz"),
    )
    out_specs = (P(("gx", "gy", "gz"), None, None), P(None, "gx", "gy", "gz"))
    return jax.shard_map(body, mesh=mesh, in_specs=in_specs, out_specs=out_specs, check_vma=False)
```

profile of v0, /device:TPU:10, one launch (start us, length us, event | category | flops | bytes accessed | tf_op | source)
XLA Modules:
  0.0 257.8 jit_solution(6869366451549435483)
XLA Ops:
  1.6 1.7 collective-permute-start.2
  19.9 1.5 pad_maximum_fusion.9
  21.5 3.4 %collective-permute-start.4 = (f32[3,10,1,128]{3,1,2,0:T(8,128)S(1)}, f32[3,10,1,128]{3,1,2,0:T(8,128)}, u32[]{:S(2)}, u32[]{:S(2)}) collective-permute-start(f32[3,10,1,128]{3,1,2,0:T(8,128)S(1)} %copy.140), channel_id=1, source_target_pairs={{0,4},{4,8},{8,12},{1,5},{5,9},{9,13},{2,6},{6,10},{10,14},{3,7},{... | collective-permute-start | bytes 46088 | tf_op jit(solution)/shard_map/ppermute | solution.py:21
  25.5 3.0 %collective-permute-start.5 = (f32[3,10,1,128]{3,1,2,0:T(8,128)}, f32[3,10,1,128]{3,1,2,0:T(8,128)}, u32[]{:S(2)}, u32[]{:S(2)}) collective-permute-start(f32[3,10,1,128]{3,1,2,0:T(8,128)} %copy.141), channel_id=1, source_target_pairs={{4,0},{8,4},{12,8},{5,1},{9,5},{13,9},{6,2},{10,6},{14,10},{7,3},{... | collective-permute-start | bytes 46088 | tf_op jit(solution)/shard_map/ppermute | solution.py:24
  29.5 2.4 copy.112
  31.9 1.9 copy.111
  33.8 3.0 %copy.113 = f32[3,10,1,128]{2,1,3,0:T(8,128)} copy(f32[3,10,1,128]{3,1,2,0:T(8,128)} %collective-permute-done.5) | data formatting | bytes 30720 | tf_op jit(solution)/shard_map/ppermute | solution.py:24
  36.8 1.6 pad_maximum_fusion.13
  38.4 3.5 %collective-permute-start.6 = (f32[3,10,66,1]{2,1,3,0:T(8,128)}, f32[3,10,66,1]{2,1,3,0:T(8,128)}, u32[]{:S(2)}, u32[]{:S(2)}) collective-permute-start(f32[3,10,66,1]{2,1,3,0:T(8,128)} %get-tuple-element.86), channel_id=1, source_target_pairs={{0,1},{1,2},{2,3},{4,5},{5,6},{6,7},{8,9},{9,10},{10,11},{12,13},{... | collective-permute-start | bytes 23768 | tf_op jit(solution)/shard_map/ppermute | solution.py:21
  41.9 3.0 %collective-permute-start.7 = (f32[3,10,66,1]{2,1,3,0:T(8,128)}, f32[3,10,66,1]{2,1,3,0:T(8,128)}, u32[]{:S(2)}, u32[]{:S(2)}) collective-permute-start(f32[3,10,66,1]{2,1,3,0:T(8,128)} %get-tuple-element.87), channel_id=1, source_target_pairs={{1,0},{2,1},{3,2},{5,4},{6,5},{7,6},{9,8},{10,9},{11,10},{13,12},{... | collective-permute-start | bytes 23768 | tf_op jit(solution)/shard_map/ppermute | solution.py:24
  46.6 2.1 collective-permute-start.1
  48.8 6.2 %pad_maximum_fusion = f32[3,10,66,130]{2,1,3,0:T(8,128)} fusion(f32[3,10,66,1]{2,1,3,0:T(8,128)} %collective-permute-done.7, f32[3,10,1,128]{2,1,3,0:T(8,128)} %copy.113, f32[3,10,64,128]{2,1,3,0:T(8,128)} %copy.112, f32[3,10,1,128]{2,1,3,0:T(8,128)S(1)} %copy.111, f32[3,10,66,1]{2,1,3,0:T(8,128)} %collective-permute-done.6), kind=kLoop, calls=%fused_computation.14 | loop fusion | flops 1029600 | bytes 2059200 | tf_op jit(solution)/shard_map/concatenate | solution.py:25
  55.0 4.7 %copy.114 = f32[3,10,66,130]{3,2,1,0:T(8,128)} copy(f32[3,10,66,130]{2,1,3,0:T(8,128)} %pad_maximum_fusion) | data formatting | bytes 2059200 | tf_op jit(solution)/shard_map/concatenate | solution.py:25
  59.7 4.4 %reshape.186 = f32[3,85800]{1,0:T(4,128)} reshape(f32[3,10,66,130]{3,2,1,0:T(8,128)} %copy.114) | data formatting | bytes 2059200 | tf_op jit(solution)/shard_map/reshape | solution.py:92
  64.1 20.7 %copy.115 = f32[3,85800]{0,1:T(8,128)} copy(f32[3,85800]{1,0:T(4,128)} %reshape.186) | data formatting | bytes 2059200 | tf_op jit(solution)/shard_map/reshape | solution.py:92
  84.8 15.2 %gather_fusion.2 = f32[512,3]{1,0:T(8,128)} fusion(f32[3,85800]{0,1:T(8,128)} %copy.115, s32[1024]{0:T(1024)S(1)} %copy-done.25), kind=kCustom, calls=%fused_computation.2 | custom fusion | bytes 14336 | tf_op jit(solution)/shard_map/gather | solution.py:93
  101.1 15.2 %gather_fusion.3 = f32[512,3]{1,0:T(8,128)} fusion(f32[3,85800]{0,1:T(8,128)} %copy.115, s32[1024]{0:T(1024)S(1)} %copy-done.24), kind=kCustom, calls=%fused_computation.3 | custom fusion | bytes 14336 | tf_op jit(solution)/shard_map/gather | solution.py:93
  121.2 17.5 %scatter_custom_fusion.4 = f32[3,73728]{0,1:T(8,128)} fusion(s32[512]{0:T(512)} %get-tuple-element.125, f32[512,3]{1,0:T(8,128)} %copy.129, f32[]{:T(128)} %constant.167.clone.1), kind=kCustom, calls=%fused_computation.12 | custom fusion | flops 1536 | bytes 885248 | tf_op jit(solution)/shard_map/scatter-add | solution.py:101
  138.6 27.6 %scatter_fusion.4 = f32[3,73728]{0,1:T(8,128)} fusion(f32[3,73728]{0,1:T(8,128)} %scatter_custom_fusion.4, s32[512]{0:T(512)S(1)} %copy-done.26, f32[512,3]{1,0:T(8,128)} %copy.130), kind=kCustom, calls=%fused_computation.11 | custom fusion | flops 1536 | bytes 20480 | tf_op jit(solution)/shard_map/scatter-add | solution.py:102
  166.2 4.4 %slice.252 = f32[3,8192]{0,1:T(8,128)} slice(f32[3,73728]{0,1:T(8,128)} %scatter_fusion.4), slice={[0:3], [65536:73728]} | slice | bytes 196608 | tf_op jit(solution)/shard_map/slice | solution.py:103
  170.6 4.4 %copy.132 = f32[3,64,128]{1,2,0:T(8,128)} copy(f32[3,64,128]{0,2,1:T(8,128)} %bitcast.42) | data formatting | bytes 196608 | tf_op jit(solution)/shard_map/reshape | solution.py:103
  175.0 2.0 collective-permute-start.8
  177.0 1.8 fusion.31
  178.8 2.8 %copy.128 = f32[3,8,64,128]{2,1,3,0:T(8,128)} copy(f32[3,8,64,128]{3,2,1,0:T(8,128)} %param.13) | data formatting | bytes 1572864 | tf_op args[5]
  181.6 2.8 %copy.142 = f32[3,8,64,128]{2,1,3,0:T(8,128)} copy(f32[3,8,64,128]{3,2,1,0:T(8,128)} %get-tuple-element.92) | data formatting | bytes 1572864
  184.4 2.9 %copy.143 = f32[3,8,64,128]{2,1,3,0:T(8,128)} copy(f32[3,8,64,128]{3,2,1,0:T(8,128)} %get-tuple-element.90) | data formatting | bytes 1572864
  187.2 22.3 %slice.250 = f32[3,65536]{0,1:T(8,128)} slice(f32[3,73728]{0,1:T(8,128)} %scatter_fusion.4), slice={[0:3], [0:65536]} | slice | bytes 1572864 | tf_op jit(solution)/shard_map/slice | solution.py:108
  209.5 21.0 %copy.133 = f32[3,8,64,128]{2,1,3,0:T(8,128)} copy(f32[3,8,64,128]{0,3,2,1:T(8,128)} %bitcast.41) | data formatting | bytes 1572864 | tf_op jit(solution)/shard_map/reshape | solution.py:108
  233.1 1.7 slice_add_fusion
  234.8 6.6 %scatter-add.53 = f32[3,8,64,128]{2,1,3,0:T(8,128)} dynamic-update-slice(f32[3,8,64,128]{2,1,3,0:T(8,128)} %copy.133, f32[3,1,64,128]{2,1,3,0:T(1,128)S(1)} %slice_add_fusion, s32[]{:T(128)} %constant.172.clone.1, s32[]{:T(128)} %constant.172.clone.1, s32[]{:T(128)} %constant.172.clone.1, s32[]{:T(128)} %constant.172.clone.1) | dynamic-update-slice | bytes 196612 | tf_op jit(solution)/shard_map/scatter-add | solution.py:109
  241.4 13.7 %fusion.6 = f32[3,8,64,128]{2,1,3,0:T(8,128)} fusion(f32[3,8,64,128]{2,1,3,0:T(8,128)} %copy.128, f32[3,10,66,1]{2,1,3,0:T(8,128)} %collective-permute-done.6, f32[3,10,1,128]{2,1,3,0:T(8,128)} %copy.113, f32[3,10,64,128]{2,1,3,0:T(8,128)} %copy.112, f32[3,10,1,128]{2,1,3,0:T(8,128)S(1)} %copy.111, f32[3,10,66,1]{2,1,3,0:T(8,128)} %collective-permute-done.7, ...), kind=kLoop, calls=%fused_computation.20 | loop fusion | flops 3735552 | bytes 4961760 | tf_op jit(solution)/shard_map/add | solution.py:113
  255.0 2.7 %copy.135 = f32[3,8,64,128]{3,2,1,0:T(8,128)} copy(f32[3,8,64,128]{2,1,3,0:T(8,128)} %fusion.6) | data formatting | bytes 1572864
  (137 shorter events, 28.9 us)
Async XLA Ops:
  1.6 18.3 %collective-permute-start.2 = (f32[3,1,64,128]{3,2,1,0:T(8,128)S(1)}, f32[3,1,64,128]{3,2,1,0:T(8,128)S(1)}, u32[]{:S(2)}, u32[]{:S(2)}) collective-permute-start(f32[3,1,64,128]{3,2,1,0:T(8,128)S(1)} %get-tuple-element.94), channel_id=1, source_target_pairs={{0,16},{1,17},{2,18},{3,19},{4,20},{5,21},{6,22},{7,23},{8,24},{9,... | collective-permute-start | bytes 294920 | tf_op jit(solution)/shard_map/ppermute | solution.py:21
  3.3 16.6 %collective-permute-start.3 = (f32[3,1,64,128]{3,2,1,0:T(8,128)S(1)}, f32[3,1,64,128]{3,2,1,0:T(8,128)S(1)}, u32[]{:S(2)}, u32[]{:S(2)}) collective-permute-start(f32[3,1,64,128]{3,2,1,0:T(8,128)S(1)} %get-tuple-element.93), channel_id=1, source_target_pairs={{16,0},{17,1},{18,2},{19,3},{20,4},{21,5},{22,6},{23,7},{24,8},{25... | collective-permute-start | bytes 294920 | tf_op jit(solution)/shard_map/ppermute | solution.py:24
  4.6 14.1 %collective-permute-start = (f32[4,8,128]{2,1,0:T(8,128)}, f32[4,8,128]{2,1,0:T(8,128)S(1)}, u32[]{:S(2)}, u32[]{:S(2)}) collective-permute-start(f32[4,8,128]{2,1,0:T(8,128)} %param.8), channel_id=1, source_target_pairs={{16,0},{17,1},{18,2},{19,3},{20,4},{21,5},{22,6},{23,7},{24,8},{25... | collective-permute-start | bytes 49160 | tf_op jit(solution)/shard_map/ppermute | solution.py:32
  8.3 11.0 %copy-start.34 = (s32[2]{0:T(128)}, s32[2]{0:T(128)S(1)}, u32[]{:S(2)}) copy-start(s32[2]{0:T(128)S(1)} %get-tuple-element.81) | copy-start | bytes 28
  9.6 10.2 %copy-start.11 = (f32[2,3,128]{2,1,0:T(4,128)}, f32[2,3,128]{2,1,0:T(4,128)S(1)}, u32[]{:S(2)}) copy-start(f32[2,3,128]{2,1,0:T(4,128)S(1)} %get-tuple-element.121) | copy-start | bytes 9220
  9.6 10.2 %copy-start.15 = (f32[2,3,128]{2,1,0:T(4,128)}, f32[2,3,128]{2,1,0:T(4,128)S(1)}, u32[]{:S(2)}) copy-start(f32[2,3,128]{2,1,0:T(4,128)S(1)} %get-tuple-element.120) | copy-start | bytes 9220
  19.9 8.7 %copy-start.2 = (f32[2,128,128]{2,1,0:T(8,128)}, f32[2,128,128]{2,1,0:T(8,128)S(1)}, u32[]{:S(2)}) copy-start(f32[2,128,128]{2,1,0:T(8,128)S(1)} %fusion.20) | copy-start | bytes 393220
  21.5 10.4 %collective-permute-start.4 = (f32[3,10,1,128]{3,1,2,0:T(8,128)S(1)}, f32[3,10,1,128]{3,1,2,0:T(8,128)}, u32[]{:S(2)}, u32[]{:S(2)}) collective-permute-start(f32[3,10,1,128]{3,1,2,0:T(8,128)S(1)} %copy.140), channel_id=1, source_target_pairs={{0,4},{4,8},{8,12},{1,5},{5,9},{9,13},{2,6},{6,10},{10,14},{3,7},{... | collective-permute-start | bytes 46088 | tf_op jit(solution)/shard_map/ppermute | solution.py:21
  25.5 8.2 %collective-permute-start.5 = (f32[3,10,1,128]{3,1,2,0:T(8,128)}, f32[3,10,1,128]{3,1,2,0:T(8,128)}, u32[]{:S(2)}, u32[]{:S(2)}) collective-permute-start(f32[3,10,1,128]{3,1,2,0:T(8,128)} %copy.141), channel_id=1, source_target_pairs={{4,0},{8,4},{12,8},{5,1},{9,5},{13,9},{6,2},{10,6},{14,10},{7,3},{... | collective-permute-start | bytes 46088 | tf_op jit(solution)/shard_map/ppermute | solution.py:24
  36.8 8.1 %copy-start.4 = (f32[2,128,128]{2,1,0:T(8,128)S(1)}, f32[2,128,128]{2,1,0:T(8,128)}, u32[]{:S(2)}) copy-start(f32[2,128,128]{2,1,0:T(8,128)} %get-tuple-element.99) | copy-start | bytes 393220
  36.8 8.1 %copy-start.5 = (f32[2,128,128]{2,1,0:T(8,128)S(1)}, f32[2,128,128]{2,1,0:T(8,128)}, u32[]{:S(2)}) copy-start(f32[2,128,128]{2,1,0:T(8,128)} %get-tuple-element.100) | copy-start | bytes 393220
  36.8 8.1 %copy-start.12 = (f32[2,3,128]{2,1,0:T(4,128)S(1)}, f32[2,3,128]{2,1,0:T(4,128)}, u32[]{:S(2)}) copy-start(f32[2,3,128]{2,1,0:T(4,128)} %copy-done.11) | copy-start | bytes 9220
  36.8 8.1 %copy-start.14 = (f32[2,3,128]{2,1,0:T(4,128)S(1)}, f32[2,3,128]{2,1,0:T(4,128)}, u32[]{:S(2)}) copy-start(f32[2,3,128]{2,1,0:T(4,128)} %copy-done.13) | copy-start | bytes 9220
  36.8 8.1 %copy-start.16 = (f32[2,3,128]{2,1,0:T(4,128)S(1)}, f32[2,3,128]{2,1,0:T(4,128)}, u32[]{:S(2)}) copy-start(f32[2,3,128]{2,1,0:T(4,128)} %copy-done.15) | copy-start | bytes 9220
  36.8 8.1 %copy-start.18 = (f32[2,3,128]{2,1,0:T(4,128)S(1)}, f32[2,3,128]{2,1,0:T(4,128)}, u32[]{:S(2)}) copy-start(f32[2,3,128]{2,1,0:T(4,128)} %copy-done.17) | copy-start | bytes 9220
  38.4 10.4 %collective-permute-start.6 = (f32[3,10,66,1]{2,1,3,0:T(8,128)}, f32[3,10,66,1]{2,1,3,0:T(8,128)}, u32[]{:S(2)}, u32[]{:S(2)}) collective-permute-start(f32[3,10,66,1]{2,1,3,0:T(8,128)} %get-tuple-element.86), channel_id=1, source_target_pairs={{0,1},{1,2},{2,3},{4,5},{5,6},{6,7},{8,9},{9,10},{10,11},{12,13},{... | collective-permute-start | bytes 23768 | tf_op jit(solution)/shard_map/ppermute | solution.py:21
  41.9 6.9 %collective-permute-start.7 = (f32[3,10,66,1]{2,1,3,0:T(8,128)}, f32[3,10,66,1]{2,1,3,0:T(8,128)}, u32[]{:S(2)}, u32[]{:S(2)}) collective-permute-start(f32[3,10,66,1]{2,1,3,0:T(8,128)} %get-tuple-element.87), channel_id=1, source_target_pairs={{1,0},{2,1},{3,2},{5,4},{6,5},{7,6},{9,8},{10,9},{11,10},{13,12},{... | collective-permute-start | bytes 23768 | tf_op jit(solution)/shard_map/ppermute | solution.py:24
  46.6 72.7 %collective-permute-start.1 = (f32[4,3,128]{2,1,0:T(4,128)S(1)}, f32[4,3,128]{2,1,0:T(4,128)S(1)}, u32[]{:S(2)}, u32[]{:S(2)}) collective-permute-start(f32[4,3,128]{2,1,0:T(4,128)S(1)} %scatter_fusion), channel_id=1, source_target_pairs={{0,16},{1,17},{2,18},{3,19},{4,20},{5,21},{6,22},{7,23},{8,24},{9,... | collective-permute-start | bytes 18440 | tf_op jit(solution)/shard_map/ppermute | solution.py:32
  64.1 20.7 %copy-start.25 = (s32[1024]{0:T(1024)S(1)}, s32[1024]{0:T(1024)}, u32[]{:S(2)}) copy-start(s32[1024]{0:T(1024)} %get-tuple-element.131) | copy-start | bytes 12292
  64.1 37.0 %copy-start.24 = (s32[1024]{0:T(1024)S(1)}, s32[1024]{0:T(1024)}, u32[]{:S(2)}) copy-start(s32[1024]{0:T(1024)} %get-tuple-element.130) | copy-start | bytes 12292
  64.1 53.3 %copy-start.6 = (f32[4,8,128]{2,1,0:T(8,128)S(1)}, f32[4,8,128]{2,1,0:T(8,128)}, u32[]{:S(2)}) copy-start(f32[4,8,128]{2,1,0:T(8,128)} %param.8) | copy-start | bytes 49156
  64.1 53.3 %copy-start.21 = (f32[4,128]{1,0:T(4,128)S(1)}, f32[4,128]{1,0:T(4,128)}, u32[]{:S(2)}) copy-start(f32[4,128]{1,0:T(4,128)} %param.12) | copy-start | bytes 6148
  64.1 53.3 %copy-start.22 = (f32[4,128]{1,0:T(4,128)S(1)}, f32[4,128]{1,0:T(4,128)}, u32[]{:S(2)}) copy-start(f32[4,128]{1,0:T(4,128)} %broadcast_subtract_fusion) | copy-start | bytes 6148
  64.1 53.3 %copy-start.27 = (f32[4,1,128]{2,1,0:T(1,128)S(1)}, f32[4,1,128]{2,1,0:T(1,128)}, u32[]{:S(2)}) copy-start(f32[4,1,128]{2,1,0:T(1,128)} %get-tuple-element.110) | copy-start | bytes 6148
  84.8 33.4 %copy-start.19 = (f32[4,1,128]{2,1,0:T(1,128)S(1)}, f32[4,1,128]{2,1,0:T(1,128)}, u32[]{:S(2)}) copy-start(f32[4,1,128]{2,1,0:T(1,128)} %get-tuple-element.109) | copy-start | bytes 6148
  84.8 33.5 %copy-start.20 = (f32[4,1,128]{2,1,0:T(1,128)S(1)}, f32[4,1,128]{2,1,0:T(1,128)}, u32[]{:S(2)}) copy-start(f32[4,1,128]{2,1,0:T(1,128)} %get-tuple-element.111) | copy-start | bytes 6148
  121.2 17.5 %copy-start.26 = (s32[512]{0:T(512)S(1)}, s32[512]{0:T(512)}, u32[]{:S(2)}) copy-start(s32[512]{0:T(512)} %get-tuple-element.124) | copy-start | bytes 6148
  175.0 58.1 %collective-permute-start.8 = (f32[3,64,128]{1,2,0:T(8,128)}, f32[3,64,128]{1,2,0:T(8,128)}, u32[]{:S(2)}, u32[]{:S(2)}) collective-permute-start(f32[3,64,128]{1,2,0:T(8,128)} %copy.132), channel_id=1, source_target_pairs={{0,16},{1,17},{2,18},{3,19},{4,20},{5,21},{6,22},{7,23},{8,24},{9,... | collective-permute-start | bytes 294920 | tf_op jit(solution)/shard_map/ppermute | solution.py:32
  209.5 21.0 %copy-start.33 = (s32[4]{0:T(128)S(1)}, s32[4]{0:T(128)}, u32[]{:S(2)}) copy-start(s32[4]{0:T(128)} %copy-done.32) | copy-start | bytes 52
  209.5 21.6 %copy-start.31 = (s32[4]{0:T(128)S(1)}, s32[4]{0:T(128)}, u32[]{:S(2)}) copy-start(s32[4]{0:T(128)} %copy-done.30) | copy-start | bytes 52
  209.5 22.3 %copy-start.23 = (f32[2,3,128]{2,1,0:T(4,128)S(1)}, f32[2,3,128]{2,1,0:T(4,128)}, u32[]{:S(2)}) copy-start(f32[2,3,128]{2,1,0:T(4,128)} %get-tuple-element.78) | copy-start | bytes 9220
  209.5 22.3 %copy-start.29 = (s32[2]{0:T(128)S(1)}, s32[2]{0:T(128)}, u32[]{:S(2)}) copy-start(s32[2]{0:T(128)} %copy-done.28) | copy-start | bytes 28
  (12 other events, 54.3 us)
where the time goes:
time: 260 us; the launch traced here: 258 us
  local copies, waits for them, and re-layouts  148 us (57%)
  other arithmetic  86.7 us (33%)
  starting transfers between devices  21.3 us (8%)
    scatter-add x1, other arithmetic, body(): deposit = deposit.at[:, drag_cell + layer].add(drag_share * terms)  27.6 us
    reshape x2, local copies, waits for them, and re-layouts, body(): flat = padded.reshape(3, -1)  25.1 us
    slice x1, local copies, waits for them, and re-layouts, body(): deposit[:, :depth * layer].reshape(3, depth, across_count, along_count)  22.3 us
    reshape x1, local copies, waits for them, and re-layouts, body(): deposit[:, :depth * layer].reshape(3, depth, across_count, along_count)  21 us
    scatter-add x1, other arithmetic, body(): deposit = deposit.at[:, drag_cell].add((1.0 - drag_share) * terms)  17.5 us
    gather x2, local copies, waits for them, and re-layouts, body(): flat[:, upper_index]  16.3 us
    gather x2, local copies, waits for them, and re-layouts, body(): flat[:, lower_index]  16.3 us
    add x1, other arithmetic, body(): fluid_next = fluid + diffuse * (beside - 6.0 * fluid) + source_gain * source  13.7 us
  transfers between devices with their start and end apart: 9, of which 0 were waited for; matrix products, arithmetic and copies ran while one was open for 57% of the time, Pallas kernels for 0%

commit v1 on v0

v1 whole, which is shorter than its diff:
```python
import functools

import jax
import jax.numpy as jnp
from jax import lax
from jax.experimental import pallas as pl
from jax.experimental.pallas import tpu as pltpu
from jax.sharding import PartitionSpec as P

soft_core = 0.01
damp_normal = 0.3
damp_tangent = 0.2
drag_coef = 1.5
diffuse = 0.1
source_gain = 0.5

F32 = jnp.float32
BF16 = jnp.bfloat16
PARTS = 3


def split_parts(value):
    parts = []
    for _ in range(PARTS):
        part = value.astype(BF16)
        parts.append(part)
        value = value - part.astype(F32)
    return parts


def places(cell, across, along):
    layer = across * along
    if layer & (layer - 1) or along & (along - 1):
        return cell // layer, cell // along % across, cell % along
    shift = along.bit_length() - 1
    high = layer.bit_length() - 1
    return (
        lax.shift_right_logical(cell, high),
        lax.shift_right_logical(cell, shift) & (across - 1),
        cell & (along - 1),
    )


def spread_block(block, store):
    rows = jnp.concatenate([block, block[7:8] * jnp.sqrt(block[6:7]), jnp.zeros((7, 128), F32)], axis=0)
    columns = jnp.transpose(rows)
    for i in range(9):
        store[i] = jnp.broadcast_to(columns[:, i : i + 1], (128, 128))


def pair_sum(left, spread):
    rows = [left[i : i + 1] for i in range(8)]
    scale = (2.0 * damp_tangent) * rows[7] * jnp.sqrt(rows[6])
    wide = [jnp.broadcast_to(row, (8, 128)) for row in rows + [scale]]
    total = [jnp.zeros((8, 128), F32) for _ in range(3)]
    for tile in range(16):
        there = [spread[i, tile * 8 : tile * 8 + 8, :] for i in range(9)]
        ex, ey, ez, wx, wy, wz = [wide[i] - there[i] for i in range(6)]
        inverse = lax.rsqrt((ex * ex + ey * ey) + (ez * ez + soft_core))
        dist = ((ex * ex + ey * ey) + (ez * ez + soft_core)) * inverse
        reach = wide[6] + there[6]
        delta = jnp.maximum(reach - dist, 0.0)
        mass = wide[7] + there[7]
        under = jnp.maximum(delta * reach * (mass * mass), 1e-30)
        tangent = (wide[8] * there[8]) * (delta * lax.rsqrt(under))
        speed = ((wx * ex + wy * ey) + wz * ez) * inverse
        along = (
            tangent
            * (
                (2.0 / 3.0 / damp_tangent) * delta
                - ((damp_normal - damp_tangent) / damp_tangent) * speed
            )
            * inverse
        )
        total[0] += along * ex - tangent * wx
        total[1] += along * ey - tangent * wy
        total[2] += along * ez - tangent * wz
    return [jnp.sum(item, axis=0, keepdims=True) for item in total]


def pack_kernel(blocks, pairs, pair_ref, flag_ref, part_ref, cell_ref, share_ref, fluid_ref, *outs):
    depth, across, along = fluid_ref.shape[1:]
    even = [flag_ref[0, axis] == 0 for axis in range(3)]
    height_outs, across_outs, along_outs = outs
    for n, out in enumerate(height_outs):
        upward = even[0] if n == 0 else jnp.logical_not(even[0])
        layer = jnp.where(upward, depth - 1, 0)
        for c in range(3):
            out[c * across : (c + 1) * across, :] = fluid_ref[c, layer]
        base = 3 * across
        for b in range(blocks):
            out[base + 8 * b : base + 8 * b + 8, :] = part_ref[b]
        base += 8 * blocks
        out[base : base + blocks, :] = cell_ref[...].astype(F32)
        out[base + blocks : base + 2 * blocks, :] = share_ref[...]
        base += 2 * blocks
        for k in range(pairs):
            for side in range(2):
                row = base + 2 * k + side
                out[row : row + 1, :] = jnp.full((1, 128), pair_ref[k, side], jnp.int32).astype(F32)
        used = base + 2 * pairs
        if used < out.shape[0]:
            out[used:, :] = jnp.zeros((out.shape[0] - used, 128), F32)
    for n, out in enumerate(across_outs):
        upward = even[1] if n == 0 else jnp.logical_not(even[1])
        for k in range(3 * depth):
            c, h = divmod(k, depth)
            last = fluid_ref[c, h, across - 1 : across, :]
            first = fluid_ref[c, h, 0:1, :]
            out[k : k + 1, :] = jnp.where(upward, last, first)
    lanes = lax.broadcasted_iota(jnp.int32, (across, along), 1)
    first = jnp.zeros((across, along), F32)
    last = jnp.zeros((across, along), F32)
    for k in range(3 * depth):
        c, h = divmod(k, depth)
        turned = fluid_ref[c, h]
        if k:
            turned = pltpu.roll(turned, 2 * k, 1)
        first = jnp.where(lanes == 2 * k, turned, first)
        last = jnp.where(lanes == (2 * k - 1) % along, turned, last)
    first = pltpu.roll(first, along - 1, 1)
    last = pltpu.roll(last, 1, 1)
    for n, out in enumerate(along_outs):
        upward = even[2] if n == 0 else jnp.logical_not(even[2])
        out[...] = jnp.where(upward, last, first)


def local_kernel(
    blocks, local_pair_ref, part_ref, cell_ref, share_ref, fluid_ref, force_ref, next_ref, spread, weights, coupled, spots
):
    depth, across, along = fluid_ref.shape[1:]
    for b in range(blocks):
        spread_block(part_ref[b], spread.at[b])

    for b in range(blocks):
        force = pair_sum(part_ref[b], spread.at[b])
        for c in range(3):
            force_ref[b, c : c + 1, :] = force[c]

    def listed(i, carry):
        a = local_pair_ref[i // 2, i % 2]
        c = local_pair_ref[i // 2, 1 - i % 2]
        force = pair_sum(part_ref[a], spread.at[c])
        for d in range(3):
            force_ref[a, d : d + 1, :] += force[d]
        return carry

    lax.fori_loop(0, 2 * local_pair_ref.shape[0], listed, 0)

    rows = lax.broadcasted_iota(jnp.int32, (across, 128), 0)
    sites = lax.broadcasted_iota(jnp.int32, (along, 128), 0)
    for b in range(blocks):
        height, over, spot = places(cell_ref[b : b + 1, :], across, along)
        share = share_ref[b : b + 1, :]
        index = jnp.broadcast_to(spot, (across, 128))
        mask = rows == over
        near = [
            jnp.where(height == h, 1.0 - share, 0.0) + jnp.where(height == h - 1, share, 0.0)
            for h in range(depth)
        ]
        spots[:, b * 128 : (b + 1) * 128] = jnp.where(sites == spot, 1.0, 0.0).astype(BF16)
        for c in range(3):
            total = jnp.zeros((8, 128), F32)
            for h in range(depth):
                seen = jnp.take_along_axis(fluid_ref[c, h], index, axis=1)
                seen = jnp.where(mask, seen, 0.0)
                total += near[h] * jnp.sum(seen.reshape(across // 8, 8, 128), axis=0)
            met = jnp.sum(total, axis=0, keepdims=True)
            drag = drag_coef * part_ref[b, 6:7, :] * (met - part_ref[b, 3 + c : 4 + c, :])
            force_ref[b, c : c + 1, :] += drag
            for h in range(depth):
                given = (-source_gain) * near[h] * drag
                weights[c * depth + h : c * depth + h + 1, b * 128 : (b + 1) * 128] = given
        ones = jnp.where(mask, 1.0, 0.0).astype(BF16)
        for n, part in enumerate(split_parts(weights[:, b * 128 : (b + 1) * 128])):
            for k in range(3 * depth):
                coupled[n, k * across : (k + 1) * across, b * 128 : (b + 1) * 128] = ones * part[k : k + 1, :]

    lanes = lax.broadcasted_iota(jnp.int32, (across, along), 1)
    downs = lax.broadcasted_iota(jnp.int32, (across, along), 0)
    for c in range(3):
        source = jnp.zeros((depth * across, along), F32)
        for n in range(PARTS):
            source += lax.dot_general(
                coupled[n, c * depth * across : (c + 1) * depth * across, :],
                spots[...],
                (((1,), (1,)), ((), ())),
                preferred_element_type=F32,
            )
        for h in range(depth):
            here = fluid_ref[c, h]
            beside = jnp.where(downs == 0, 0.0, pltpu.roll(here, 1, 0))
            beside += jnp.where(downs == across - 1, 0.0, pltpu.roll(here, across - 1, 0))
            beside += jnp.where(lanes == 0, 0.0, pltpu.roll(here, 1, 1))
            beside += jnp.where(lanes == along - 1, 0.0, pltpu.roll(here, along - 1, 1))
            if h > 0:
                beside += fluid_ref[c, h - 1]
            if h < depth - 1:
                beside += fluid_ref[c, h + 1]
            next_ref[c, h] = (
                here + diffuse * (beside - 6.0 * here) + source[h * across : (h + 1) * across, :]
            )


def finish_kernel(
    blocks, pairs, flag_ref, pair_ref, part_ref, cell_ref, share_ref, fluid_ref, force_ref, next_ref, ins, outs, scratch
):
    out_force, out_next = outs
    spread, coupled, spots = scratch
    depth, across, along = fluid_ref.shape[1:]
    height_ins, across_ins, along_ins = ins
    even = [flag_ref[0, axis] == 0 for axis in range(3)]

    def ordered(refs, axis):
        first = refs[0][...]
        if len(refs) == 1:
            return jnp.where(even[axis], 0.0, first), jnp.where(even[axis], first, 0.0)
        second = refs[1][...]
        return jnp.where(even[axis], second, first), jnp.where(even[axis], first, second)

    across_low, across_high = ordered(across_ins, 1)
    along_low, along_high = ordered(along_ins, 2)
    edges = diffuse * (along_low + along_high)
    across_low = diffuse * across_low
    across_high = diffuse * across_high
    lanes = lax.broadcasted_iota(jnp.int32, (across, along), 1)
    downs = lax.broadcasted_iota(jnp.int32, (across, along), 0)
    rim = jnp.logical_or(lanes == 0, lanes == along - 1)
    for k in range(3 * depth):
        c, h = divmod(k, depth)
        value = next_ref[c, h]
        value += jnp.where(rim, pltpu.roll(edges, (along - 2 * k) % along, 1) if k else edges, 0.0)
        value += jnp.where(downs == 0, across_low[k : k + 1, :], 0.0)
        value += jnp.where(downs == across - 1, across_high[k : k + 1, :], 0.0)
        out_next[c, h] = value
    for b in range(blocks):
        out_force[b] = force_ref[b]

    rows = lax.broadcasted_iota(jnp.int32, (across, 128), 0)
    sites = lax.broadcasted_iota(jnp.int32, (along, 128), 0)
    for n, blob in enumerate(height_ins):
        above = even[0] if n == 0 else jnp.logical_not(even[0])
        own_layer = jnp.where(above, depth - 1, 0)
        base = 3 * across
        there = [blob[base + 8 * b : base + 8 * b + 8, :] for b in range(blocks)]
        base += 8 * blocks
        cells = blob[base : base + blocks, :].astype(jnp.int32)
        shares = blob[base + blocks : base + 2 * blocks, :]
        base += 2 * blocks
        for k in range(pairs):
            theirs = [blob[base + 2 * k + side : base + 2 * k + side + 1, :] for side in range(2)]
            ours = [jnp.full((1, 128), pair_ref[k, side], jnp.int32).astype(F32) for side in range(2)]
            to = jnp.where(above, ours[0], theirs[1])
            by = jnp.where(above, ours[1], theirs[0])
            left = part_ref[0]
            right = there[0]
            for b in range(1, blocks):
                left = jnp.where(to == b, part_ref[b], left)
                right = jnp.where(by == b, there[b], right)
            spread_block(right, spread)
            force = pair_sum(left, spread)
            for b in range(blocks):
                for c in range(3):
                    out_force[b, c : c + 1, :] += jnp.where(to == b, force[c], 0.0)
        for b in range(blocks):
            cell = jnp.where(above, cell_ref[b : b + 1, :], cells[b : b + 1, :])
            share = jnp.where(above, share_ref[b : b + 1, :], shares[b : b + 1, :])
            owner = jnp.where(above, part_ref[b], there[b])
            height, over, spot = places(cell, across, along)
            top = height == depth - 1
            index = jnp.broadcast_to(spot, (across, 128))
            mask = rows == over
            seen_share = jnp.where(top, jnp.where(above, share, 1.0 - share), 0.0)
            home_share = jnp.where(jnp.logical_and(top, jnp.logical_not(above)), share, 0.0)
            given_share = (-source_gain) * jnp.where(above, 1.0 - share, share)
            own_share = jnp.where(jnp.logical_and(top, jnp.logical_not(above)), 1.0, 0.0)
            spots[:, b * 128 : (b + 1) * 128] = jnp.where(sites == spot, 1.0, 0.0).astype(BF16)
            ones = jnp.where(mask, 1.0, 0.0).astype(BF16)
            for c in range(3):
                seen = jnp.take_along_axis(blob[c * across : (c + 1) * across, :], index, axis=1)
                home = jnp.take_along_axis(fluid_ref[c, 0], index, axis=1)
                met = jnp.where(mask, seen_share * seen + home_share * home, 0.0)
                met = jnp.sum(met, axis=0, keepdims=True)
                drag = drag_coef * owner[6:7, :] * (met - own_share * owner[3 + c : 4 + c, :])
                out_force[b, c : c + 1, :] += jnp.where(above, drag, 0.0)
                for m, part in enumerate(split_parts(given_share * drag)):
                    coupled[m, c * across : (c + 1) * across, b * 128 : (b + 1) * 128] = ones * part
        source = jnp.zeros((3 * across, along), F32)
        for m in range(PARTS):
            source += lax.dot_general(
                coupled[m], spots[...], (((1,), (1,)), ((), ())), preferred_element_type=F32
            )
        for c in range(3):
            out_next[c, own_layer] += (
                diffuse * blob[c * across : (c + 1) * across, :] + source[c * across : (c + 1) * across, :]
            )


def exchange(payloads, axis):
    count = lax.axis_size(axis)
    results = []
    for n, payload in enumerate(payloads):
        route = []
        for i in range(n, count - 1, 2):
            route += [(i, i + 1), (i + 1, i)]
        results.append(lax.ppermute(payload, axis, route))
    return results


def body(particles, local_pairs, cross_pairs, drag_cell, drag_share, fluid):
    blocks = particles.shape[0]
    pairs = cross_pairs.shape[0]
    _, depth, across, along = fluid.shape
    axes = ("gx", "gy", "gz")
    flags = jnp.stack([lax.axis_index(axis) % 2 for axis in axes]).astype(jnp.int32).reshape(1, 3)
    counts = [min(2, lax.axis_size(axis) - 1) for axis in axes]
    blob_rows = 3 * across + 10 * blocks + 2 * pairs
    blob_rows += -blob_rows % 8
    shapes = [(blob_rows, along), (3 * depth, along), (across, along)]
    vmem = pl.BlockSpec(memory_space=pltpu.VMEM)
    smem = pl.BlockSpec(memory_space=pltpu.SMEM)

    packed = pl.pallas_call(
        functools.partial(grouped_pack, blocks, pairs, tuple(counts)),
        out_shape=[jax.ShapeDtypeStruct(shape, F32) for shape, n in zip(shapes, counts) for _ in range(n)],
        in_specs=[smem, smem, vmem, vmem, vmem, vmem],
        out_specs=[vmem] * sum(counts),
        name="pack",
    )(cross_pairs, flags, particles, drag_cell, drag_share, fluid)
    received = []
    at = 0
    for axis, n in zip(axes, counts):
        received += exchange(packed[at : at + n], axis)
        at += n

    force, partial = pl.pallas_call(
        functools.partial(local_kernel, blocks),
        out_shape=[
            jax.ShapeDtypeStruct((blocks, 3, 128), F32),
            jax.ShapeDtypeStruct(fluid.shape, F32),
        ],
        in_specs=[smem, vmem, vmem, vmem, vmem],
        out_specs=[vmem, vmem],
        scratch_shapes=[
            pltpu.VMEM((blocks, 9, 128, 128), F32),
            pltpu.VMEM((3 * depth, blocks * 128), F32),
            pltpu.VMEM((PARTS, 3 * depth * across, blocks * 128), BF16),
            pltpu.VMEM((along, blocks * 128), BF16),
        ],
        name="local",
    )(local_pairs, particles, drag_cell, drag_share, fluid)

    return tuple(
        pl.pallas_call(
            functools.partial(grouped_finish, blocks, pairs, tuple(counts)),
            out_shape=[
                jax.ShapeDtypeStruct((blocks, 3, 128), F32),
                jax.ShapeDtypeStruct(fluid.shape, F32),
            ],
            in_specs=[smem, smem] + [vmem] * (6 + len(received)),
            out_specs=[vmem, vmem],
            scratch_shapes=[
                pltpu.VMEM((9, 128, 128), F32),
                pltpu.VMEM((PARTS, 3 * across, blocks * 128), BF16),
                pltpu.VMEM((along, blocks * 128), BF16),
            ],
            name="finish",
        )(flags, cross_pairs, particles, drag_cell, drag_share, fluid, force, partial, *received)
    )


def by_axis(refs, counts):
    groups, at = [], 0
    for n in counts:
        groups.append(refs[at : at + n])
        at += n
    return groups


def grouped_pack(blocks, pairs, counts, *refs):
    pack_kernel(blocks, pairs, *refs[:6], *by_axis(refs[6:], counts))


def grouped_finish(blocks, pairs, counts, *refs):
    n = sum(counts)
    finish_kernel(
        blocks, pairs, *refs[:8], by_axis(refs[8 : 8 + n], counts), refs[8 + n : 10 + n], refs[10 + n :]
    )


def solution(mesh):
    in_specs = (
        P(("gx", "gy", "gz"), None, None),
        P(("gx", "gy", "gz"), None),
        P(("gx", "gy", "gz"), None),
        P(("gx", "gy", "gz"), None),
        P(("gx", "gy", "gz"), None),
        P(None, "gx", "gy", "gz"),
    )
    out_specs = (P(("gx", "gy", "gz"), None, None), P(None, "gx", "gy", "gz"))
    return jax.shard_map(body, mesh=mesh, in_specs=in_specs, out_specs=out_specs, check_vma=False)
```

time: 260 us -> 26.7 us (0.10)
  local copies, waits for them, and re-layouts: 148 us -> 2.62 us
  other arithmetic: 86.7 us -> 0.58 us
  Pallas kernels: 0 us -> 12.5 us
  starting transfers between devices: 21.3 us -> 10 us
    reshape x4 -> x0, local copies, waits for them, and re-layouts: 50.4 us -> none  [the longest x2 25.1 us: body(): flat = padded.reshape(3, -1)]
    scatter-add x6 -> x0, other arithmetic: 47.6 us -> none  [the longest x1 27.6 us: body(): deposit = deposit.at[:, drag_cell + layer].add(drag_share * terms)]
    gather x8 -> x0, local copies, waits for them, and re-layouts: 36.9 us -> none  [the longest x2 16.3 us: body(): flat[:, upper_index]]
    slice x12 -> x0, local copies, waits for them, and re-layouts: 27.8 us -> none  [the longest x1 22.3 us: body(): deposit[:, :depth * layer].reshape(3, depth, across_count, along_count)]
    add x2 -> x0, other arithmetic: 15.4 us -> none  [the longest x1 13.7 us: body(): fluid_next = fluid + diffuse * (beside - 6.0 * fluid) + source_gain * source]
    pallas_call x0 -> x3, Pallas kernels: none -> 12.5 us  [the longest x1 6.49 us: body(): pl.pallas_call(functools.partial(local_kernel, blocks), out_shape=[jax.Sh...]
    unnamed x78 -> x13, local copies, waits for them, and re-layouts: 13 us -> 1.33 us
    ppermute x9 -> x5, starting transfers between devices: 21.3 us -> 10 us  [exchange(): results.append(lax.ppermute(payload, axis, route))]
  transfers between devices with their start and end apart: 9 -> 5, of which waited for: 0 -> 0; matrix products, arithmetic and copies ran while one was open for 57% -> 3% of each run, Pallas kernels for 0% -> 24%
where the time goes in v1:
time: 26.7 us; the launch traced here: 26.5 us
  Pallas kernels  12.5 us (47%)
  starting transfers between devices  10 us (37%)
  local copies, waits for them, and re-layouts  2.62 us (10%)
  between operations  0.75 us (3%)
  other arithmetic  0.58 us (2%)
    ppermute x5, starting transfers between devices, exchange(): results.append(lax.ppermute(payload, axis, route))  10 us
    pallas_call x1, Pallas kernels, body(): pl.pallas_call(functools.partial(local_kernel, blocks), out_shape=[jax.Sh...  6.49 us
    pallas_call x1, Pallas kernels, body(): pl.pallas_call(functools.partial(grouped_finish, blocks, pairs, tuple(cou...  3.82 us
    pallas_call x1, Pallas kernels, body(): pl.pallas_call(functools.partial(grouped_pack, blocks, pairs, tuple(count...  2.15 us
    unnamed x13, local copies, waits for them, and re-layouts  1.33 us
    pallas_call x1, local copies, waits for them, and re-layouts, body(): pl.pallas_call(functools.partial(grouped_finish, blocks, pairs, tuple(cou...  1.29 us
    reshape x1, other arithmetic, body(): jnp.stack([lax.axis_index(axis) % 2 for axis in axes]).astype(jnp.int32)  0.58 us
  transfers between devices with their start and end apart: 5, of which 0 were waited for; matrix products, arithmetic and copies ran while one was open for 3% of the time, Pallas kernels for 24%

profile of v1, /device:TPU:10, one launch (start us, length us, event | category | flops | bytes accessed | tf_op | source)
XLA Modules:
  0.0 26.5 jit_solution(14827010783273134440)
XLA Ops:
  0.7 0.6 %add_bitcast_fusion.refs_1_.refs_0_ = s32[1,3]{1,0:T(1,128)} fusion(s32[1]{0:T(128)} %bitcast.2, s32[1]{0:T(128)} %bitcast.1, s32[1]{0:T(128)} %bitcast), kind=kLoop, calls=%fused_computation | loop fusion | flops 6 | bytes 24 | tf_op jit(solution)/shard_map/reshape | solution.py:315
  1.2 2.1 %pack.1 = (f32[240,128]{1,0:T(8,128)}, f32[24,128]{1,0:T(8,128)}, f32[24,128]{1,0:T(8,128)}, f32[64,128]{1,0:T(8,128)}, f32[64,128]{1,0:T(8,128)}) custom-call(s32[2,2]{1,0:T(2,128)} %refs_1_.1, s32[1,3]{1,0:T(1,128)} %add_bitcast_fusion.refs_1_.refs_0_, f32[4,8,128]{2,1,0:T(8,128)} %refs_2_.3, s32[4,128]{1,0:T(4,128)} %refs_3_.3, f32[4,128]{1,0:T(4,128)} %refs_4_.3, ...), custom_call_target="tpu_custom_call" | custom-call | tf_op jit(solution)/shard_map/pack/pallas_call | solution.py:323
  3.4 0.0 collective-permute-start
  3.4 0.5 %collective-permute-start.3 = (f32[64,128]{1,0:T(8,128)}, f32[64,128]{1,0:T(8,128)S(1)}, u32[]{:S(2)}, u32[]{:S(2)}) collective-permute-start(f32[64,128]{1,0:T(8,128)} %get-tuple-element.14), channel_id=1, source_target_pairs={{0,1},{1,0},{2,3},{3,2},{4,5},{5,4},{6,7},{7,6},{8,9},{9,8},{10,11... | collective-permute-start | bytes 98312 | tf_op jit(solution)/shard_map/ppermute | solution.py:306
  3.9 4.6 %collective-permute-start.4 = (f32[64,128]{1,0:T(8,128)}, f32[64,128]{1,0:T(8,128)S(1)}, u32[]{:S(2)}, u32[]{:S(2)}) collective-permute-start(f32[64,128]{1,0:T(8,128)} %get-tuple-element.15), channel_id=1, source_target_pairs={{1,2},{2,1},{5,6},{6,5},{9,10},{10,9},{13,14},{14,13},{17,18},{18,... | collective-permute-start | bytes 98312 | tf_op jit(solution)/shard_map/ppermute | solution.py:306
  8.5 0.0 copy-start.5
  8.5 0.6 %collective-permute-start.1 = (f32[24,128]{1,0:T(8,128)}, f32[24,128]{1,0:T(8,128)S(1)}, u32[]{:S(2)}, u32[]{:S(2)}) collective-permute-start(f32[24,128]{1,0:T(8,128)} %get-tuple-element.12), channel_id=1, source_target_pairs={{0,4},{4,0},{8,12},{12,8},{1,5},{5,1},{9,13},{13,9},{2,6},{6,2},{1... | collective-permute-start | bytes 36872 | tf_op jit(solution)/shard_map/ppermute | solution.py:306
  9.1 4.3 %collective-permute-start.2 = (f32[24,128]{1,0:T(8,128)}, f32[24,128]{1,0:T(8,128)S(1)}, u32[]{:S(2)}, u32[]{:S(2)}) collective-permute-start(f32[24,128]{1,0:T(8,128)} %get-tuple-element.13), channel_id=1, source_target_pairs={{4,8},{8,4},{5,9},{9,5},{6,10},{10,6},{7,11},{11,7},{20,24},{24,20... | collective-permute-start | bytes 36872 | tf_op jit(solution)/shard_map/ppermute | solution.py:306
  13.5 0.0 copy-done.5
  13.5 0.7 %copy.8.local_pair_ref = s32[4,2]{1,0:T(4,128)} copy(s32[4,2]{0,1:T(2,128)S(1)} %copy-done.5) | data formatting | bytes 64 | tf_op args[1]
  14.1 6.5 %local.1 = (f32[4,3,128]{2,1,0:T(4,128)}, f32[3,8,64,128]{3,2,1,0:T(8,128)}) custom-call(s32[4,2]{1,0:T(4,128)} %copy.8.local_pair_ref, f32[4,8,128]{2,1,0:T(8,128)} %refs_2_.3, s32[4,128]{1,0:T(4,128)} %refs_3_.3, f32[4,128]{1,0:T(4,128)} %refs_4_.3, f32[3,8,64,128]{3,2,1,0:T(8,128)} %refs_5_.3), custom_call_target="tpu_custom_call" | custom-call | tf_op jit(solution)/shard_map/local/pallas_call | solution.py:336
  20.6 0.0 collective-permute-done.1.refs_9_
  20.6 0.0 copy-start.3
  20.6 0.0 collective-permute-done.2.refs_10_
  20.6 0.0 copy-start.4
  20.6 0.0 collective-permute-done.3.refs_11_
  20.7 0.0 copy-start.1
  20.7 0.0 collective-permute-done.4.refs_12_
  20.7 0.0 copy-start.2
  20.7 0.0 collective-permute-done.refs_8_
  20.7 0.0 copy-start
  20.7 0.5 %copy-done.3 = f32[24,128]{1,0:T(8,128)} copy-done((f32[24,128]{1,0:T(8,128)}, f32[24,128]{1,0:T(8,128)S(1)}, u32[]{:S(2)}) %copy-start.3) | copy-done | bytes 12312
  21.2 0.0 copy-done.4
  21.2 0.0 copy-done.1
  21.3 0.0 copy-done.2
  21.3 0.1 copy-done
  21.4 3.8 %finish.1 = (f32[4,3,128]{2,1,0:T(4,128)}, f32[3,8,64,128]{3,2,1,0:T(8,128)}) custom-call(s32[1,3]{1,0:T(1,128)} %add_bitcast_fusion.refs_1_.refs_0_, s32[2,2]{1,0:T(2,128)} %refs_1_.1, f32[4,8,128]{2,1,0:T(8,128)} %refs_2_.3, s32[4,128]{1,0:T(4,128)} %refs_3_.3, f32[4,128]{1,0:T(4,128)} %refs_4_.3, f32[3,8,64,128]{3,2,1,0:T(8,128)} %refs_5_.3, ...), custom_call_target="tpu_custom_call" | custom-call | tf_op jit(solution)/shard_map/finish/pallas_call | solution.py:354
  25.2 1.3 %copy.9 = f32[4,3,128]{2,0,1:T(4,128)} copy(f32[4,3,128]{2,1,0:T(4,128)} %get-tuple-element.16) | data formatting | bytes 12288 | tf_op jit(solution)/shard_map/finish/pallas_call | solution.py:354
Async XLA Ops:
  3.4 17.3 %collective-permute-start = (f32[240,128]{1,0:T(8,128)}, f32[240,128]{1,0:T(8,128)S(1)}, u32[]{:S(2)}, u32[]{:S(2)}) collective-permute-start(f32[240,128]{1,0:T(8,128)} %get-tuple-element.11), channel_id=1, source_target_pairs={{0,16},{16,0},{1,17},{17,1},{2,18},{18,2},{3,19},{19,3},{4,20},{20... | collective-permute-start | bytes 368648 | tf_op jit(solution)/shard_map/ppermute | solution.py:306
  3.4 17.3 %collective-permute-start.3 = (f32[64,128]{1,0:T(8,128)}, f32[64,128]{1,0:T(8,128)S(1)}, u32[]{:S(2)}, u32[]{:S(2)}) collective-permute-start(f32[64,128]{1,0:T(8,128)} %get-tuple-element.14), channel_id=1, source_target_pairs={{0,1},{1,0},{2,3},{3,2},{4,5},{5,4},{6,7},{7,6},{8,9},{9,8},{10,11... | collective-permute-start | bytes 98312 | tf_op jit(solution)/shard_map/ppermute | solution.py:306
  3.9 16.8 %collective-permute-start.4 = (f32[64,128]{1,0:T(8,128)}, f32[64,128]{1,0:T(8,128)S(1)}, u32[]{:S(2)}, u32[]{:S(2)}) collective-permute-start(f32[64,128]{1,0:T(8,128)} %get-tuple-element.15), channel_id=1, source_target_pairs={{1,2},{2,1},{5,6},{6,5},{9,10},{10,9},{13,14},{14,13},{17,18},{18,... | collective-permute-start | bytes 98312 | tf_op jit(solution)/shard_map/ppermute | solution.py:306
  8.5 5.0 %copy-start.5 = (s32[4,2]{0,1:T(2,128)S(1)}, s32[4,2]{0,1:T(2,128)}, u32[]{:S(2)}) copy-start(s32[4,2]{0,1:T(2,128)} %param.7) | copy-start | bytes 100
  8.5 12.1 %collective-permute-start.1 = (f32[24,128]{1,0:T(8,128)}, f32[24,128]{1,0:T(8,128)S(1)}, u32[]{:S(2)}, u32[]{:S(2)}) collective-permute-start(f32[24,128]{1,0:T(8,128)} %get-tuple-element.12), channel_id=1, source_target_pairs={{0,4},{4,0},{8,12},{12,8},{1,5},{5,1},{9,13},{13,9},{2,6},{6,2},{1... | collective-permute-start | bytes 36872 | tf_op jit(solution)/shard_map/ppermute | solution.py:306
  9.1 11.5 %collective-permute-start.2 = (f32[24,128]{1,0:T(8,128)}, f32[24,128]{1,0:T(8,128)S(1)}, u32[]{:S(2)}, u32[]{:S(2)}) collective-permute-start(f32[24,128]{1,0:T(8,128)} %get-tuple-element.13), channel_id=1, source_target_pairs={{4,8},{8,4},{5,9},{9,5},{6,10},{10,6},{7,11},{11,7},{20,24},{24,20... | collective-permute-start | bytes 36872 | tf_op jit(solution)/shard_map/ppermute | solution.py:306
  20.6 0.6 %copy-start.3 = (f32[24,128]{1,0:T(8,128)}, f32[24,128]{1,0:T(8,128)S(1)}, u32[]{:S(2)}) copy-start(f32[24,128]{1,0:T(8,128)S(1)} %collective-permute-done.1.refs_9_) | copy-start | bytes 36868
  20.6 0.6 %copy-start.4 = (f32[24,128]{1,0:T(8,128)}, f32[24,128]{1,0:T(8,128)S(1)}, u32[]{:S(2)}) copy-start(f32[24,128]{1,0:T(8,128)S(1)} %collective-permute-done.2.refs_10_) | copy-start | bytes 36868
  20.7 0.6 %copy-start.1 = (f32[64,128]{1,0:T(8,128)}, f32[64,128]{1,0:T(8,128)S(1)}, u32[]{:S(2)}) copy-start(f32[64,128]{1,0:T(8,128)S(1)} %collective-permute-done.3.refs_11_) | copy-start | bytes 98308
  20.7 0.6 %copy-start.2 = (f32[64,128]{1,0:T(8,128)}, f32[64,128]{1,0:T(8,128)S(1)}, u32[]{:S(2)}) copy-start(f32[64,128]{1,0:T(8,128)S(1)} %collective-permute-done.4.refs_12_) | copy-start | bytes 98308
  20.7 0.7 %copy-start = (f32[240,128]{1,0:T(8,128)}, f32[240,128]{1,0:T(8,128)S(1)}, u32[]{:S(2)}) copy-start(f32[240,128]{1,0:T(8,128)S(1)} %collective-permute-done.refs_8_) | copy-start | bytes 368644

commit v2 on v0

v2 whole, which is shorter than its diff:
```python
import functools

import jax
import jax.numpy as jnp
from jax import lax
from jax.experimental import pallas as pl
from jax.experimental.pallas import tpu as pltpu
from jax.sharding import PartitionSpec as P

soft_core = 0.01
damp_normal = 0.3
damp_tangent = 0.2
drag_coef = 1.5
diffuse = 0.1
source_gain = 0.5

F32 = jnp.float32
BF16 = jnp.bfloat16
PARTS = 3
LANES = 128
SUBLANES = 8
AXES = ("gx", "gy", "gz")


def split_parts(value):
    parts = []
    for _ in range(PARTS):
        part = value.astype(BF16).astype(F32)
        parts.append(part)
        value = value - part
    return parts


def places(cell, across, along):
    layer = across * along
    if layer & (layer - 1) or along & (along - 1):
        return cell // layer, cell // along % across, cell % along
    shift = along.bit_length() - 1
    high = layer.bit_length() - 1
    return (
        lax.shift_right_logical(cell, high),
        lax.shift_right_logical(cell, shift) & (across - 1),
        cell & (along - 1),
    )


def turn_rows(tile, sign):
    rows = lax.broadcasted_iota(jnp.int32, (SUBLANES, LANES), 0)
    for bit in (1, 2, 4):
        tile = jnp.where(rows & bit != 0, pltpu.roll(tile, sign * bit % LANES, 1), tile)
    return tile


def spread_block(block, store):
    rows = [block[i : i + 1] for i in range(8)]
    rows.append(rows[7] * jnp.sqrt(rows[6]))
    for i, row in enumerate(rows):
        tile = turn_rows(jnp.broadcast_to(row, (SUBLANES, LANES)), 1)
        for t in range(LANES // SUBLANES):
            store[i, t * SUBLANES : (t + 1) * SUBLANES, :] = pltpu.roll(tile, t * SUBLANES, 1) if t else tile


def pair_sum(left, spread, tiles, back):
    rows = [left[i : i + 1] for i in range(8)]
    rows.append((2.0 * damp_tangent) * rows[7] * jnp.sqrt(rows[6]))
    wide = [jnp.broadcast_to(row, (SUBLANES, LANES)) for row in rows]
    subs = lax.broadcasted_iota(jnp.int32, (SUBLANES, LANES), 0)
    total, react = [None] * 3, [None] * 3
    for tile in reversed(range(tiles)):
        there = [spread[i, tile * SUBLANES : (tile + 1) * SUBLANES, :] for i in range(9)]
        ex, ey, ez, wx, wy, wz = [wide[i] - there[i] for i in range(6)]
        square = (ex * ex + ey * ey) + (ez * ez + soft_core)
        inverse = lax.rsqrt(square)
        reach = wide[6] + there[6]
        delta = jnp.maximum(reach - square * inverse, 0.0)
        mass = wide[7] + there[7]
        under = jnp.maximum((delta * reach) * (mass * mass), 1e-30)
        tangent = (wide[8] * there[8]) * (delta * lax.rsqrt(under))
        speed = ((wx * ex + wy * ey) + wz * ez) * inverse
        along = (
            (2.0 / 3.0 / damp_tangent) * delta - ((damp_normal - damp_tangent) / damp_tangent) * speed
        ) * (tangent * inverse)
        for d, (e, w) in enumerate(((ex, wx), (ey, wy), (ez, wz))):
            force = along * e - tangent * w
            total[d] = force if total[d] is None else total[d] + force
            if back:
                if back == "short" and tile == tiles - 1:
                    force = jnp.where(subs == SUBLANES - 1, 0.0, force)
                react[d] = force if react[d] is None else force + pltpu.roll(react[d], LANES - SUBLANES, 1)
    total = [jnp.sum(item, axis=0, keepdims=True) for item in total]
    if back:
        react = [-jnp.sum(turn_rows(item, -1), axis=0, keepdims=True) for item in react]
    return total, react


def blob_layout(across, blocks, pairs):
    bodies = 3 * across
    cells = bodies + 8 * blocks
    shares = cells + blocks
    lists = shares + blocks
    rows = lists + 2 * pairs
    return bodies, cells, shares, lists, rows + -rows % 8


def parities():
    return [lax.rem(lax.axis_index(axis), 2) == 0 for axis in AXES]


def pack_kernel(counts, pair_ref, part_ref, cell_ref, share_ref, fluid_hbm, *refs):
    fluid_ref, outs, sems = refs[0], refs[1:-1], refs[-1]
    height_outs, across_outs, along_outs = by_axis(outs, counts)
    depth, across, along = fluid_ref.shape[1:]
    blocks, pairs = part_ref.shape[0], pair_ref.shape[0]
    bodies, cells, shares, lists, rows = blob_layout(across, blocks, pairs)
    copies = [pltpu.make_async_copy(fluid_hbm.at[c], fluid_ref.at[c], sems.at[c]) for c in range(3)]
    for copy in copies:
        copy.start()
    even = parities()
    for n, out in enumerate(height_outs):
        for b in range(blocks):
            out[bodies + 8 * b : bodies + 8 * b + 8, :] = part_ref[b]
        out[cells:shares, :] = cell_ref[...].astype(F32)
        out[shares:lists, :] = share_ref[...]
        for k in range(pairs):
            for side in range(2):
                row = lists + 2 * k + side
                out[row : row + 1, :] = jnp.full((1, LANES), pair_ref[k, side], jnp.int32).astype(F32)
        used = lists + 2 * pairs
        if used < rows:
            out[used:rows, :] = jnp.zeros((rows - used, LANES), F32)

    lanes = lax.broadcasted_iota(jnp.int32, (across, along), 1)
    first = jnp.zeros((across, along), F32)
    last = jnp.zeros((across, along), F32)
    for c in range(3):
        copies[c].wait()
        for n, out in enumerate(height_outs):
            upward = even[0] if n == 0 else jnp.logical_not(even[0])
            out[c * across : (c + 1) * across, :] = fluid_ref[c, jnp.where(upward, depth - 1, 0)]
        for h in range(depth):
            k = c * depth + h
            here = fluid_ref[c, h]
            for n, out in enumerate(across_outs):
                upward = even[1] if n == 0 else jnp.logical_not(even[1])
                out[k : k + 1, :] = jnp.where(upward, here[across - 1 : across], here[0:1])
            turned = pltpu.roll(here, 2 * k, 1) if k else here
            first = jnp.where(lanes == 2 * k, turned, first)
            last = jnp.where(lanes == (2 * k - 1) % along, turned, last)
    first = pltpu.roll(first, along - 1, 1)
    last = pltpu.roll(last, 1, 1)
    for n, out in enumerate(along_outs):
        upward = even[2] if n == 0 else jnp.logical_not(even[2])
        out[...] = jnp.where(upward, last, first)


def local_kernel(
    blocks, pairs, pair_hbm, blob_ref, fluid_ref, force_ref, next_ref, spread, found, weights, coupled, spots, pair_ref, sem
):
    depth, across, along = fluid_ref.shape[1:]
    listed = pair_ref.shape[1]
    fold = spots.shape[0] // along
    half = across // fold
    wide = blocks * LANES
    bodies, cells, shares, _, _ = blob_layout(across, blocks, pairs)
    copy = pltpu.make_async_copy(pair_hbm, pair_ref, sem)
    copy.start()
    rows = lax.broadcasted_iota(jnp.int32, (across, LANES), 0)
    halves = lax.broadcasted_iota(jnp.int32, (half, LANES), 0)
    sites = lax.broadcasted_iota(jnp.int32, (fold * along, LANES), 0)

    def body_of(b):
        return blob_ref[bodies + 8 * b : bodies + 8 * b + 8, :]

    for b in range(blocks):
        spread_block(body_of(b), spread.at[b])
    for b in range(blocks):
        ahead, behind = pair_sum(pltpu.roll(body_of(b), LANES - 1, 1), spread.at[b], LANES // 2 // SUBLANES, "short")
        for c in range(3):
            force_ref[c, b : b + 1, :] = pltpu.roll(ahead[c], 1, 1) + behind[c]

        height, over, spot = places(blob_ref[cells + b : cells + b + 1, :].astype(jnp.int32), across, along)
        share = blob_ref[shares + b : shares + b + 1, :]
        index = jnp.broadcast_to(spot, (across, LANES))
        mask = rows == over
        column = slice(b * LANES, (b + 1) * LANES)
        near = [
            jnp.where(height == h, 1.0 - share, jnp.where(height == h - 1, share, 0.0)) for h in range(depth)
        ]
        one_hot = jnp.where(sites == jnp.where(over >= half, along, 0) + spot, 1.0, 0.0).astype(BF16)
        for n in range(PARTS):
            spots[:, n * wide + b * LANES : n * wide + (b + 1) * LANES] = one_hot
        ones = jnp.where(halves == jnp.where(over >= half, over - half, over), 1.0, 0.0).astype(BF16)
        for c in range(3):
            total = jnp.zeros((SUBLANES, LANES), F32)
            for h in range(depth):
                seen = jnp.take_along_axis(fluid_ref[c, h], index, axis=1)
                seen = jnp.where(mask, seen, 0.0)
                total += near[h] * jnp.sum(seen.reshape(across // SUBLANES, SUBLANES, LANES), axis=0)
            met = jnp.sum(total, axis=0, keepdims=True)
            drag = drag_coef * blob_ref[bodies + 8 * b + 6 : bodies + 8 * b + 7, :] * (
                met - blob_ref[bodies + 8 * b + 3 + c : bodies + 8 * b + 4 + c, :]
            )
            force_ref[c, b : b + 1, :] += drag
            for h in range(depth):
                weights[c * depth + h : c * depth + h + 1, column] = (-source_gain) * near[h] * drag
        for n, part in enumerate(split_parts(weights[:, column])):
            for k in range(3 * depth):
                line = jnp.broadcast_to(part[k : k + 1], (16, LANES)).astype(BF16)
                line = jnp.concatenate([line] * (half // 16), axis=0)
                coupled[k * half : (k + 1) * half, n * wide + b * LANES : n * wide + (b + 1) * LANES] = ones * line

    copy.wait()
    for i in range(listed):
        a, c = pair_ref[0, i], pair_ref[1, i]
        left = blob_ref[pl.ds(pl.multiple_of(bodies + 8 * a, 8), 8), :]
        ahead, behind = pair_sum(left, spread.at[c], LANES // SUBLANES, "all")
        for side, (block, forces) in enumerate(((a, ahead), (c, behind))):
            for d in range(3):
                found[2 * i + side, d : d + 1, :] = forces[d]
    for b in range(blocks):
        for d in range(3):
            total = force_ref[d, b : b + 1, :]
            for i in range(listed):
                for side in range(2):
                    total += jnp.where(pair_ref[side, i] == b, found[2 * i + side, d : d + 1, :], 0.0)
            force_ref[d, b : b + 1, :] = total

    lanes = lax.broadcasted_iota(jnp.int32, (across, along), 1)
    downs = lax.broadcasted_iota(jnp.int32, (across, along), 0)
    for c in range(3):
        source = lax.dot_general(
            coupled[c * depth * half : (c + 1) * depth * half, :],
            spots[...],
            (((1,), (1,)), ((), ())),
            preferred_element_type=F32,
        )
        for h in range(depth):
            here = fluid_ref[c, h]
            beside = jnp.where(downs == 0, 0.0, pltpu.roll(here, 1, 0))
            beside += jnp.where(downs == across - 1, 0.0, pltpu.roll(here, across - 1, 0))
            beside += jnp.where(lanes == 0, 0.0, pltpu.roll(here, 1, 1))
            beside += jnp.where(lanes == along - 1, 0.0, pltpu.roll(here, along - 1, 1))
            if h > 0:
                beside += fluid_ref[c, h - 1]
            if h < depth - 1:
                beside += fluid_ref[c, h + 1]
            given = [
                source[h * half : (h + 1) * half, f * along : (f + 1) * along] for f in range(fold)
            ]
            next_ref[c, h] = here + diffuse * (beside - 6.0 * here) + jnp.concatenate(given, axis=0)


def finish_kernel(counts, blocks, pairs, force_ref, partial_ref, *refs):
    n_in = sum(counts)
    sent = refs[: counts[0]]
    height_ins, across_ins, along_ins = by_axis(refs[counts[0] : counts[0] + n_in], counts)
    out_force, next_hbm, next_ref, spread, coupled, spots, sems = refs[counts[0] + n_in :]
    depth, across, along = partial_ref.shape[1:]
    fold = spots.shape[0] // along
    half = across // fold
    wide = blocks * LANES
    bodies, cells, shares, lists, _ = blob_layout(across, blocks, pairs)
    even = parities()

    def ordered(arrived, axis):
        first = arrived[0][...]
        if len(arrived) == 1:
            return jnp.where(even[axis], 0.0, first), jnp.where(even[axis], first, 0.0)
        second = arrived[1][...]
        return jnp.where(even[axis], second, first), jnp.where(even[axis], first, second)

    across_low, across_high = ordered(across_ins, 1)
    across_low = diffuse * across_low
    across_high = diffuse * across_high
    edges = along_ins[0][...]
    if len(along_ins) > 1:
        edges = edges + along_ins[1][...]
    edges = diffuse * edges
    lanes = lax.broadcasted_iota(jnp.int32, (across, along), 1)
    downs = lax.broadcasted_iota(jnp.int32, (across, along), 0)
    rim = jnp.logical_or(lanes == 0, lanes == along - 1)
    copies = []
    for c in range(3):
        for h in range(depth):
            k = c * depth + h
            value = partial_ref[c, h]
            value += jnp.where(rim, pltpu.roll(edges, (along - 2 * k) % along, 1) if k else edges, 0.0)
            value += jnp.where(downs == 0, across_low[k : k + 1, :], 0.0)
            value += jnp.where(downs == across - 1, across_high[k : k + 1, :], 0.0)
            next_ref[c, h] = value
        if depth > 2:
            inner = pl.ds(1, depth - 2)
            copies.append(pltpu.make_async_copy(next_ref.at[c, inner], next_hbm.at[c, inner], sems.at[c]))
            copies[-1].start()

    rows = lax.broadcasted_iota(jnp.int32, (across, LANES), 0)
    halves = lax.broadcasted_iota(jnp.int32, (half, LANES), 0)
    sites = lax.broadcasted_iota(jnp.int32, (fold * along, LANES), 0)
    coupling = [[jnp.zeros((1, LANES), F32)] * blocks for _ in range(3)]
    for n, blob in enumerate(height_ins):
        own = sent[n]
        above = even[0] if n == 0 else jnp.logical_not(even[0])
        own_layer = jnp.where(above, depth - 1, 0)
        for b in range(blocks):
            cell = jnp.where(above, own[cells + b : cells + b + 1, :], blob[cells + b : cells + b + 1, :])
            share = jnp.where(above, own[shares + b : shares + b + 1, :], blob[shares + b : shares + b + 1, :])
            body = slice(bodies + 8 * b, bodies + 8 * b + 8)
            owner = jnp.where(above, own[body, :], blob[body, :])
            height, over, spot = places(cell.astype(jnp.int32), across, along)
            top = height == depth - 1
            below = jnp.logical_not(above)
            index = jnp.broadcast_to(spot, (across, LANES))
            mask = rows == over
            seen_share = jnp.where(top, jnp.where(above, share, 1.0 - share), 0.0)
            home_share = jnp.where(jnp.logical_and(top, below), share, 0.0)
            given_share = (-source_gain) * jnp.where(above, 1.0 - share, share)
            own_share = jnp.where(jnp.logical_and(top, below), 1.0, 0.0)
            one_hot = jnp.where(sites == jnp.where(over >= half, along, 0) + spot, 1.0, 0.0).astype(BF16)
            for m in range(PARTS):
                spots[:, m * wide + b * LANES : m * wide + (b + 1) * LANES] = one_hot
            ones = jnp.where(halves == jnp.where(over >= half, over - half, over), 1.0, 0.0).astype(BF16)
            for c in range(3):
                face = slice(c * across, (c + 1) * across)
                seen = jnp.take_along_axis(blob[face, :], index, axis=1)
                home = jnp.take_along_axis(own[face, :], index, axis=1)
                met = jnp.where(mask, seen_share * seen + home_share * home, 0.0)
                met = jnp.sum(met, axis=0, keepdims=True)
                drag = drag_coef * owner[6:7] * (met - own_share * owner[3 + c : 4 + c])
                coupling[c][b] += jnp.where(above, drag, 0.0)
                for m, part in enumerate(split_parts(given_share * drag)):
                    line = jnp.broadcast_to(part, (16, LANES)).astype(BF16)
                    line = jnp.concatenate([line] * (half // 16), axis=0)
                    coupled[c * half : (c + 1) * half, m * wide + b * LANES : m * wide + (b + 1) * LANES] = (
                        ones * line
                    )
        source = lax.dot_general(
            coupled[...], spots[...], (((1,), (1,)), ((), ())), preferred_element_type=F32
        )
        for c in range(3):
            given = [source[c * half : (c + 1) * half, f * along : (f + 1) * along] for f in range(fold)]
            next_ref[c, own_layer] += diffuse * blob[c * across : (c + 1) * across, :] + jnp.concatenate(given, axis=0)
    for n, h in enumerate(sorted({0, depth - 1})):
        copies.append(pltpu.make_async_copy(next_ref.at[:, h], next_hbm.at[:, h], sems.at[3 + n]))
        copies[-1].start()

    for n, blob in enumerate(height_ins):
        own = sent[n]
        above = even[0] if n == 0 else jnp.logical_not(even[0])
        for k in range(pairs):
            ours = [own[lists + 2 * k + side : lists + 2 * k + side + 1, :] for side in range(2)]
            theirs = [blob[lists + 2 * k + side : lists + 2 * k + side + 1, :] for side in range(2)]
            to = jnp.where(above, ours[0], theirs[1])
            by = jnp.where(above, ours[1], theirs[0])
            left = own[bodies : bodies + 8, :]
            right = blob[bodies : bodies + 8, :]
            for b in range(1, blocks):
                body = slice(bodies + 8 * b, bodies + 8 * b + 8)
                left = jnp.where(to == b, own[body, :], left)
                right = jnp.where(by == b, blob[body, :], right)
            spread_block(right, spread.at[n * pairs + k])
            force, _ = pair_sum(left, spread.at[n * pairs + k], LANES // SUBLANES, None)
            for b in range(blocks):
                for c in range(3):
                    coupling[c][b] += jnp.where(to == b, force[c], 0.0)
    for b in range(blocks):
        for c in range(3):
            out_force[c, b : b + 1, :] = force_ref[c, b : b + 1, :] + coupling[c][b]
    for copy in copies:
        copy.wait()


def by_axis(refs, counts):
    groups, at = [], 0
    for n in counts:
        groups.append(refs[at : at + n])
        at += n
    return groups


def exchange(payloads, axis):
    count = lax.axis_size(axis)
    results = []
    for n, payload in enumerate(payloads):
        route = []
        for i in range(n, count - 1, 2):
            route += [(i, i + 1), (i + 1, i)]
        results.append(lax.ppermute(payload, axis, route))
    return results


def body(particles, local_pairs, cross_pairs, drag_cell, drag_share, fluid):
    blocks = particles.shape[0]
    pairs = cross_pairs.shape[0]
    listed = local_pairs.shape[0]
    _, depth, across, along = fluid.shape
    counts = [min(2, lax.axis_size(axis) - 1) for axis in AXES]
    fold = 2 if across % 32 == 0 else 1
    half = across // fold
    wide = PARTS * blocks * LANES
    rows = blob_layout(across, blocks, pairs)[-1]
    shapes = [(rows, along), (3 * depth, along), (across, along)]
    vmem = pl.BlockSpec(memory_space=pltpu.VMEM)
    smem = pl.BlockSpec(memory_space=pltpu.SMEM)
    hbm = pl.BlockSpec(memory_space=pl.ANY)

    def kept(value):
        return pltpu.with_memory_space_constraint(value, pltpu.VMEM)

    fluid_kept, *packed = pl.pallas_call(
        functools.partial(pack_kernel, counts),
        out_shape=[pltpu.VMEM(fluid.shape, F32)]
        + [pltpu.VMEM(shape, F32) for shape, n in zip(shapes, counts) for _ in range(n)],
        in_specs=[smem, vmem, vmem, vmem, hbm],
        out_specs=[vmem] * (1 + sum(counts)),
        scratch_shapes=[pltpu.SemaphoreType.DMA((3,))],
        name="pack",
    )(cross_pairs, particles, drag_cell, drag_share, fluid)
    received = []
    for axis, payloads in zip(AXES, by_axis(packed, counts)):
        received += exchange(payloads, axis)

    force, partial = pl.pallas_call(
        functools.partial(local_kernel, blocks, pairs),
        out_shape=[pltpu.VMEM((3, blocks, LANES), F32), pltpu.VMEM(fluid.shape, F32)],
        in_specs=[hbm, vmem, vmem],
        out_specs=[vmem, vmem],
        scratch_shapes=[
            pltpu.VMEM((blocks, 9, LANES, LANES), F32),
            pltpu.VMEM((2 * listed, SUBLANES, LANES), F32),
            pltpu.VMEM((3 * depth, blocks * LANES), F32),
            pltpu.VMEM((3 * depth * half, wide), BF16),
            pltpu.VMEM((fold * along, wide), BF16),
            pltpu.SMEM((2, listed), jnp.int32),
            pltpu.SemaphoreType.DMA,
        ],
        name="local",
    )(local_pairs.T, kept(packed[0]), kept(fluid_kept))

    out_force, out_next = pl.pallas_call(
        functools.partial(finish_kernel, counts, blocks, pairs),
        out_shape=[
            jax.ShapeDtypeStruct((3, blocks, LANES), F32),
            jax.ShapeDtypeStruct(fluid.shape, F32),
        ],
        in_specs=[vmem] * (2 + counts[0] + len(received)),
        out_specs=[vmem, hbm],
        scratch_shapes=[
            pltpu.VMEM(fluid.shape, F32),
            pltpu.VMEM((counts[0] * pairs, 9, LANES, LANES), F32),
            pltpu.VMEM((3 * half, wide), BF16),
            pltpu.VMEM((fold * along, wide), BF16),
            pltpu.SemaphoreType.DMA((5,)),
        ],
        name="finish",
    )(*[kept(value) for value in [force, partial, *packed[: counts[0]], *received]])
    return jnp.transpose(out_force, (1, 0, 2)), out_next


def solution(mesh):
    in_specs = (
        P(("gx", "gy", "gz"), None, None),
        P(("gx", "gy", "gz"), None),
        P(("gx", "gy", "gz"), None),
        P(("gx", "gy", "gz"), None),
        P(("gx", "gy", "gz"), None),
        P(None, "gx", "gy", "gz"),
    )
    out_specs = (P(("gx", "gy", "gz"), None, None), P(None, "gx", "gy", "gz"))
    return jax.shard_map(body, mesh=mesh, in_specs=in_specs, out_specs=out_specs, check_vma=False)
```

time: 260 us -> 28.8 us (0.11)
  local copies, waits for them, and re-layouts: 148 us -> 0 us
  other arithmetic: 86.7 us -> 0 us
  Pallas kernels: 0 us -> 17.8 us
  starting transfers between devices: 21.3 us -> 10.1 us
    reshape x4 -> x0, local copies, waits for them, and re-layouts: 50.4 us -> none  [the longest x2 25.1 us: body(): flat = padded.reshape(3, -1)]
    scatter-add x6 -> x0, other arithmetic: 47.6 us -> none  [the longest x1 27.6 us: body(): deposit = deposit.at[:, drag_cell + layer].add(drag_share * terms)]
    gather x8 -> x0, local copies, waits for them, and re-layouts: 36.9 us -> none  [the longest x2 16.3 us: body(): flat[:, upper_index]]
    slice x12 -> x0, local copies, waits for them, and re-layouts: 27.8 us -> none  [the longest x1 22.3 us: body(): deposit[:, :depth * layer].reshape(3, depth, across_count, along_count)]
    pallas_call x0 -> x3, Pallas kernels: none -> 17.8 us  [the longest x1 11.3 us: body(): pl.pallas_call(functools.partial(local_kernel, blocks, pairs), out_shape=...]
    add x2 -> x0, other arithmetic: 15.4 us -> none  [the longest x1 13.7 us: body(): fluid_next = fluid + diffuse * (beside - 6.0 * fluid) + source_gain * source]
    unnamed x78 -> x0, local copies, waits for them, and re-layouts: 13 us -> none
    ppermute x9 -> x5, starting transfers between devices: 21.3 us -> 10.1 us  [exchange(): results.append(lax.ppermute(payload, axis, route))]
  transfers between devices with their start and end apart: 9 -> 5, of which waited for: 0 -> 0; matrix products, arithmetic and copies ran while one was open for 57% -> 0% of each run, Pallas kernels for 0% -> 39%
where the time goes in v2:
time: 28.8 us; the launch traced here: 28.6 us
  Pallas kernels  17.8 us (62%)
  starting transfers between devices  10.1 us (35%)
  between operations  0.71 us (2%)
    pallas_call x1, Pallas kernels, body(): pl.pallas_call(functools.partial(local_kernel, blocks, pairs), out_shape=...  11.3 us
    ppermute x5, starting transfers between devices, exchange(): results.append(lax.ppermute(payload, axis, route))  10.1 us
    pallas_call x1, Pallas kernels, body(): pl.pallas_call(functools.partial(finish_kernel, counts, blocks, pairs), o...  4.22 us
    pallas_call x1, Pallas kernels, body(): pl.pallas_call(functools.partial(pack_kernel, counts), out_shape=[pltpu.V...  2.28 us
  transfers between devices with their start and end apart: 5, of which 0 were waited for; matrix products, arithmetic and copies ran while one was open for 0% of the time, Pallas kernels for 39%

profile of v2, /device:TPU:10, one launch (start us, length us, event | category | flops | bytes accessed | tf_op | source)
XLA Modules:
  0.0 28.6 jit_solution(5767213255848595571)
XLA Ops:
  0.6 2.3 %pack.1 = (f32[3,8,64,128]{3,2,1,0:T(8,128)S(1)}, f32[240,128]{1,0:T(8,128)S(1)}, f32[24,128]{1,0:T(8,128)S(1)}, f32[24,128]{1,0:T(8,128)S(1)}, f32[64,128]{1,0:T(8,128)S(1)}, /*index=5*/f32[64,128]{1,0:T(8,128)S(1)}) custom-call(s32[2,2]{1,0:T(2,128)} %pair_ref.1, f32[4,8,128]{2,1,0:T(8,128)} %part_ref.1, s32[4,128]{1,0:T(4,128)} %cell_ref.1, ...), custom_call_target="tpu_custom_call" | custom-call | tf_op jit(solution)/shard_map/pack/pallas_call | solution.py:409
  2.9 0.1 collective-permute-start
  3.0 0.5 %collective-permute-start.3 = (f32[64,128]{1,0:T(8,128)S(1)}, f32[64,128]{1,0:T(8,128)S(1)}, u32[]{:S(2)}, u32[]{:S(2)}) collective-permute-start(f32[64,128]{1,0:T(8,128)S(1)} %get-tuple-element.18), channel_id=1, source_target_pairs={{0,1},{1,0},{2,3},{3,2},{4,5},{5,4},{6,7},{7,6},{8,9},{9,8},{10,11... | collective-permute-start | bytes 98312 | tf_op jit(solution)/shard_map/ppermute | solution.py:387
  3.5 4.6 %collective-permute-start.4 = (f32[64,128]{1,0:T(8,128)S(1)}, f32[64,128]{1,0:T(8,128)S(1)}, u32[]{:S(2)}, u32[]{:S(2)}) collective-permute-start(f32[64,128]{1,0:T(8,128)S(1)} %get-tuple-element.19), channel_id=1, source_target_pairs={{1,2},{2,1},{5,6},{6,5},{9,10},{10,9},{13,14},{14,13},{17,18},{18,... | collective-permute-start | bytes 98312 | tf_op jit(solution)/shard_map/ppermute | solution.py:387
  8.1 0.6 %collective-permute-start.1 = (f32[24,128]{1,0:T(8,128)S(1)}, f32[24,128]{1,0:T(8,128)S(1)}, u32[]{:S(2)}, u32[]{:S(2)}) collective-permute-start(f32[24,128]{1,0:T(8,128)S(1)} %get-tuple-element.16), channel_id=1, source_target_pairs={{0,4},{4,0},{8,12},{12,8},{1,5},{5,1},{9,13},{13,9},{2,6},{6,2},{1... | collective-permute-start | bytes 36872 | tf_op jit(solution)/shard_map/ppermute | solution.py:387
  8.7 4.3 %collective-permute-start.2 = (f32[24,128]{1,0:T(8,128)S(1)}, f32[24,128]{1,0:T(8,128)S(1)}, u32[]{:S(2)}, u32[]{:S(2)}) collective-permute-start(f32[24,128]{1,0:T(8,128)S(1)} %get-tuple-element.17), channel_id=1, source_target_pairs={{4,8},{8,4},{5,9},{9,5},{6,10},{10,6},{7,11},{11,7},{20,24},{24,20... | collective-permute-start | bytes 36872 | tf_op jit(solution)/shard_map/ppermute | solution.py:387
  13.1 11.3 %local.1 = (f32[3,4,128]{2,1,0:T(4,128)S(1)}, f32[3,8,64,128]{3,2,1,0:T(8,128)S(1)}) custom-call(s32[2,4]{1,0:T(2,128)} %bitcast.2, f32[240,128]{1,0:T(8,128)S(1)} %get-tuple-element.12.blob_ref.refs_0_, f32[3,8,64,128]{3,2,1,0:T(8,128)S(1)} %get-tuple-element.13.fluid_ref), custom_call_target="tpu_custom_call" | custom-call | tf_op jit(solution)/shard_map/local/pallas_call | solution.py:422
  24.3 0.0 collective-permute-done.1.refs_2_
  24.4 0.0 collective-permute-done.2.refs_3_
  24.4 0.0 collective-permute-done.3.refs_4_
  24.4 0.0 collective-permute-done.4.refs_5_
  24.4 0.0 collective-permute-done.refs_1_
  24.4 4.2 %finish.1 = (f32[3,4,128]{2,1,0:T(4,128)}, f32[3,8,64,128]{3,2,1,0:T(8,128)}) custom-call(f32[3,4,128]{2,1,0:T(4,128)S(1)} %get-tuple-element.14.force_ref, f32[3,8,64,128]{3,2,1,0:T(8,128)S(1)} %get-tuple-element.15.partial_ref, f32[240,128]{1,0:T(8,128)S(1)} %get-tuple-element.12.blob_ref.refs_0_, f32[240,128]{1,0:T(8,128)S(1)} %collective-permute-done.refs_1_, ...), custom_call_target="tpu_custom_call" | custom-call | tf_op jit(solution)/shard_map/finish/pallas_call | solution.py:439
Async XLA Ops:
  2.9 21.5 %collective-permute-start = (f32[240,128]{1,0:T(8,128)S(1)}, f32[240,128]{1,0:T(8,128)S(1)}, u32[]{:S(2)}, u32[]{:S(2)}) collective-permute-start(f32[240,128]{1,0:T(8,128)S(1)} %get-tuple-element.12.blob_ref.refs_0_), channel_id=1, source_target_pairs={{0,16},{16,0},{1,17},{17,1},{2,18},{18,2},{3,19},{19,3},{4,20},{20... | collective-permute-start | bytes 368648 | tf_op jit(solution)/shard_map/ppermute | solution.py:387
  3.0 21.4 %collective-permute-start.3 = (f32[64,128]{1,0:T(8,128)S(1)}, f32[64,128]{1,0:T(8,128)S(1)}, u32[]{:S(2)}, u32[]{:S(2)}) collective-permute-start(f32[64,128]{1,0:T(8,128)S(1)} %get-tuple-element.18), channel_id=1, source_target_pairs={{0,1},{1,0},{2,3},{3,2},{4,5},{5,4},{6,7},{7,6},{8,9},{9,8},{10,11... | collective-permute-start | bytes 98312 | tf_op jit(solution)/shard_map/ppermute | solution.py:387
  3.5 20.9 %collective-permute-start.4 = (f32[64,128]{1,0:T(8,128)S(1)}, f32[64,128]{1,0:T(8,128)S(1)}, u32[]{:S(2)}, u32[]{:S(2)}) collective-permute-start(f32[64,128]{1,0:T(8,128)S(1)} %get-tuple-element.19), channel_id=1, source_target_pairs={{1,2},{2,1},{5,6},{6,5},{9,10},{10,9},{13,14},{14,13},{17,18},{18,... | collective-permute-start | bytes 98312 | tf_op jit(solution)/shard_map/ppermute | solution.py:387
  8.1 16.2 %collective-permute-start.1 = (f32[24,128]{1,0:T(8,128)S(1)}, f32[24,128]{1,0:T(8,128)S(1)}, u32[]{:S(2)}, u32[]{:S(2)}) collective-permute-start(f32[24,128]{1,0:T(8,128)S(1)} %get-tuple-element.16), channel_id=1, source_target_pairs={{0,4},{4,0},{8,12},{12,8},{1,5},{5,1},{9,13},{13,9},{2,6},{6,2},{1... | collective-permute-start | bytes 36872 | tf_op jit(solution)/shard_map/ppermute | solution.py:387
  8.7 15.6 %collective-permute-start.2 = (f32[24,128]{1,0:T(8,128)S(1)}, f32[24,128]{1,0:T(8,128)S(1)}, u32[]{:S(2)}, u32[]{:S(2)}) collective-permute-start(f32[24,128]{1,0:T(8,128)S(1)} %get-tuple-element.17), channel_id=1, source_target_pairs={{4,8},{8,4},{5,9},{9,5},{6,10},{10,6},{7,11},{11,7},{20,24},{24,20... | collective-permute-start | bytes 36872 | tf_op jit(solution)/shard_map/ppermute | solution.py:387

commit v3 on v2

--- a/solution.py
+++ b/solution.py
@@ -44,30 +44,38 @@
     )
 
 
-def turn_rows(tile, sign):
-    rows = lax.broadcasted_iota(jnp.int32, (SUBLANES, LANES), 0)
-    for bit in (1, 2, 4):
-        tile = jnp.where(rows & bit != 0, pltpu.roll(tile, sign * bit % LANES, 1), tile)
-    return tile
-
-
-def spread_block(block, store):
-    rows = [block[i : i + 1] for i in range(8)]
-    rows.append(rows[7] * jnp.sqrt(rows[6]))
-    for i, row in enumerate(rows):
-        tile = turn_rows(jnp.broadcast_to(row, (SUBLANES, LANES)), 1)
-        for t in range(LANES // SUBLANES):
-            store[i, t * SUBLANES : (t + 1) * SUBLANES, :] = pltpu.roll(tile, t * SUBLANES, 1) if t else tile
-
-
-def pair_sum(left, spread, tiles, back):
+def parts_of(value):
+    return jnp.concatenate([part.astype(BF16) for part in split_parts(value)], axis=1)
+
+
+def spread_blocks(blocks):
+    columns = []
+    for block in blocks:
+        rows = jnp.concatenate([block, block[7:8] * jnp.sqrt(block[6:7])], axis=0)
+        parts = split_parts(rows)
+        parts.append(jnp.zeros((32 - 9 * PARTS, LANES), F32))
+        columns.append(jnp.transpose(jnp.concatenate(parts, axis=0)).astype(BF16))
+    lines = lax.broadcasted_iota(jnp.int32, (32, LANES), 0)
+    picks = []
+    for i in range(9):
+        pick = lines == i
+        for n in range(1, PARTS):
+            pick = jnp.logical_or(pick, lines == i + 9 * n)
+        picks.append(jnp.where(pick, 1.0, 0.0).astype(BF16))
+    return jnp.dot(
+        jnp.concatenate(columns, axis=0), jnp.concatenate(picks, axis=1), preferred_element_type=F32
+    )
+
+
+def pair_sum(left, spread, start, react):
     rows = [left[i : i + 1] for i in range(8)]
     rows.append((2.0 * damp_tangent) * rows[7] * jnp.sqrt(rows[6]))
     wide = [jnp.broadcast_to(row, (SUBLANES, LANES)) for row in rows]
-    subs = lax.broadcasted_iota(jnp.int32, (SUBLANES, LANES), 0)
-    total, react = [None] * 3, [None] * 3
-    for tile in reversed(range(tiles)):
-        there = [spread[i, tile * SUBLANES : (tile + 1) * SUBLANES, :] for i in range(9)]
+    lanes = lax.broadcasted_iota(jnp.int32, (SUBLANES, LANES), 1)
+    total = [None] * 3
+    for tile in range(LANES // SUBLANES):
+        place = pl.ds(pl.multiple_of(start + tile * SUBLANES, SUBLANES), SUBLANES)
+        there = [spread[place, i * LANES : (i + 1) * LANES] for i in range(9)]
         ex, ey, ez, wx, wy, wz = [wide[i] - there[i] for i in range(6)]
         square = (ex * ex + ey * ey) + (ez * ez + soft_core)
         inverse = lax.rsqrt(square)
@@ -80,17 +88,20 @@
         along = (
             (2.0 / 3.0 / damp_tangent) * delta - ((damp_normal - damp_tangent) / damp_tangent) * speed
         ) * (tangent * inverse)
+        column = None
         for d, (e, w) in enumerate(((ex, wx), (ey, wy), (ez, wz))):
             force = along * e - tangent * w
             total[d] = force if total[d] is None else total[d] + force
-            if back:
-                if back == "short" and tile == tiles - 1:
-                    force = jnp.where(subs == SUBLANES - 1, 0.0, force)
-                react[d] = force if react[d] is None else force + pltpu.roll(react[d], LANES - SUBLANES, 1)
+            if react is not None:
+                across_sum = jnp.broadcast_to(jnp.sum(force, axis=1, keepdims=True), (SUBLANES, LANES))
+                column = across_sum if column is None else jnp.where(lanes == d, across_sum, column)
+        if react is not None:
+            react[tile * SUBLANES : (tile + 1) * SUBLANES, :] = column
     total = [jnp.sum(item, axis=0, keepdims=True) for item in total]
-    if back:
-        react = [-jnp.sum(turn_rows(item, -1), axis=0, keepdims=True) for item in react]
-    return total, react
+    if react is None:
+        return total, None
+    turned = jnp.transpose(react[...])
+    return total, [-turned[d : d + 1] for d in range(3)]
 
 
 def blob_layout(across, blocks, pairs):
@@ -106,16 +117,22 @@
     return [lax.rem(lax.axis_index(axis), 2) == 0 for axis in AXES]
 
 
-def pack_kernel(counts, pair_ref, part_ref, cell_ref, share_ref, fluid_hbm, *refs):
-    fluid_ref, outs, sems = refs[0], refs[1:-1], refs[-1]
+def pack_kernel(counts, pair_hbm, part_hbm, cell_hbm, share_hbm, fluid_hbm, *refs):
+    n_out = 1 + sum(counts)
+    fluid_ref, outs = refs[0], refs[1:n_out]
+    pair_ref, part_ref, cell_ref, share_ref, sems = refs[n_out:]
     height_outs, across_outs, along_outs = by_axis(outs, counts)
     depth, across, along = fluid_ref.shape[1:]
     blocks, pairs = part_ref.shape[0], pair_ref.shape[0]
     bodies, cells, shares, lists, rows = blob_layout(across, blocks, pairs)
     copies = [pltpu.make_async_copy(fluid_hbm.at[c], fluid_ref.at[c], sems.at[c]) for c in range(3)]
-    for copy in copies:
+    small = [(pair_hbm, pair_ref), (part_hbm, part_ref), (cell_hbm, cell_ref), (share_hbm, share_ref)]
+    small = [pltpu.make_async_copy(source, target, sems.at[3 + n]) for n, (source, target) in enumerate(small)]
+    for copy in copies + small:
         copy.start()
     even = parities()
+    for copy in small:
+        copy.wait()
     for n, out in enumerate(height_outs):
         for b in range(blocks):
             out[bodies + 8 * b : bodies + 8 * b + 8, :] = part_ref[b]
@@ -153,8 +170,18 @@
         out[...] = jnp.where(upward, last, first)
 
 
+def lane_one_hot(sites, target):
+    return jnp.where(sites == target, 1.0, 0.0).astype(BF16)
+
+
+def place_lines(ones, part, half):
+    line = jnp.broadcast_to(part, (16, LANES)).astype(BF16)
+    return ones * jnp.concatenate([line] * (half // 16), axis=0)
+
+
 def local_kernel(
-    blocks, pairs, pair_hbm, blob_ref, fluid_ref, force_ref, next_ref, spread, found, weights, coupled, spots, pair_ref, sem
+    blocks, pairs, pair_hbm, blob_ref, fluid_ref, force_ref, next_ref,
+    spread, react, pieces, seen_ref, picks, found, weights, coupled, spots, pair_ref, sem,
 ):
     depth, across, along = fluid_ref.shape[1:]
     listed = pair_ref.shape[1]
@@ -167,34 +194,64 @@
     rows = lax.broadcasted_iota(jnp.int32, (across, LANES), 0)
     halves = lax.broadcasted_iota(jnp.int32, (half, LANES), 0)
     sites = lax.broadcasted_iota(jnp.int32, (fold * along, LANES), 0)
+    lanes = lax.broadcasted_iota(jnp.int32, (across, along), 1)
+    downs = lax.broadcasted_iota(jnp.int32, (across, along), 0)
+    slabs = [(c, h) for c in range(3) for h in range(depth)]
 
     def body_of(b):
         return blob_ref[bodies + 8 * b : bodies + 8 * b + 8, :]
 
+    def spot_of(b):
+        return places(blob_ref[cells + b : cells + b + 1, :].astype(jnp.int32), across, along)
+
+    def stencil(c, h):
+        here = fluid_ref[c, h]
+        beside = jnp.where(downs == 0, 0.0, pltpu.roll(here, 1, 0))
+        beside += jnp.where(downs == across - 1, 0.0, pltpu.roll(here, across - 1, 0))
+        beside += jnp.where(lanes == 0, 0.0, pltpu.roll(here, 1, 1))
+        beside += jnp.where(lanes == along - 1, 0.0, pltpu.roll(here, along - 1, 1))
+        if h > 0:
+            beside += fluid_ref[c, h - 1]
+        if h < depth - 1:
+            beside += fluid_ref[c, h + 1]
+        next_ref[c, h] = here + diffuse * (beside - 6.0 * here)
+
+    spread[...] = spread_blocks([body_of(b) for b in range(blocks)])
+    for k, (c, h) in enumerate(slabs):
+        pieces[k * across : (k + 1) * across, :] = parts_of(fluid_ref[c, h])
     for b in range(blocks):
-        spread_block(body_of(b), spread.at[b])
+        height, over, spot = spot_of(b)
+        column = slice(b * LANES, (b + 1) * LANES)
+        one_hot = lane_one_hot(sites[:along], spot)
+        for n in range(PARTS):
+            picks[n * along : (n + 1) * along, column] = one_hot
+        one_hot = lane_one_hot(sites, jnp.where(over >= half, along, 0) + spot)
+        for n in range(PARTS):
+            spots[:, n * wide + b * LANES : n * wide + (b + 1) * LANES] = one_hot
+    seen_ref[...] = jnp.dot(pieces[...], picks[...], preferred_element_type=F32)
+
+    turns = blocks + listed
+    share_out = [slabs[i * len(slabs) // turns : (i + 1) * len(slabs) // turns] for i in range(turns)]
     for b in range(blocks):
-        ahead, behind = pair_sum(pltpu.roll(body_of(b), LANES - 1, 1), spread.at[b], LANES // 2 // SUBLANES, "short")
+        for c, h in share_out[b]:
+            stencil(c, h)
+        force, _ = pair_sum(body_of(b), spread, b * LANES, None)
         for c in range(3):
-            force_ref[c, b : b + 1, :] = pltpu.roll(ahead[c], 1, 1) + behind[c]
-
-        height, over, spot = places(blob_ref[cells + b : cells + b + 1, :].astype(jnp.int32), across, along)
+            force_ref[c, b : b + 1, :] = force[c]
+
+    for b in range(blocks):
+        height, over, _ = spot_of(b)
         share = blob_ref[shares + b : shares + b + 1, :]
-        index = jnp.broadcast_to(spot, (across, LANES))
         mask = rows == over
         column = slice(b * LANES, (b + 1) * LANES)
         near = [
             jnp.where(height == h, 1.0 - share, jnp.where(height == h - 1, share, 0.0)) for h in range(depth)
         ]
-        one_hot = jnp.where(sites == jnp.where(over >= half, along, 0) + spot, 1.0, 0.0).astype(BF16)
-        for n in range(PARTS):
-            spots[:, n * wide + b * LANES : n * wide + (b + 1) * LANES] = one_hot
-        ones = jnp.where(halves == jnp.where(over >= half, over - half, over), 1.0, 0.0).astype(BF16)
         for c in range(3):
             total = jnp.zeros((SUBLANES, LANES), F32)
             for h in range(depth):
-                seen = jnp.take_along_axis(fluid_ref[c, h], index, axis=1)
-                seen = jnp.where(mask, seen, 0.0)
+                k = c * depth + h
+                seen = jnp.where(mask, seen_ref[k * across : (k + 1) * across, column], 0.0)
                 total += near[h] * jnp.sum(seen.reshape(across // SUBLANES, SUBLANES, LANES), axis=0)
             met = jnp.sum(total, axis=0, keepdims=True)
             drag = drag_coef * blob_ref[bodies + 8 * b + 6 : bodies + 8 * b + 7, :] * (
@@ -203,18 +260,30 @@
             force_ref[c, b : b + 1, :] += drag
             for h in range(depth):
                 weights[c * depth + h : c * depth + h + 1, column] = (-source_gain) * near[h] * drag
+        ones = lane_one_hot(halves, jnp.where(over >= half, over - half, over))
         for n, part in enumerate(split_parts(weights[:, column])):
             for k in range(3 * depth):
-                line = jnp.broadcast_to(part[k : k + 1], (16, LANES)).astype(BF16)
-                line = jnp.concatenate([line] * (half // 16), axis=0)
-                coupled[k * half : (k + 1) * half, n * wide + b * LANES : n * wide + (b + 1) * LANES] = ones * line
+                coupled[k * half : (k + 1) * half, n * wide + b * LANES : n * wide + (b + 1) * LANES] = place_lines(
+                    ones, part[k : k + 1], half
+                )
+    sources = [
+        lax.dot_general(
+            coupled[c * depth * half : (c + 1) * depth * half, :],
+            spots[...],
+            (((1,), (1,)), ((), ())),
+            preferred_element_type=F32,
+        )
+        for c in range(3)
+    ]
 
     copy.wait()
     for i in range(listed):
+        for c, h in share_out[blocks + i]:
+            stencil(c, h)
         a, c = pair_ref[0, i], pair_ref[1, i]
         left = blob_ref[pl.ds(pl.multiple_of(bodies + 8 * a, 8), 8), :]
-        ahead, behind = pair_sum(left, spread.at[c], LANES // SUBLANES, "all")
-        for side, (block, forces) in enumerate(((a, ahead), (c, behind))):
+        ahead, behind = pair_sum(left, spread, c * LANES, react.at[i])
+        for side, forces in enumerate((ahead, behind)):
             for d in range(3):
                 found[2 * i + side, d : d + 1, :] = forces[d]
     for b in range(blocks):
@@ -224,37 +293,16 @@
                 for side in range(2):
                     total += jnp.where(pair_ref[side, i] == b, found[2 * i + side, d : d + 1, :], 0.0)
             force_ref[d, b : b + 1, :] = total
-
-    lanes = lax.broadcasted_iota(jnp.int32, (across, along), 1)
-    downs = lax.broadcasted_iota(jnp.int32, (across, along), 0)
-    for c in range(3):
-        source = lax.dot_general(
-            coupled[c * depth * half : (c + 1) * depth * half, :],
-            spots[...],
-            (((1,), (1,)), ((), ())),
-            preferred_element_type=F32,
-        )
-        for h in range(depth):
-            here = fluid_ref[c, h]
-            beside = jnp.where(downs == 0, 0.0, pltpu.roll(here, 1, 0))
-            beside += jnp.where(downs == across - 1, 0.0, pltpu.roll(here, across - 1, 0))
-            beside += jnp.where(lanes == 0, 0.0, pltpu.roll(here, 1, 1))
-            beside += jnp.where(lanes == along - 1, 0.0, pltpu.roll(here, along - 1, 1))
-            if h > 0:
-                beside += fluid_ref[c, h - 1]
-            if h < depth - 1:
-                beside += fluid_ref[c, h + 1]
-            given = [
-                source[h * half : (h + 1) * half, f * along : (f + 1) * along] for f in range(fold)
-            ]
-            next_ref[c, h] = here + diffuse * (beside - 6.0 * here) + jnp.concatenate(given, axis=0)
+    for k, (c, h) in enumerate(slabs):
+        given = [sources[c][h * half : (h + 1) * half, f * along : (f + 1) * along] for f in range(fold)]
+        next_ref[c, h] += jnp.concatenate(given, axis=0)
 
 
 def finish_kernel(counts, blocks, pairs, force_ref, partial_ref, *refs):
     n_in = sum(counts)
     sent = refs[: counts[0]]
     height_ins, across_ins, along_ins = by_axis(refs[counts[0] : counts[0] + n_in], counts)
-    out_force, next_hbm, next_ref, spread, coupled, spots, sems = refs[counts[0] + n_in :]
+    out_force, next_hbm, next_ref, spread, pieces, picks, seen_ref, coupled, spots, sems = refs[counts[0] + n_in :]
     depth, across, along = partial_ref.shape[1:]
     fold = spots.shape[0] // along
     half = across // fold
@@ -301,37 +349,46 @@
         own = sent[n]
         above = even[0] if n == 0 else jnp.logical_not(even[0])
         own_layer = jnp.where(above, depth - 1, 0)
+        below = jnp.logical_not(above)
+        for k in range(3):
+            face = slice(k * across, (k + 1) * across)
+            pieces[face, :] = parts_of(blob[face, :])
+            pieces[(3 + k) * across : (4 + k) * across, :] = parts_of(own[face, :])
+        lined = []
         for b in range(blocks):
             cell = jnp.where(above, own[cells + b : cells + b + 1, :], blob[cells + b : cells + b + 1, :])
+            height, over, spot = places(cell.astype(jnp.int32), across, along)
+            lined.append((height, over))
+            one_hot = lane_one_hot(sites[:along], spot)
+            for m in range(PARTS):
+                picks[m * along : (m + 1) * along, b * LANES : (b + 1) * LANES] = one_hot
+            one_hot = lane_one_hot(sites, jnp.where(over >= half, along, 0) + spot)
+            for m in range(PARTS):
+                spots[:, m * wide + b * LANES : m * wide + (b + 1) * LANES] = one_hot
+        seen_ref[...] = jnp.dot(pieces[...], picks[...], preferred_element_type=F32)
+        for b in range(blocks):
+            height, over = lined[b]
             share = jnp.where(above, own[shares + b : shares + b + 1, :], blob[shares + b : shares + b + 1, :])
             body = slice(bodies + 8 * b, bodies + 8 * b + 8)
             owner = jnp.where(above, own[body, :], blob[body, :])
-            height, over, spot = places(cell.astype(jnp.int32), across, along)
             top = height == depth - 1
-            below = jnp.logical_not(above)
-            index = jnp.broadcast_to(spot, (across, LANES))
             mask = rows == over
+            column = slice(b * LANES, (b + 1) * LANES)
             seen_share = jnp.where(top, jnp.where(above, share, 1.0 - share), 0.0)
             home_share = jnp.where(jnp.logical_and(top, below), share, 0.0)
             given_share = (-source_gain) * jnp.where(above, 1.0 - share, share)
             own_share = jnp.where(jnp.logical_and(top, below), 1.0, 0.0)
-            one_hot = jnp.where(sites == jnp.where(over >= half, along, 0) + spot, 1.0, 0.0).astype(BF16)
-            for m in range(PARTS):
-                spots[:, m * wide + b * LANES : m * wide + (b + 1) * LANES] = one_hot
-            ones = jnp.where(halves == jnp.where(over >= half, over - half, over), 1.0, 0.0).astype(BF16)
+            ones = lane_one_hot(halves, jnp.where(over >= half, over - half, over))
             for c in range(3):
-                face = slice(c * across, (c + 1) * across)
-                seen = jnp.take_along_axis(blob[face, :], index, axis=1)
-                home = jnp.take_along_axis(own[face, :], index, axis=1)
+                seen = seen_ref[c * across : (c + 1) * across, column]
+                home = seen_ref[(3 + c) * across : (4 + c) * across, column]
                 met = jnp.where(mask, seen_share * seen + home_share * home, 0.0)
                 met = jnp.sum(met, axis=0, keepdims=True)
                 drag = drag_coef * owner[6:7] * (met - own_share * owner[3 + c : 4 + c])
                 coupling[c][b] += jnp.where(above, drag, 0.0)
                 for m, part in enumerate(split_parts(given_share * drag)):
-                    line = jnp.broadcast_to(part, (16, LANES)).astype(BF16)
-                    line = jnp.concatenate([line] * (half // 16), axis=0)
                     coupled[c * half : (c + 1) * half, m * wide + b * LANES : m * wide + (b + 1) * LANES] = (
-                        ones * line
+                        place_lines(ones, part, half)
                     )
         source = lax.dot_general(
             coupled[...], spots[...], (((1,), (1,)), ((), ())), preferred_element_type=F32
@@ -343,6 +400,7 @@
         copies.append(pltpu.make_async_copy(next_ref.at[:, h], next_hbm.at[:, h], sems.at[3 + n]))
         copies[-1].start()
 
+    meetings, partners = [], []
     for n, blob in enumerate(height_ins):
         own = sent[n]
         above = even[0] if n == 0 else jnp.logical_not(even[0])
@@ -357,11 +415,14 @@
                 body = slice(bodies + 8 * b, bodies + 8 * b + 8)
                 left = jnp.where(to == b, own[body, :], left)
                 right = jnp.where(by == b, blob[body, :], right)
-            spread_block(right, spread.at[n * pairs + k])
-            force, _ = pair_sum(left, spread.at[n * pairs + k], LANES // SUBLANES, None)
-            for b in range(blocks):
-                for c in range(3):
-                    coupling[c][b] += jnp.where(to == b, force[c], 0.0)
+            meetings.append((to, left))
+            partners.append(right)
+    spread[...] = spread_blocks(partners)
+    for i, (to, left) in enumerate(meetings):
+        force, _ = pair_sum(left, spread, i * LANES, None)
+        for b in range(blocks):
+            for c in range(3):
+                coupling[c][b] += jnp.where(to == b, force[c], 0.0)
     for b in range(blocks):
         for c in range(3):
             out_force[c, b : b + 1, :] = force_ref[c, b : b + 1, :] + coupling[c][b]
@@ -400,7 +461,6 @@
     rows = blob_layout(across, blocks, pairs)[-1]
     shapes = [(rows, along), (3 * depth, along), (across, along)]
     vmem = pl.BlockSpec(memory_space=pltpu.VMEM)
-    smem = pl.BlockSpec(memory_space=pltpu.SMEM)
     hbm = pl.BlockSpec(memory_space=pl.ANY)
 
     def kept(value):
@@ -410,9 +470,15 @@
         functools.partial(pack_kernel, counts),
         out_shape=[pltpu.VMEM(fluid.shape, F32)]
         + [pltpu.VMEM(shape, F32) for shape, n in zip(shapes, counts) for _ in range(n)],
-        in_specs=[smem, vmem, vmem, vmem, hbm],
+        in_specs=[hbm] * 5,
         out_specs=[vmem] * (1 + sum(counts)),
-        scratch_shapes=[pltpu.SemaphoreType.DMA((3,))],
+        scratch_shapes=[
+            pltpu.SMEM(cross_pairs.shape, jnp.int32),
+            pltpu.VMEM(particles.shape, F32),
+            pltpu.VMEM(drag_cell.shape, jnp.int32),
+            pltpu.VMEM(drag_share.shape, F32),
+            pltpu.SemaphoreType.DMA((7,)),
+        ],
         name="pack",
     )(cross_pairs, particles, drag_cell, drag_share, fluid)
     received = []
@@ -425,7 +491,11 @@
         in_specs=[hbm, vmem, vmem],
         out_specs=[vmem, vmem],
         scratch_shapes=[
-            pltpu.VMEM((blocks, 9, LANES, LANES), F32),
+            pltpu.VMEM((blocks * LANES, 9 * LANES), F32),
+            pltpu.VMEM((listed, LANES, LANES), F32),
+            pltpu.VMEM((3 * depth * across, PARTS * along), BF16),
+            pltpu.VMEM((3 * depth * across, blocks * LANES), F32),
+            pltpu.VMEM((PARTS * along, blocks * LANES), BF16),
             pltpu.VMEM((2 * listed, SUBLANES, LANES), F32),
             pltpu.VMEM((3 * depth, blocks * LANES), F32),
             pltpu.VMEM((3 * depth * half, wide), BF16),
@@ -446,7 +516,10 @@
         out_specs=[vmem, hbm],
         scratch_shapes=[
             pltpu.VMEM(fluid.shape, F32),
-            pltpu.VMEM((counts[0] * pairs, 9, LANES, LANES), F32),
+            pltpu.VMEM((counts[0] * pairs * LANES, 9 * LANES), F32),
+            pltpu.VMEM((6 * across, PARTS * along), BF16),
+            pltpu.VMEM((PARTS * along, blocks * LANES), BF16),
+            pltpu.VMEM((6 * across, blocks * LANES), F32),
             pltpu.VMEM((3 * half, wide), BF16),
             pltpu.VMEM((fold * along, wide), BF16),
             pltpu.SemaphoreType.DMA((5,)),

time: 28.8 us -> 18.8 us (0.65)
  Pallas kernels: 17.8 us -> 7.79 us
    pallas_call x1, Pallas kernels: 11.3 us -> 3.74 us  [body(): pl.pallas_call(functools.partial(local_kernel, blocks, pairs), out_shape=...]
    pallas_call x1, Pallas kernels: 4.22 us -> 2.39 us  [body(): pl.pallas_call(functools.partial(finish_kernel, counts, blocks, pairs), o...]
    pallas_call x1, Pallas kernels: 2.28 us -> 1.66 us  [body(): pl.pallas_call(functools.partial(pack_kernel, counts), out_shape=[pltpu.V...]
  transfers between devices with their start and end apart: 5 -> 5, of which waited for: 0 -> 0; matrix products, arithmetic and copies ran while one was open for 0% -> 0% of each run, Pallas kernels for 39% -> 20%
where the time goes in v3:
time: 18.8 us; the launch traced here: 18.6 us
  starting transfers between devices  10.1 us (54%)
  Pallas kernels  7.79 us (41%)
  between operations  0.71 us (4%)
    ppermute x5, starting transfers between devices, exchange(): results.append(lax.ppermute(payload, axis, route))  10.1 us
    pallas_call x1, Pallas kernels, body(): pl.pallas_call(functools.partial(local_kernel, blocks, pairs), out_shape=...  3.74 us
    pallas_call x1, Pallas kernels, body(): pl.pallas_call(functools.partial(finish_kernel, counts, blocks, pairs), o...  2.39 us
    pallas_call x1, Pallas kernels, body(): pl.pallas_call(functools.partial(pack_kernel, counts), out_shape=[pltpu.V...  1.66 us
  transfers between devices with their start and end apart: 5, of which 0 were waited for; matrix products, arithmetic and copies ran while one was open for 0% of the time, Pallas kernels for 20%

profile of v3, /device:TPU:10, one launch (start us, length us, event | category | flops | bytes accessed | tf_op | source)
XLA Modules:
  0.0 18.6 jit_solution(15269610858889447054)
XLA Ops:
  0.6 1.7 %pack.1 = (f32[3,8,64,128]{3,2,1,0:T(8,128)S(1)}, f32[240,128]{1,0:T(8,128)S(1)}, f32[24,128]{1,0:T(8,128)S(1)}, f32[24,128]{1,0:T(8,128)S(1)}, f32[64,128]{1,0:T(8,128)S(1)}, /*index=5*/f32[64,128]{1,0:T(8,128)S(1)}) custom-call(s32[2,2]{1,0:T(2,128)} %pair_hbm.1, f32[4,8,128]{2,1,0:T(8,128)} %part_hbm.1, s32[4,128]{1,0:T(4,128)} %cell_hbm.1, ...), custom_call_target="tpu_custom_call" | custom-call | tf_op jit(solution)/shard_map/pack/pallas_call | solution.py:469
  2.3 0.1 collective-permute-start
  2.4 0.5 %collective-permute-start.3 = (f32[64,128]{1,0:T(8,128)S(1)}, f32[64,128]{1,0:T(8,128)S(1)}, u32[]{:S(2)}, u32[]{:S(2)}) collective-permute-start(f32[64,128]{1,0:T(8,128)S(1)} %get-tuple-element.18), channel_id=1, source_target_pairs={{0,1},{1,0},{2,3},{3,2},{4,5},{5,4},{6,7},{7,6},{8,9},{9,8},{10,11... | collective-permute-start | bytes 98312 | tf_op jit(solution)/shard_map/ppermute | solution.py:448
  2.9 4.6 %collective-permute-start.4 = (f32[64,128]{1,0:T(8,128)S(1)}, f32[64,128]{1,0:T(8,128)S(1)}, u32[]{:S(2)}, u32[]{:S(2)}) collective-permute-start(f32[64,128]{1,0:T(8,128)S(1)} %get-tuple-element.19), channel_id=1, source_target_pairs={{1,2},{2,1},{5,6},{6,5},{9,10},{10,9},{13,14},{14,13},{17,18},{18,... | collective-permute-start | bytes 98312 | tf_op jit(solution)/shard_map/ppermute | solution.py:448
  7.5 0.6 %collective-permute-start.1 = (f32[24,128]{1,0:T(8,128)S(1)}, f32[24,128]{1,0:T(8,128)S(1)}, u32[]{:S(2)}, u32[]{:S(2)}) collective-permute-start(f32[24,128]{1,0:T(8,128)S(1)} %get-tuple-element.16), channel_id=1, source_target_pairs={{0,4},{4,0},{8,12},{12,8},{1,5},{5,1},{9,13},{13,9},{2,6},{6,2},{1... | collective-permute-start | bytes 36872 | tf_op jit(solution)/shard_map/ppermute | solution.py:448
  8.1 4.3 %collective-permute-start.2 = (f32[24,128]{1,0:T(8,128)S(1)}, f32[24,128]{1,0:T(8,128)S(1)}, u32[]{:S(2)}, u32[]{:S(2)}) collective-permute-start(f32[24,128]{1,0:T(8,128)S(1)} %get-tuple-element.17), channel_id=1, source_target_pairs={{4,8},{8,4},{5,9},{9,5},{6,10},{10,6},{7,11},{11,7},{20,24},{24,20... | collective-permute-start | bytes 36872 | tf_op jit(solution)/shard_map/ppermute | solution.py:448
  12.5 3.7 %local.1 = (f32[3,4,128]{2,1,0:T(4,128)S(1)}, f32[3,8,64,128]{3,2,1,0:T(8,128)S(1)}) custom-call(s32[2,4]{1,0:T(2,128)} %bitcast.2, f32[240,128]{1,0:T(8,128)S(1)} %get-tuple-element.12.blob_ref.refs_0_, f32[3,8,64,128]{3,2,1,0:T(8,128)S(1)} %get-tuple-element.13.fluid_ref), custom_call_target="tpu_custom_call" | custom-call | tf_op jit(solution)/shard_map/local/pallas_call | solution.py:488
  16.2 0.0 collective-permute-done.1.refs_2_
  16.2 0.0 collective-permute-done.2.refs_3_
  16.2 0.0 collective-permute-done.3.refs_4_
  16.2 0.0 collective-permute-done.4.refs_5_
  16.2 0.0 collective-permute-done.refs_1_
  16.3 2.4 %finish.1 = (f32[3,4,128]{2,1,0:T(4,128)}, f32[3,8,64,128]{3,2,1,0:T(8,128)}) custom-call(f32[3,4,128]{2,1,0:T(4,128)S(1)} %get-tuple-element.14.force_ref, f32[3,8,64,128]{3,2,1,0:T(8,128)S(1)} %get-tuple-element.15.partial_ref, f32[240,128]{1,0:T(8,128)S(1)} %get-tuple-element.12.blob_ref.refs_0_, f32[240,128]{1,0:T(8,128)S(1)} %collective-permute-done.refs_1_, ...), custom_call_target="tpu_custom_call" | custom-call | tf_op jit(solution)/shard_map/finish/pallas_call | solution.py:509
Async XLA Ops:
  2.3 13.9 %collective-permute-start = (f32[240,128]{1,0:T(8,128)S(1)}, f32[240,128]{1,0:T(8,128)S(1)}, u32[]{:S(2)}, u32[]{:S(2)}) collective-permute-start(f32[240,128]{1,0:T(8,128)S(1)} %get-tuple-element.12.blob_ref.refs_0_), channel_id=1, source_target_pairs={{0,16},{16,0},{1,17},{17,1},{2,18},{18,2},{3,19},{19,3},{4,20},{20... | collective-permute-start | bytes 368648 | tf_op jit(solution)/shard_map/ppermute | solution.py:448
  2.4 13.8 %collective-permute-start.3 = (f32[64,128]{1,0:T(8,128)S(1)}, f32[64,128]{1,0:T(8,128)S(1)}, u32[]{:S(2)}, u32[]{:S(2)}) collective-permute-start(f32[64,128]{1,0:T(8,128)S(1)} %get-tuple-element.18), channel_id=1, source_target_pairs={{0,1},{1,0},{2,3},{3,2},{4,5},{5,4},{6,7},{7,6},{8,9},{9,8},{10,11... | collective-permute-start | bytes 98312 | tf_op jit(solution)/shard_map/ppermute | solution.py:448
  2.9 13.3 %collective-permute-start.4 = (f32[64,128]{1,0:T(8,128)S(1)}, f32[64,128]{1,0:T(8,128)S(1)}, u32[]{:S(2)}, u32[]{:S(2)}) collective-permute-start(f32[64,128]{1,0:T(8,128)S(1)} %get-tuple-element.19), channel_id=1, source_target_pairs={{1,2},{2,1},{5,6},{6,5},{9,10},{10,9},{13,14},{14,13},{17,18},{18,... | collective-permute-start | bytes 98312 | tf_op jit(solution)/shard_map/ppermute | solution.py:448
  7.5 8.7 %collective-permute-start.1 = (f32[24,128]{1,0:T(8,128)S(1)}, f32[24,128]{1,0:T(8,128)S(1)}, u32[]{:S(2)}, u32[]{:S(2)}) collective-permute-start(f32[24,128]{1,0:T(8,128)S(1)} %get-tuple-element.16), channel_id=1, source_target_pairs={{0,4},{4,0},{8,12},{12,8},{1,5},{5,1},{9,13},{13,9},{2,6},{6,2},{1... | collective-permute-start | bytes 36872 | tf_op jit(solution)/shard_map/ppermute | solution.py:448
  8.1 8.1 %collective-permute-start.2 = (f32[24,128]{1,0:T(8,128)S(1)}, f32[24,128]{1,0:T(8,128)S(1)}, u32[]{:S(2)}, u32[]{:S(2)}) collective-permute-start(f32[24,128]{1,0:T(8,128)S(1)} %get-tuple-element.17), channel_id=1, source_target_pairs={{4,8},{8,4},{5,9},{9,5},{6,10},{10,6},{7,11},{11,7},{20,24},{24,20... | collective-permute-start | bytes 36872 | tf_op jit(solution)/shard_map/ppermute | solution.py:448

commit v4 on v3

--- a/solution.py
+++ b/solution.py
@@ -16,15 +16,16 @@
 
 F32 = jnp.float32
 BF16 = jnp.bfloat16
-PARTS = 3
+PARTS = 2
+EXACT = 3
 LANES = 128
 SUBLANES = 8
 AXES = ("gx", "gy", "gz")
 
 
-def split_parts(value):
+def split_parts(value, count=PARTS):
     parts = []
-    for _ in range(PARTS):
+    for _ in range(count):
         part = value.astype(BF16).astype(F32)
         parts.append(part)
         value = value - part
@@ -52,14 +53,14 @@
     columns = []
     for block in blocks:
         rows = jnp.concatenate([block, block[7:8] * jnp.sqrt(block[6:7])], axis=0)
-        parts = split_parts(rows)
-        parts.append(jnp.zeros((32 - 9 * PARTS, LANES), F32))
+        parts = split_parts(rows, EXACT)
+        parts.append(jnp.zeros((32 - 9 * EXACT, LANES), F32))
         columns.append(jnp.transpose(jnp.concatenate(parts, axis=0)).astype(BF16))
     lines = lax.broadcasted_iota(jnp.int32, (32, LANES), 0)
     picks = []
     for i in range(9):
         pick = lines == i
-        for n in range(1, PARTS):
+        for n in range(1, EXACT):
             pick = jnp.logical_or(pick, lines == i + 9 * n)
         picks.append(jnp.where(pick, 1.0, 0.0).astype(BF16))
     return jnp.dot(
@@ -118,8 +119,8 @@
 
 
 def pack_kernel(counts, pair_hbm, part_hbm, cell_hbm, share_hbm, fluid_hbm, *refs):
-    n_out = 1 + sum(counts)
-    fluid_ref, outs = refs[0], refs[1:n_out]
+    n_out = 2 + sum(counts)
+    fluid_ref, wrap_ref, outs = refs[0], refs[1], refs[2:n_out]
     pair_ref, part_ref, cell_ref, share_ref, sems = refs[n_out:]
     height_outs, across_outs, along_outs = by_axis(outs, counts)
     depth, across, along = fluid_ref.shape[1:]
@@ -165,6 +166,7 @@
             last = jnp.where(lanes == (2 * k - 1) % along, turned, last)
     first = pltpu.roll(first, along - 1, 1)
     last = pltpu.roll(last, 1, 1)
+    wrap_ref[...] = first + last
     for n, out in enumerate(along_outs):
         upward = even[2] if n == 0 else jnp.logical_not(even[2])
         out[...] = jnp.where(upward, last, first)
@@ -176,7 +178,8 @@
 
 def place_lines(ones, part, half):
     line = jnp.broadcast_to(part, (16, LANES)).astype(BF16)
-    return ones * jnp.concatenate([line] * (half // 16), axis=0)
+    line = jnp.concatenate([line] * (half // 16), axis=0)
+    return jnp.where(ones > 0, line, jnp.zeros_like(line))
 
 
 def local_kernel(
@@ -194,8 +197,7 @@
     rows = lax.broadcasted_iota(jnp.int32, (across, LANES), 0)
     halves = lax.broadcasted_iota(jnp.int32, (half, LANES), 0)
     sites = lax.broadcasted_iota(jnp.int32, (fold * along, LANES), 0)
-    lanes = lax.broadcasted_iota(jnp.int32, (across, along), 1)
-    downs = lax.broadcasted_iota(jnp.int32, (across, along), 0)
+    subs = lax.broadcasted_iota(jnp.int32, (SUBLANES, along), 0)
     slabs = [(c, h) for c in range(3) for h in range(depth)]
 
     def body_of(b):
@@ -205,16 +207,23 @@
         return places(blob_ref[cells + b : cells + b + 1, :].astype(jnp.int32), across, along)
 
     def stencil(c, h):
-        here = fluid_ref[c, h]
-        beside = jnp.where(downs == 0, 0.0, pltpu.roll(here, 1, 0))
-        beside += jnp.where(downs == across - 1, 0.0, pltpu.roll(here, across - 1, 0))
-        beside += jnp.where(lanes == 0, 0.0, pltpu.roll(here, 1, 1))
-        beside += jnp.where(lanes == along - 1, 0.0, pltpu.roll(here, along - 1, 1))
-        if h > 0:
-            beside += fluid_ref[c, h - 1]
-        if h < depth - 1:
-            beside += fluid_ref[c, h + 1]
-        next_ref[c, h] = here + diffuse * (beside - 6.0 * here)
+        for t in range(across // SUBLANES):
+            at = t * SUBLANES
+            here = fluid_ref[c, h, at : at + SUBLANES, :]
+            if t > 0:
+                beside = fluid_ref[c, h, at - 1 : at + SUBLANES - 1, :]
+            else:
+                beside = jnp.where(subs == 0, 0.0, pltpu.roll(here, 1, 0))
+            if at + SUBLANES < across:
+                beside += fluid_ref[c, h, at + 1 : at + SUBLANES + 1, :]
+            else:
+                beside += jnp.where(subs == SUBLANES - 1, 0.0, pltpu.roll(here, SUBLANES - 1, 0))
+            beside += pltpu.roll(here, 1, 1) + pltpu.roll(here, along - 1, 1)
+            if h > 0:
+                beside += fluid_ref[c, h - 1, at : at + SUBLANES, :]
+            if h < depth - 1:
+                beside += fluid_ref[c, h + 1, at : at + SUBLANES, :]
+            next_ref[c, h, at : at + SUBLANES, :] = (1.0 - 6.0 * diffuse) * here + diffuse * beside
 
     spread[...] = spread_blocks([body_of(b) for b in range(blocks)])
     for k, (c, h) in enumerate(slabs):
@@ -298,7 +307,7 @@
         next_ref[c, h] += jnp.concatenate(given, axis=0)
 
 
-def finish_kernel(counts, blocks, pairs, force_ref, partial_ref, *refs):
+def finish_kernel(counts, blocks, pairs, force_ref, partial_ref, wrap_ref, *refs):
     n_in = sum(counts)
     sent = refs[: counts[0]]
     height_ins, across_ins, along_ins = by_axis(refs[counts[0] : counts[0] + n_in], counts)
@@ -323,9 +332,10 @@
     edges = along_ins[0][...]
     if len(along_ins) > 1:
         edges = edges + along_ins[1][...]
-    edges = diffuse * edges
+    edges = diffuse * (edges - wrap_ref[...])
     lanes = lax.broadcasted_iota(jnp.int32, (across, along), 1)
-    downs = lax.broadcasted_iota(jnp.int32, (across, along), 0)
+    subs = lax.broadcasted_iota(jnp.int32, (SUBLANES, along), 0)
+    tail = across - SUBLANES
     rim = jnp.logical_or(lanes == 0, lanes == along - 1)
     copies = []
     for c in range(3):
@@ -333,9 +343,9 @@
             k = c * depth + h
             value = partial_ref[c, h]
             value += jnp.where(rim, pltpu.roll(edges, (along - 2 * k) % along, 1) if k else edges, 0.0)
-            value += jnp.where(downs == 0, across_low[k : k + 1, :], 0.0)
-            value += jnp.where(downs == across - 1, across_high[k : k + 1, :], 0.0)
             next_ref[c, h] = value
+            next_ref[c, h, :SUBLANES, :] += jnp.where(subs == 0, across_low[k : k + 1, :], 0.0)
+            next_ref[c, h, tail:, :] += jnp.where(subs == SUBLANES - 1, across_high[k : k + 1, :], 0.0)
         if depth > 2:
             inner = pl.ds(1, depth - 2)
             copies.append(pltpu.make_async_copy(next_ref.at[c, inner], next_hbm.at[c, inner], sems.at[c]))
@@ -466,12 +476,12 @@
     def kept(value):
         return pltpu.with_memory_space_constraint(value, pltpu.VMEM)
 
-    fluid_kept, *packed = pl.pallas_call(
+    fluid_kept, wrapped, *packed = pl.pallas_call(
         functools.partial(pack_kernel, counts),
-        out_shape=[pltpu.VMEM(fluid.shape, F32)]
+        out_shape=[pltpu.VMEM(fluid.shape, F32), pltpu.VMEM((across, along), F32)]
         + [pltpu.VMEM(shape, F32) for shape, n in zip(shapes, counts) for _ in range(n)],
         in_specs=[hbm] * 5,
-        out_specs=[vmem] * (1 + sum(counts)),
+        out_specs=[vmem] * (2 + sum(counts)),
         scratch_shapes=[
             pltpu.SMEM(cross_pairs.shape, jnp.int32),
             pltpu.VMEM(particles.shape, F32),
@@ -512,7 +522,7 @@
             jax.ShapeDtypeStruct((3, blocks, LANES), F32),
             jax.ShapeDtypeStruct(fluid.shape, F32),
         ],
-        in_specs=[vmem] * (2 + counts[0] + len(received)),
+        in_specs=[vmem] * (3 + counts[0] + len(received)),
         out_specs=[vmem, hbm],
         scratch_shapes=[
             pltpu.VMEM(fluid.shape, F32),
@@ -525,7 +535,7 @@
             pltpu.SemaphoreType.DMA((5,)),
         ],
         name="finish",
-    )(*[kept(value) for value in [force, partial, *packed[: counts[0]], *received]])
+    )(*[kept(value) for value in [force, partial, wrapped, *packed[: counts[0]], *received]])
     return jnp.transpose(out_force, (1, 0, 2)), out_next
 
 

time: 18.8 us -> 17.9 us (0.952)
  Pallas kernels: 7.79 us -> 6.8 us
    pallas_call x1, Pallas kernels: 3.74 us -> 2.94 us  [body(): pl.pallas_call(functools.partial(local_kernel, blocks, pairs), out_shape=...]
  transfers between devices with their start and end apart: 5 -> 5, of which waited for: 0 -> 0; matrix products, arithmetic and copies ran while one was open for 0% -> 0% of each run, Pallas kernels for 20% -> 17%
where the time goes in v4:
time: 17.9 us; the launch traced here: 17.7 us
  starting transfers between devices  10.1 us (56%)
  Pallas kernels  6.8 us (38%)
  between operations  0.71 us (4%)
    ppermute x5, starting transfers between devices, exchange(): results.append(lax.ppermute(payload, axis, route))  10.1 us
    pallas_call x1, Pallas kernels, body(): pl.pallas_call(functools.partial(local_kernel, blocks, pairs), out_shape=...  2.94 us
    pallas_call x1, Pallas kernels, body(): pl.pallas_call(functools.partial(finish_kernel, counts, blocks, pairs), o...  2.2 us
    pallas_call x1, Pallas kernels, body(): pl.pallas_call(functools.partial(pack_kernel, counts), out_shape=[pltpu.V...  1.67 us
  transfers between devices with their start and end apart: 5, of which 0 were waited for; matrix products, arithmetic and copies ran while one was open for 0% of the time, Pallas kernels for 17%

profile of v4, /device:TPU:10, one launch (start us, length us, event | category | flops | bytes accessed | tf_op | source)
XLA Modules:
  0.0 17.7 jit_solution(9455322600896467567)
XLA Ops:
  0.6 1.7 %pack.1 = (f32[3,8,64,128]{3,2,1,0:T(8,128)S(1)}, f32[64,128]{1,0:T(8,128)S(1)}, f32[240,128]{1,0:T(8,128)S(1)}, f32[24,128]{1,0:T(8,128)S(1)}, f32[24,128]{1,0:...) custom-call(s32[2,2]{1,0:T(2,128)} %pair_hbm.1, f32[4,8,128]{2,1,0:T(8,128)} %part_hbm.1, s32[4,128]{1,0:T(4,128)} %cell_hbm.1, ...), custom_call_target="tpu_custom_call" | custom-call | tf_op jit(solution)/shard_map/pack/pallas_call | solution.py:479
  2.3 0.1 collective-permute-start
  2.4 0.5 %collective-permute-start.3 = (f32[64,128]{1,0:T(8,128)S(1)}, f32[64,128]{1,0:T(8,128)S(1)}, u32[]{:S(2)}, u32[]{:S(2)}) collective-permute-start(f32[64,128]{1,0:T(8,128)S(1)} %get-tuple-element.20), channel_id=1, source_target_pairs={{0,1},{1,0},{2,3},{3,2},{4,5},{5,4},{6,7},{7,6},{8,9},{9,8},{10,11... | collective-permute-start | bytes 98312 | tf_op jit(solution)/shard_map/ppermute | solution.py:458
  2.9 4.6 %collective-permute-start.4 = (f32[64,128]{1,0:T(8,128)S(1)}, f32[64,128]{1,0:T(8,128)S(1)}, u32[]{:S(2)}, u32[]{:S(2)}) collective-permute-start(f32[64,128]{1,0:T(8,128)S(1)} %get-tuple-element.21), channel_id=1, source_target_pairs={{1,2},{2,1},{5,6},{6,5},{9,10},{10,9},{13,14},{14,13},{17,18},{18,... | collective-permute-start | bytes 98312 | tf_op jit(solution)/shard_map/ppermute | solution.py:458
  7.5 0.6 %collective-permute-start.1 = (f32[24,128]{1,0:T(8,128)S(1)}, f32[24,128]{1,0:T(8,128)S(1)}, u32[]{:S(2)}, u32[]{:S(2)}) collective-permute-start(f32[24,128]{1,0:T(8,128)S(1)} %get-tuple-element.18), channel_id=1, source_target_pairs={{0,4},{4,0},{8,12},{12,8},{1,5},{5,1},{9,13},{13,9},{2,6},{6,2},{1... | collective-permute-start | bytes 36872 | tf_op jit(solution)/shard_map/ppermute | solution.py:458
  8.1 4.3 %collective-permute-start.2 = (f32[24,128]{1,0:T(8,128)S(1)}, f32[24,128]{1,0:T(8,128)S(1)}, u32[]{:S(2)}, u32[]{:S(2)}) collective-permute-start(f32[24,128]{1,0:T(8,128)S(1)} %get-tuple-element.19), channel_id=1, source_target_pairs={{4,8},{8,4},{5,9},{9,5},{6,10},{10,6},{7,11},{11,7},{20,24},{24,20... | collective-permute-start | bytes 36872 | tf_op jit(solution)/shard_map/ppermute | solution.py:458
  12.5 2.9 %local.1 = (f32[3,4,128]{2,1,0:T(4,128)S(1)}, f32[3,8,64,128]{3,2,1,0:T(8,128)S(1)}) custom-call(s32[2,4]{1,0:T(2,128)} %bitcast.2, f32[240,128]{1,0:T(8,128)S(1)} %get-tuple-element.13.blob_ref.refs_0_, f32[3,8,64,128]{3,2,1,0:T(8,128)S(1)} %get-tuple-element.14.fluid_ref), custom_call_target="tpu_custom_call" | custom-call | tf_op jit(solution)/shard_map/local/pallas_call | solution.py:498
  15.4 0.0 collective-permute-done.1.refs_2_
  15.4 0.0 collective-permute-done.2.refs_3_
  15.4 0.0 collective-permute-done.3.refs_4_
  15.4 0.0 collective-permute-done.4.refs_5_
  15.4 0.0 collective-permute-done.refs_1_
  15.5 2.2 %finish.1 = (f32[3,4,128]{2,1,0:T(4,128)}, f32[3,8,64,128]{3,2,1,0:T(8,128)}) custom-call(f32[3,4,128]{2,1,0:T(4,128)S(1)} %get-tuple-element.15.force_ref, f32[3,8,64,128]{3,2,1,0:T(8,128)S(1)} %get-tuple-element.16.partial_ref, f32[64,128]{1,0:T(8,128)S(1)} %get-tuple-element.17.wrap_ref, f32[240,128]{1,0:T(8,128)S(1)} %get-tuple-element.13.blob_ref.refs_0_, ...), custom_call_target="tpu_custom_call" | custom-call | tf_op jit(solution)/shard_map/finish/pallas_call | solution.py:519
Async XLA Ops:
  2.3 13.1 %collective-permute-start = (f32[240,128]{1,0:T(8,128)S(1)}, f32[240,128]{1,0:T(8,128)S(1)}, u32[]{:S(2)}, u32[]{:S(2)}) collective-permute-start(f32[240,128]{1,0:T(8,128)S(1)} %get-tuple-element.13.blob_ref.refs_0_), channel_id=1, source_target_pairs={{0,16},{16,0},{1,17},{17,1},{2,18},{18,2},{3,19},{19,3},{4,20},{20... | collective-permute-start | bytes 368648 | tf_op jit(solution)/shard_map/ppermute | solution.py:458
  2.4 13.0 %collective-permute-start.3 = (f32[64,128]{1,0:T(8,128)S(1)}, f32[64,128]{1,0:T(8,128)S(1)}, u32[]{:S(2)}, u32[]{:S(2)}) collective-permute-start(f32[64,128]{1,0:T(8,128)S(1)} %get-tuple-element.20), channel_id=1, source_target_pairs={{0,1},{1,0},{2,3},{3,2},{4,5},{5,4},{6,7},{7,6},{8,9},{9,8},{10,11... | collective-permute-start | bytes 98312 | tf_op jit(solution)/shard_map/ppermute | solution.py:458
  2.9 12.5 %collective-permute-start.4 = (f32[64,128]{1,0:T(8,128)S(1)}, f32[64,128]{1,0:T(8,128)S(1)}, u32[]{:S(2)}, u32[]{:S(2)}) collective-permute-start(f32[64,128]{1,0:T(8,128)S(1)} %get-tuple-element.21), channel_id=1, source_target_pairs={{1,2},{2,1},{5,6},{6,5},{9,10},{10,9},{13,14},{14,13},{17,18},{18,... | collective-permute-start | bytes 98312 | tf_op jit(solution)/shard_map/ppermute | solution.py:458
  7.5 7.9 %collective-permute-start.1 = (f32[24,128]{1,0:T(8,128)S(1)}, f32[24,128]{1,0:T(8,128)S(1)}, u32[]{:S(2)}, u32[]{:S(2)}) collective-permute-start(f32[24,128]{1,0:T(8,128)S(1)} %get-tuple-element.18), channel_id=1, source_target_pairs={{0,4},{4,0},{8,12},{12,8},{1,5},{5,1},{9,13},{13,9},{2,6},{6,2},{1... | collective-permute-start | bytes 36872 | tf_op jit(solution)/shard_map/ppermute | solution.py:458
  8.1 7.3 %collective-permute-start.2 = (f32[24,128]{1,0:T(8,128)S(1)}, f32[24,128]{1,0:T(8,128)S(1)}, u32[]{:S(2)}, u32[]{:S(2)}) collective-permute-start(f32[24,128]{1,0:T(8,128)S(1)} %get-tuple-element.19), channel_id=1, source_target_pairs={{4,8},{8,4},{5,9},{9,5},{6,10},{10,6},{7,11},{11,7},{20,24},{24,20... | collective-permute-start | bytes 36872 | tf_op jit(solution)/shard_map/ppermute | solution.py:458

commit v5 on v4

--- a/solution.py
+++ b/solution.py
@@ -20,6 +20,7 @@
 EXACT = 3
 LANES = 128
 SUBLANES = 8
+GRANT = 32 * 1024 * 1024
 AXES = ("gx", "gy", "gz")
 
 
@@ -119,17 +120,20 @@
 
 
 def pack_kernel(counts, pair_hbm, part_hbm, cell_hbm, share_hbm, fluid_hbm, *refs):
-    n_out = 2 + sum(counts)
-    fluid_ref, wrap_ref, outs = refs[0], refs[1], refs[2:n_out]
+    n_out = 5 + sum(counts)
+    fluid_ref, pieces, picks, spots, spread = refs[:5]
+    height_outs, across_outs, along_outs = by_axis(refs[5:n_out], counts)
     pair_ref, part_ref, cell_ref, share_ref, sems = refs[n_out:]
-    height_outs, across_outs, along_outs = by_axis(outs, counts)
     depth, across, along = fluid_ref.shape[1:]
     blocks, pairs = part_ref.shape[0], pair_ref.shape[0]
+    fold = spots.shape[0] // along
+    half = across // fold
+    wide = blocks * LANES
     bodies, cells, shares, lists, rows = blob_layout(across, blocks, pairs)
+    small = [(part_hbm, part_ref), (cell_hbm, cell_ref), (share_hbm, share_ref), (pair_hbm, pair_ref)]
+    small = [pltpu.make_async_copy(source, target, sems.at[3 + n]) for n, (source, target) in enumerate(small)]
     copies = [pltpu.make_async_copy(fluid_hbm.at[c], fluid_ref.at[c], sems.at[c]) for c in range(3)]
-    small = [(pair_hbm, pair_ref), (part_hbm, part_ref), (cell_hbm, cell_ref), (share_hbm, share_ref)]
-    small = [pltpu.make_async_copy(source, target, sems.at[3 + n]) for n, (source, target) in enumerate(small)]
-    for copy in copies + small:
+    for copy in small + copies:
         copy.start()
     even = parities()
     for copy in small:
@@ -146,6 +150,15 @@
         used = lists + 2 * pairs
         if used < rows:
             out[used:rows, :] = jnp.zeros((rows - used, LANES), F32)
+    spread[...] = spread_blocks([part_ref[b] for b in range(blocks)])
+    for b in range(blocks):
+        _, over, spot = places(cell_ref[b : b + 1, :], across, along)
+        mark_cells(picks, spots, b, over, spot, half, wide)
+    sites = lax.broadcasted_iota(jnp.int32, (along, along), 0)
+    lanes = lax.broadcasted_iota(jnp.int32, (along, along), 1)
+    near = jnp.where(jnp.abs(sites - lanes) == 1, 1.0, 0.0).astype(BF16)
+    for n in range(PARTS):
+        picks[n * along : (n + 1) * along, wide : wide + along] = near
 
     lanes = lax.broadcasted_iota(jnp.int32, (across, along), 1)
     first = jnp.zeros((across, along), F32)
@@ -164,12 +177,23 @@
             turned = pltpu.roll(here, 2 * k, 1) if k else here
             first = jnp.where(lanes == 2 * k, turned, first)
             last = jnp.where(lanes == (2 * k - 1) % along, turned, last)
+            pieces[k * across : (k + 1) * across, :] = parts_of(here)
     first = pltpu.roll(first, along - 1, 1)
     last = pltpu.roll(last, 1, 1)
-    wrap_ref[...] = first + last
     for n, out in enumerate(along_outs):
         upward = even[2] if n == 0 else jnp.logical_not(even[2])
         out[...] = jnp.where(upward, last, first)
+
+
+def mark_cells(picks, spots, b, over, spot, half, wide):
+    along = picks.shape[0] // PARTS
+    sites = lax.broadcasted_iota(jnp.int32, (spots.shape[0], LANES), 0)
+    one_hot = lane_one_hot(sites[:along], spot)
+    for n in range(PARTS):
+        picks[n * along : (n + 1) * along, b * LANES : (b + 1) * LANES] = one_hot
+    one_hot = lane_one_hot(sites, jnp.where(over >= half, along, 0) + spot)
+    for n in range(PARTS):
+        spots[:, n * wide + b * LANES : n * wide + (b + 1) * LANES] = one_hot
 
 
 def lane_one_hot(sites, target):
@@ -183,8 +207,8 @@
 
 
 def local_kernel(
-    blocks, pairs, pair_hbm, blob_ref, fluid_ref, force_ref, next_ref,
-    spread, react, pieces, seen_ref, picks, found, weights, coupled, spots, pair_ref, sem,
+    blocks, pairs, pair_hbm, blob_ref, fluid_ref, pieces, picks, spots, spread, force_ref, next_ref,
+    react, seen_ref, found, weights, coupled, pair_ref, sem,
 ):
     depth, across, along = fluid_ref.shape[1:]
     listed = pair_ref.shape[1]
@@ -196,7 +220,6 @@
     copy.start()
     rows = lax.broadcasted_iota(jnp.int32, (across, LANES), 0)
     halves = lax.broadcasted_iota(jnp.int32, (half, LANES), 0)
-    sites = lax.broadcasted_iota(jnp.int32, (fold * along, LANES), 0)
     subs = lax.broadcasted_iota(jnp.int32, (SUBLANES, along), 0)
     slabs = [(c, h) for c in range(3) for h in range(depth)]
 
@@ -218,25 +241,14 @@
                 beside += fluid_ref[c, h, at + 1 : at + SUBLANES + 1, :]
             else:
                 beside += jnp.where(subs == SUBLANES - 1, 0.0, pltpu.roll(here, SUBLANES - 1, 0))
-            beside += pltpu.roll(here, 1, 1) + pltpu.roll(here, along - 1, 1)
+            line = (c * depth + h) * across + at
+            beside += seen_ref[line : line + SUBLANES, wide : wide + along]
             if h > 0:
                 beside += fluid_ref[c, h - 1, at : at + SUBLANES, :]
             if h < depth - 1:
                 beside += fluid_ref[c, h + 1, at : at + SUBLANES, :]
             next_ref[c, h, at : at + SUBLANES, :] = (1.0 - 6.0 * diffuse) * here + diffuse * beside
 
-    spread[...] = spread_blocks([body_of(b) for b in range(blocks)])
-    for k, (c, h) in enumerate(slabs):
-        pieces[k * across : (k + 1) * across, :] = parts_of(fluid_ref[c, h])
-    for b in range(blocks):
-        height, over, spot = spot_of(b)
-        column = slice(b * LANES, (b + 1) * LANES)
-        one_hot = lane_one_hot(sites[:along], spot)
-        for n in range(PARTS):
-            picks[n * along : (n + 1) * along, column] = one_hot
-        one_hot = lane_one_hot(sites, jnp.where(over >= half, along, 0) + spot)
-        for n in range(PARTS):
-            spots[:, n * wide + b * LANES : n * wide + (b + 1) * LANES] = one_hot
     seen_ref[...] = jnp.dot(pieces[...], picks[...], preferred_element_type=F32)
 
     turns = blocks + listed
@@ -307,7 +319,7 @@
         next_ref[c, h] += jnp.concatenate(given, axis=0)
 
 
-def finish_kernel(counts, blocks, pairs, force_ref, partial_ref, wrap_ref, *refs):
+def finish_kernel(counts, blocks, pairs, force_ref, partial_ref, *refs):
     n_in = sum(counts)
     sent = refs[: counts[0]]
     height_ins, across_ins, along_ins = by_axis(refs[counts[0] : counts[0] + n_in], counts)
@@ -332,7 +344,7 @@
     edges = along_ins[0][...]
     if len(along_ins) > 1:
         edges = edges + along_ins[1][...]
-    edges = diffuse * (edges - wrap_ref[...])
+    edges = diffuse * edges
     lanes = lax.broadcasted_iota(jnp.int32, (across, along), 1)
     subs = lax.broadcasted_iota(jnp.int32, (SUBLANES, along), 0)
     tail = across - SUBLANES
@@ -353,7 +365,6 @@
 
     rows = lax.broadcasted_iota(jnp.int32, (across, LANES), 0)
     halves = lax.broadcasted_iota(jnp.int32, (half, LANES), 0)
-    sites = lax.broadcasted_iota(jnp.int32, (fold * along, LANES), 0)
     coupling = [[jnp.zeros((1, LANES), F32)] * blocks for _ in range(3)]
     for n, blob in enumerate(height_ins):
         own = sent[n]
@@ -369,12 +380,7 @@
             cell = jnp.where(above, own[cells + b : cells + b + 1, :], blob[cells + b : cells + b + 1, :])
             height, over, spot = places(cell.astype(jnp.int32), across, along)
             lined.append((height, over))
-            one_hot = lane_one_hot(sites[:along], spot)
-            for m in range(PARTS):
-                picks[m * along : (m + 1) * along, b * LANES : (b + 1) * LANES] = one_hot
-            one_hot = lane_one_hot(sites, jnp.where(over >= half, along, 0) + spot)
-            for m in range(PARTS):
-                spots[:, m * wide + b * LANES : m * wide + (b + 1) * LANES] = one_hot
+            mark_cells(picks, spots, b, over, spot, half, wide)
         seen_ref[...] = jnp.dot(pieces[...], picks[...], preferred_element_type=F32)
         for b in range(blocks):
             height, over = lined[b]
@@ -476,12 +482,18 @@
     def kept(value):
         return pltpu.with_memory_space_constraint(value, pltpu.VMEM)
 
-    fluid_kept, wrapped, *packed = pl.pallas_call(
+    fluid_kept, pieces, picks, spots, spread, *packed = pl.pallas_call(
         functools.partial(pack_kernel, counts),
-        out_shape=[pltpu.VMEM(fluid.shape, F32), pltpu.VMEM((across, along), F32)]
+        out_shape=[
+            pltpu.VMEM(fluid.shape, F32),
+            pltpu.VMEM((3 * depth * across, PARTS * along), BF16),
+            pltpu.VMEM((PARTS * along, blocks * LANES + along), BF16),
+            pltpu.VMEM((fold * along, wide), BF16),
+            pltpu.VMEM((blocks * LANES, 9 * LANES), F32),
+        ]
         + [pltpu.VMEM(shape, F32) for shape, n in zip(shapes, counts) for _ in range(n)],
         in_specs=[hbm] * 5,
-        out_specs=[vmem] * (2 + sum(counts)),
+        out_specs=[vmem] * (5 + sum(counts)),
         scratch_shapes=[
             pltpu.SMEM(cross_pairs.shape, jnp.int32),
             pltpu.VMEM(particles.shape, F32),
@@ -489,6 +501,7 @@
             pltpu.VMEM(drag_share.shape, F32),
             pltpu.SemaphoreType.DMA((7,)),
         ],
+        compiler_params=pltpu.CompilerParams(vmem_limit_bytes=GRANT),
         name="pack",
     )(cross_pairs, particles, drag_cell, drag_share, fluid)
     received = []
@@ -498,23 +511,20 @@
     force, partial = pl.pallas_call(
         functools.partial(local_kernel, blocks, pairs),
         out_shape=[pltpu.VMEM((3, blocks, LANES), F32), pltpu.VMEM(fluid.shape, F32)],
-        in_specs=[hbm, vmem, vmem],
+        in_specs=[hbm] + [vmem] * 6,
         out_specs=[vmem, vmem],
         scratch_shapes=[
-            pltpu.VMEM((blocks * LANES, 9 * LANES), F32),
             pltpu.VMEM((listed, LANES, LANES), F32),
-            pltpu.VMEM((3 * depth * across, PARTS * along), BF16),
-            pltpu.VMEM((3 * depth * across, blocks * LANES), F32),
-            pltpu.VMEM((PARTS * along, blocks * LANES), BF16),
+            pltpu.VMEM((3 * depth * across, blocks * LANES + along), F32),
             pltpu.VMEM((2 * listed, SUBLANES, LANES), F32),
             pltpu.VMEM((3 * depth, blocks * LANES), F32),
             pltpu.VMEM((3 * depth * half, wide), BF16),
-            pltpu.VMEM((fold * along, wide), BF16),
             pltpu.SMEM((2, listed), jnp.int32),
             pltpu.SemaphoreType.DMA,
         ],
+        compiler_params=pltpu.CompilerParams(vmem_limit_bytes=GRANT),
         name="local",
-    )(local_pairs.T, kept(packed[0]), kept(fluid_kept))
+    )(local_pairs.T, *[kept(value) for value in (packed[0], fluid_kept, pieces, picks, spots, spread)])
 
     out_force, out_next = pl.pallas_call(
         functools.partial(finish_kernel, counts, blocks, pairs),
@@ -522,7 +532,7 @@
             jax.ShapeDtypeStruct((3, blocks, LANES), F32),
             jax.ShapeDtypeStruct(fluid.shape, F32),
         ],
-        in_specs=[vmem] * (3 + counts[0] + len(received)),
+        in_specs=[vmem] * (2 + counts[0] + len(received)),
         out_specs=[vmem, hbm],
         scratch_shapes=[
             pltpu.VMEM(fluid.shape, F32),
@@ -534,8 +544,9 @@
             pltpu.VMEM((fold * along, wide), BF16),
             pltpu.SemaphoreType.DMA((5,)),
         ],
+        compiler_params=pltpu.CompilerParams(vmem_limit_bytes=GRANT),
         name="finish",
-    )(*[kept(value) for value in [force, partial, wrapped, *packed[: counts[0]], *received]])
+    )(*[kept(value) for value in [force, partial, *packed[: counts[0]], *received]])
     return jnp.transpose(out_force, (1, 0, 2)), out_next
 
 

time: 17.9 us -> 22.5 us (1.26)
  local copies, waits for them, and re-layouts: 0 us -> 4.56 us
    unnamed x0 -> x12, local copies, waits for them, and re-layouts: none -> 4.56 us
  transfers between devices with their start and end apart: 5 -> 5, of which waited for: 0 -> 0; matrix products, arithmetic and copies ran while one was open for 0% -> 0% of each run, Pallas kernels for 17% -> 12%
where the time goes in v5:
time: 22.5 us; the launch traced here: 22.2 us
  starting transfers between devices  10.1 us (45%)
  Pallas kernels  6.75 us (30%)
  local copies, waits for them, and re-layouts  4.56 us (20%)
  between operations  0.73 us (3%)
    ppermute x5, starting transfers between devices, exchange(): results.append(lax.ppermute(payload, axis, route))  10.1 us
    unnamed x12, local copies, waits for them, and re-layouts  4.56 us
    pallas_call x1, Pallas kernels, body(): pl.pallas_call(functools.partial(local_kernel, blocks, pairs), out_shape=...  2.76 us
    pallas_call x1, Pallas kernels, body(): pl.pallas_call(functools.partial(finish_kernel, counts, blocks, pairs), o...  2.23 us
    pallas_call x1, Pallas kernels, body(): pl.pallas_call(functools.partial(pack_kernel, counts), out_shape=[pltpu.V...  1.77 us
  transfers between devices with their start and end apart: 5, of which 0 were waited for; matrix products, arithmetic and copies ran while one was open for 0% of the time, Pallas kernels for 12%

profile of v5, /device:TPU:10, one launch (start us, length us, event | category | flops | bytes accessed | tf_op | source)
XLA Modules:
  0.0 22.2 jit_solution(996522102892652502)
XLA Ops:
  0.6 0.0 copy-start
  0.6 1.1 %copy-done = f32[3,8,64,128]{3,2,1,0:T(8,128)S(1)} copy-done((f32[3,8,64,128]{3,2,1,0:T(8,128)S(1)}, f32[3,8,64,128]{3,2,1,0:T(8,128)}, u32[]{:S(2)}) %copy-start) | copy-done | bytes 786456
  1.8 0.0 copy-start.1
  1.8 0.7 %copy-done.1 = f32[4,8,128]{2,1,0:T(8,128)S(1)} copy-done((f32[4,8,128]{2,1,0:T(8,128)S(1)}, f32[4,8,128]{2,1,0:T(8,128)}, u32[]{:S(2)}) %copy-start.1) | copy-done | bytes 16408
  2.5 0.0 copy-start.2
  2.5 0.7 %copy-done.2 = s32[4,128]{1,0:T(4,128)S(1)} copy-done((s32[4,128]{1,0:T(4,128)S(1)}, s32[4,128]{1,0:T(4,128)}, u32[]{:S(2)}) %copy-start.2) | copy-done | bytes 2072
  3.2 0.0 copy-start.3
  3.2 0.7 %copy-done.3 = f32[4,128]{1,0:T(4,128)S(1)} copy-done((f32[4,128]{1,0:T(4,128)S(1)}, f32[4,128]{1,0:T(4,128)}, u32[]{:S(2)}) %copy-start.3) | copy-done | bytes 2072
  3.8 0.0 copy-start.4
  3.8 0.7 %copy-done.4 = s32[2,2]{1,0:T(2,128)S(1)} copy-done((s32[2,2]{1,0:T(2,128)S(1)}, s32[2,2]{1,0:T(2,128)}, u32[]{:S(2)}) %copy-start.4) | copy-done | bytes 40
  4.5 1.8 %pack.1 = (f32[3,8,64,128]{3,2,1,0:T(8,128)S(1)}, bf16[1536,256]{1,0:T(8,128)(2,1)S(1)}, bf16[256,640]{1,0:T(8,128)(2,1)S(1)}, bf16[256,1024]{1,0:T(8,128)(2,1)S...) custom-call(s32[2,2]{1,0:T(2,128)S(1)} %copy-done.4, ...), custom_call_target="tpu_custom_call" | custom-call | tf_op jit(solution)/shard_map/pack/pallas_call | solution.py:485
  6.3 0.1 collective-permute-start
  6.4 0.5 %collective-permute-start.3 = (f32[64,128]{1,0:T(8,128)S(1)}, f32[64,128]{1,0:T(8,128)S(1)}, u32[]{:S(2)}, u32[]{:S(2)}) collective-permute-start(f32[64,128]{1,0:T(8,128)S(1)} %get-tuple-element.26), channel_id=1, source_target_pairs={{0,1},{1,0},{2,3},{3,2},{4,5},{5,4},{6,7},{7,6},{8,9},{9,8},{10,11... | collective-permute-start | bytes 98312 | tf_op jit(solution)/shard_map/ppermute | solution.py:464
  6.9 4.6 %collective-permute-start.4 = (f32[64,128]{1,0:T(8,128)S(1)}, f32[64,128]{1,0:T(8,128)S(1)}, u32[]{:S(2)}, u32[]{:S(2)}) collective-permute-start(f32[64,128]{1,0:T(8,128)S(1)} %get-tuple-element.27), channel_id=1, source_target_pairs={{1,2},{2,1},{5,6},{6,5},{9,10},{10,9},{13,14},{14,13},{17,18},{18,... | collective-permute-start | bytes 98312 | tf_op jit(solution)/shard_map/ppermute | solution.py:464
  11.5 0.6 %collective-permute-start.1 = (f32[24,128]{1,0:T(8,128)S(1)}, f32[24,128]{1,0:T(8,128)S(1)}, u32[]{:S(2)}, u32[]{:S(2)}) collective-permute-start(f32[24,128]{1,0:T(8,128)S(1)} %get-tuple-element.24), channel_id=1, source_target_pairs={{0,4},{4,0},{8,12},{12,8},{1,5},{5,1},{9,13},{13,9},{2,6},{6,2},{1... | collective-permute-start | bytes 36872 | tf_op jit(solution)/shard_map/ppermute | solution.py:464
  12.1 4.3 %collective-permute-start.2 = (f32[24,128]{1,0:T(8,128)S(1)}, f32[24,128]{1,0:T(8,128)S(1)}, u32[]{:S(2)}, u32[]{:S(2)}) collective-permute-start(f32[24,128]{1,0:T(8,128)S(1)} %get-tuple-element.25), channel_id=1, source_target_pairs={{4,8},{8,4},{5,9},{9,5},{6,10},{10,6},{7,11},{11,7},{20,24},{24,20... | collective-permute-start | bytes 36872 | tf_op jit(solution)/shard_map/ppermute | solution.py:464
  16.5 0.0 copy-start.5
  16.5 0.7 %copy-done.5 = s32[4,2]{0,1:T(2,128)S(1)} copy-done((s32[4,2]{0,1:T(2,128)S(1)}, s32[4,2]{0,1:T(2,128)}, u32[]{:S(2)}) %copy-start.5) | copy-done | bytes 56
  17.1 2.8 %local.1 = (f32[3,4,128]{2,1,0:T(4,128)S(1)}, f32[3,8,64,128]{3,2,1,0:T(8,128)S(1)}) custom-call(s32[2,4]{1,0:T(2,128)S(1)} %bitcast.2, f32[240,128]{1,0:T(8,128)S(1)} %get-tuple-element.16.blob_ref.refs_0_, f32[3,8,64,128]{3,2,1,0:T(8,128)S(1)} %get-tuple-element.17.fluid_ref, bf16[1536,256]{1,0:T(8,128)(2,1)S(1)} %get-tuple-element.18.pieces, ...), custom_call_target="tpu_custom_call" | custom-call | tf_op jit(solution)/shard_map/local/pallas_call | solution.py:511
  19.9 0.0 collective-permute-done.1.refs_2_
  19.9 0.0 collective-permute-done.2.refs_3_
  19.9 0.0 collective-permute-done.3.refs_4_
  19.9 0.0 collective-permute-done.4.refs_5_
  19.9 0.0 collective-permute-done.refs_1_
  20.0 2.2 %finish.1 = (f32[3,4,128]{2,1,0:T(4,128)}, f32[3,8,64,128]{3,2,1,0:T(8,128)}) custom-call(f32[3,4,128]{2,1,0:T(4,128)S(1)} %get-tuple-element.22.force_ref, f32[3,8,64,128]{3,2,1,0:T(8,128)S(1)} %get-tuple-element.23.partial_ref, f32[240,128]{1,0:T(8,128)S(1)} %get-tuple-element.16.blob_ref.refs_0_, f32[240,128]{1,0:T(8,128)S(1)} %collective-permute-done.refs_1_, ...), custom_call_target="tpu_custom_call" | custom-call | tf_op jit(solution)/shard_map/finish/pallas_call | solution.py:529
Async XLA Ops:
  0.6 1.1 %copy-start = (f32[3,8,64,128]{3,2,1,0:T(8,128)S(1)}, f32[3,8,64,128]{3,2,1,0:T(8,128)}, u32[]{:S(2)}) copy-start(f32[3,8,64,128]{3,2,1,0:T(8,128)} %fluid_hbm.1) | copy-start | bytes 2359300
  1.8 0.7 %copy-start.1 = (f32[4,8,128]{2,1,0:T(8,128)S(1)}, f32[4,8,128]{2,1,0:T(8,128)}, u32[]{:S(2)}) copy-start(f32[4,8,128]{2,1,0:T(8,128)} %part_hbm.1) | copy-start | bytes 49156
  2.5 0.7 %copy-start.2 = (s32[4,128]{1,0:T(4,128)S(1)}, s32[4,128]{1,0:T(4,128)}, u32[]{:S(2)}) copy-start(s32[4,128]{1,0:T(4,128)} %cell_hbm.1) | copy-start | bytes 6148
  3.2 0.7 %copy-start.3 = (f32[4,128]{1,0:T(4,128)S(1)}, f32[4,128]{1,0:T(4,128)}, u32[]{:S(2)}) copy-start(f32[4,128]{1,0:T(4,128)} %share_hbm.1) | copy-start | bytes 6148
  3.8 0.7 %copy-start.4 = (s32[2,2]{1,0:T(2,128)S(1)}, s32[2,2]{1,0:T(2,128)}, u32[]{:S(2)}) copy-start(s32[2,2]{1,0:T(2,128)} %pair_hbm.1) | copy-start | bytes 52
  6.3 13.6 %collective-permute-start = (f32[240,128]{1,0:T(8,128)S(1)}, f32[240,128]{1,0:T(8,128)S(1)}, u32[]{:S(2)}, u32[]{:S(2)}) collective-permute-start(f32[240,128]{1,0:T(8,128)S(1)} %get-tuple-element.16.blob_ref.refs_0_), channel_id=1, source_target_pairs={{0,16},{16,0},{1,17},{17,1},{2,18},{18,2},{3,19},{19,3},{4,20},{20... | collective-permute-start | bytes 368648 | tf_op jit(solution)/shard_map/ppermute | solution.py:464
  6.4 13.5 %collective-permute-start.3 = (f32[64,128]{1,0:T(8,128)S(1)}, f32[64,128]{1,0:T(8,128)S(1)}, u32[]{:S(2)}, u32[]{:S(2)}) collective-permute-start(f32[64,128]{1,0:T(8,128)S(1)} %get-tuple-element.26), channel_id=1, source_target_pairs={{0,1},{1,0},{2,3},{3,2},{4,5},{5,4},{6,7},{7,6},{8,9},{9,8},{10,11... | collective-permute-start | bytes 98312 | tf_op jit(solution)/shard_map/ppermute | solution.py:464
  6.9 13.0 %collective-permute-start.4 = (f32[64,128]{1,0:T(8,128)S(1)}, f32[64,128]{1,0:T(8,128)S(1)}, u32[]{:S(2)}, u32[]{:S(2)}) collective-permute-start(f32[64,128]{1,0:T(8,128)S(1)} %get-tuple-element.27), channel_id=1, source_target_pairs={{1,2},{2,1},{5,6},{6,5},{9,10},{10,9},{13,14},{14,13},{17,18},{18,... | collective-permute-start | bytes 98312 | tf_op jit(solution)/shard_map/ppermute | solution.py:464
  11.5 8.4 %collective-permute-start.1 = (f32[24,128]{1,0:T(8,128)S(1)}, f32[24,128]{1,0:T(8,128)S(1)}, u32[]{:S(2)}, u32[]{:S(2)}) collective-permute-start(f32[24,128]{1,0:T(8,128)S(1)} %get-tuple-element.24), channel_id=1, source_target_pairs={{0,4},{4,0},{8,12},{12,8},{1,5},{5,1},{9,13},{13,9},{2,6},{6,2},{1... | collective-permute-start | bytes 36872 | tf_op jit(solution)/shard_map/ppermute | solution.py:464
  12.1 7.8 %collective-permute-start.2 = (f32[24,128]{1,0:T(8,128)S(1)}, f32[24,128]{1,0:T(8,128)S(1)}, u32[]{:S(2)}, u32[]{:S(2)}) collective-permute-start(f32[24,128]{1,0:T(8,128)S(1)} %get-tuple-element.25), channel_id=1, source_target_pairs={{4,8},{8,4},{5,9},{9,5},{6,10},{10,6},{7,11},{11,7},{20,24},{24,20... | collective-permute-start | bytes 36872 | tf_op jit(solution)/shard_map/ppermute | solution.py:464
  16.5 0.7 %copy-start.5 = (s32[4,2]{0,1:T(2,128)S(1)}, s32[4,2]{0,1:T(2,128)}, u32[]{:S(2)}) copy-start(s32[4,2]{0,1:T(2,128)} %param.7) | copy-start | bytes 100

commit v6 on v5

--- a/solution.py
+++ b/solution.py
@@ -119,10 +119,10 @@
     return [lax.rem(lax.axis_index(axis), 2) == 0 for axis in AXES]
 
 
-def pack_kernel(counts, pair_hbm, part_hbm, cell_hbm, share_hbm, fluid_hbm, *refs):
-    n_out = 5 + sum(counts)
-    fluid_ref, pieces, picks, spots, spread = refs[:5]
-    height_outs, across_outs, along_outs = by_axis(refs[5:n_out], counts)
+def pack_kernel(counts, list_hbm, pair_hbm, part_hbm, cell_hbm, share_hbm, fluid_hbm, *refs):
+    n_out = 6 + sum(counts)
+    list_ref, fluid_ref, pieces, picks, spots, spread = refs[:6]
+    height_outs, across_outs, along_outs = by_axis(refs[6:n_out], counts)
     pair_ref, part_ref, cell_ref, share_ref, sems = refs[n_out:]
     depth, across, along = fluid_ref.shape[1:]
     blocks, pairs = part_ref.shape[0], pair_ref.shape[0]
@@ -130,7 +130,7 @@
     half = across // fold
     wide = blocks * LANES
     bodies, cells, shares, lists, rows = blob_layout(across, blocks, pairs)
-    small = [(part_hbm, part_ref), (cell_hbm, cell_ref), (share_hbm, share_ref), (pair_hbm, pair_ref)]
+    small = [(part_hbm, part_ref), (cell_hbm, cell_ref), (share_hbm, share_ref), (pair_hbm, pair_ref), (list_hbm, list_ref)]
     small = [pltpu.make_async_copy(source, target, sems.at[3 + n]) for n, (source, target) in enumerate(small)]
     copies = [pltpu.make_async_copy(fluid_hbm.at[c], fluid_ref.at[c], sems.at[c]) for c in range(3)]
     for copy in small + copies:
@@ -207,8 +207,8 @@
 
 
 def local_kernel(
-    blocks, pairs, pair_hbm, blob_ref, fluid_ref, pieces, picks, spots, spread, force_ref, next_ref,
-    react, seen_ref, found, weights, coupled, pair_ref, sem,
+    blocks, pairs, pair_ref, blob_ref, fluid_ref, pieces, picks, spots, spread, force_ref, next_ref, source_ref,
+    react, seen_ref, found, weights, coupled,
 ):
     depth, across, along = fluid_ref.shape[1:]
     listed = pair_ref.shape[1]
@@ -216,8 +216,6 @@
     half = across // fold
     wide = blocks * LANES
     bodies, cells, shares, _, _ = blob_layout(across, blocks, pairs)
-    copy = pltpu.make_async_copy(pair_hbm, pair_ref, sem)
-    copy.start()
     rows = lax.broadcasted_iota(jnp.int32, (across, LANES), 0)
     halves = lax.broadcasted_iota(jnp.int32, (half, LANES), 0)
     subs = lax.broadcasted_iota(jnp.int32, (SUBLANES, along), 0)
@@ -287,17 +285,12 @@
                 coupled[k * half : (k + 1) * half, n * wide + b * LANES : n * wide + (b + 1) * LANES] = place_lines(
                     ones, part[k : k + 1], half
                 )
-    sources = [
-        lax.dot_general(
-            coupled[c * depth * half : (c + 1) * depth * half, :],
-            spots[...],
-            (((1,), (1,)), ((), ())),
-            preferred_element_type=F32,
+    for c in range(3):
+        face = slice(c * depth * half, (c + 1) * depth * half)
+        source_ref[face, :] = lax.dot_general(
+            coupled[face, :], spots[...], (((1,), (1,)), ((), ())), preferred_element_type=F32
         )
-        for c in range(3)
-    ]
-
-    copy.wait()
+
     for i in range(listed):
         for c, h in share_out[blocks + i]:
             stencil(c, h)
@@ -314,12 +307,9 @@
                 for side in range(2):
                     total += jnp.where(pair_ref[side, i] == b, found[2 * i + side, d : d + 1, :], 0.0)
             force_ref[d, b : b + 1, :] = total
-    for k, (c, h) in enumerate(slabs):
-        given = [sources[c][h * half : (h + 1) * half, f * along : (f + 1) * along] for f in range(fold)]
-        next_ref[c, h] += jnp.concatenate(given, axis=0)
-
-
-def finish_kernel(counts, blocks, pairs, force_ref, partial_ref, *refs):
+
+
+def finish_kernel(counts, blocks, pairs, force_ref, partial_ref, source_ref, *refs):
     n_in = sum(counts)
     sent = refs[: counts[0]]
     height_ins, across_ins, along_ins = by_axis(refs[counts[0] : counts[0] + n_in], counts)
@@ -353,7 +343,10 @@
     for c in range(3):
         for h in range(depth):
             k = c * depth + h
-            value = partial_ref[c, h]
+            given = [
+                source_ref[k * half : (k + 1) * half, f * along : (f + 1) * along] for f in range(fold)
+            ]
+            value = partial_ref[c, h] + jnp.concatenate(given, axis=0)
             value += jnp.where(rim, pltpu.roll(edges, (along - 2 * k) % along, 1) if k else edges, 0.0)
             next_ref[c, h] = value
             next_ref[c, h, :SUBLANES, :] += jnp.where(subs == 0, across_low[k : k + 1, :], 0.0)
@@ -477,14 +470,16 @@
     rows = blob_layout(across, blocks, pairs)[-1]
     shapes = [(rows, along), (3 * depth, along), (across, along)]
     vmem = pl.BlockSpec(memory_space=pltpu.VMEM)
-    hbm = pl.BlockSpec(memory_space=pl.ANY)
+    hbm = pl.BlockSpec(memory_space=pltpu.HBM)
+    smem = pl.BlockSpec(memory_space=pltpu.SMEM)
 
     def kept(value):
         return pltpu.with_memory_space_constraint(value, pltpu.VMEM)
 
-    fluid_kept, pieces, picks, spots, spread, *packed = pl.pallas_call(
+    listing, fluid_kept, pieces, picks, spots, spread, *packed = pl.pallas_call(
         functools.partial(pack_kernel, counts),
         out_shape=[
+            pltpu.SMEM((2, listed), jnp.int32),
             pltpu.VMEM(fluid.shape, F32),
             pltpu.VMEM((3 * depth * across, PARTS * along), BF16),
             pltpu.VMEM((PARTS * along, blocks * LANES + along), BF16),
@@ -492,39 +487,49 @@
             pltpu.VMEM((blocks * LANES, 9 * LANES), F32),
         ]
         + [pltpu.VMEM(shape, F32) for shape, n in zip(shapes, counts) for _ in range(n)],
-        in_specs=[hbm] * 5,
-        out_specs=[vmem] * (5 + sum(counts)),
+        in_specs=[hbm] * 6,
+        out_specs=[smem] + [vmem] * (5 + sum(counts)),
         scratch_shapes=[
             pltpu.SMEM(cross_pairs.shape, jnp.int32),
             pltpu.VMEM(particles.shape, F32),
             pltpu.VMEM(drag_cell.shape, jnp.int32),
             pltpu.VMEM(drag_share.shape, F32),
-            pltpu.SemaphoreType.DMA((7,)),
+            pltpu.SemaphoreType.DMA((8,)),
         ],
         compiler_params=pltpu.CompilerParams(vmem_limit_bytes=GRANT),
         name="pack",
-    )(cross_pairs, particles, drag_cell, drag_share, fluid)
+    )(
+        *[
+            pltpu.with_memory_space_constraint(value, pltpu.HBM)
+            for value in (local_pairs.T, cross_pairs, particles, drag_cell, drag_share, fluid)
+        ]
+    )
     received = []
     for axis, payloads in zip(AXES, by_axis(packed, counts)):
         received += exchange(payloads, axis)
 
-    force, partial = pl.pallas_call(
+    force, partial, source = pl.pallas_call(
         functools.partial(local_kernel, blocks, pairs),
-        out_shape=[pltpu.VMEM((3, blocks, LANES), F32), pltpu.VMEM(fluid.shape, F32)],
-        in_specs=[hbm] + [vmem] * 6,
-        out_specs=[vmem, vmem],
+        out_shape=[
+            pltpu.VMEM((3, blocks, LANES), F32),
+            pltpu.VMEM(fluid.shape, F32),
+            pltpu.VMEM((3 * depth * half, fold * along), F32),
+        ],
+        in_specs=[smem] + [vmem] * 6,
+        out_specs=[vmem] * 3,
         scratch_shapes=[
             pltpu.VMEM((listed, LANES, LANES), F32),
             pltpu.VMEM((3 * depth * across, blocks * LANES + along), F32),
             pltpu.VMEM((2 * listed, SUBLANES, LANES), F32),
             pltpu.VMEM((3 * depth, blocks * LANES), F32),
             pltpu.VMEM((3 * depth * half, wide), BF16),
-            pltpu.SMEM((2, listed), jnp.int32),
-            pltpu.SemaphoreType.DMA,
         ],
         compiler_params=pltpu.CompilerParams(vmem_limit_bytes=GRANT),
         name="local",
-    )(local_pairs.T, *[kept(value) for value in (packed[0], fluid_kept, pieces, picks, spots, spread)])
+    )(
+        pltpu.with_memory_space_constraint(listing, pltpu.SMEM),
+        *[kept(value) for value in (packed[0], fluid_kept, pieces, picks, spots, spread)],
+    )
 
     out_force, out_next = pl.pallas_call(
         functools.partial(finish_kernel, counts, blocks, pairs),
@@ -532,7 +537,7 @@
             jax.ShapeDtypeStruct((3, blocks, LANES), F32),
             jax.ShapeDtypeStruct(fluid.shape, F32),
         ],
-        in_specs=[vmem] * (2 + counts[0] + len(received)),
+        in_specs=[vmem] * (3 + counts[0] + len(received)),
         out_specs=[vmem, hbm],
         scratch_shapes=[
             pltpu.VMEM(fluid.shape, F32),
@@ -546,7 +551,7 @@
         ],
         compiler_params=pltpu.CompilerParams(vmem_limit_bytes=GRANT),
         name="finish",
-    )(*[kept(value) for value in [force, partial, *packed[: counts[0]], *received]])
+    )(*[kept(value) for value in [force, partial, source, *packed[: counts[0]], *received]])
     return jnp.transpose(out_force, (1, 0, 2)), out_next
 
 

time: 22.5 us -> 18.5 us (0.82)
  the two profiles are of different devices: /device:TPU:10 before, /device:TPU:12 now
where the time goes in v6:
time: 18.5 us; the launch traced here: 18.2 us
  starting transfers between devices  9.12 us (49%)
  Pallas kernels  6.71 us (36%)
  waiting for transfers between devices  1.69 us (9%)
  between operations  0.69 us (4%)
    ppermute x5, starting transfers between devices, exchange(): results.append(lax.ppermute(payload, axis, route))  9.12 us
    pallas_call x1, Pallas kernels, body(): pl.pallas_call(functools.partial(local_kernel, blocks, pairs), out_shape=...  2.4 us
    pallas_call x1, Pallas kernels, body(): pl.pallas_call(functools.partial(finish_kernel, counts, blocks, pairs), o...  2.25 us
    pallas_call x1, Pallas kernels, body(): pl.pallas_call(functools.partial(pack_kernel, counts), out_shape=[pltpu.S...  2.06 us
    ppermute x5, waiting for transfers between devices, exchange(): results.append(lax.ppermute(payload, axis, route))  1.69 us
  transfers between devices with their start and end apart: 5, of which 1 were waited for; matrix products, arithmetic and copies ran while one was open for 0% of the time, Pallas kernels for 13%

profile of v6, /device:TPU:12, one launch (start us, length us, event | category | flops | bytes accessed | tf_op | source)
XLA Modules:
  0.0 18.2 jit_solution(11550762695906968755)
XLA Ops:
  0.6 2.1 %pack.1 = (s32[2,4]{1,0:T(2,128)S(4)}, f32[3,8,64,128]{3,2,1,0:T(8,128)S(1)}, bf16[1536,256]{1,0:T(8,128)(2,1)S(1)}, bf16[256,640]{1,0:T(8,128)(2,1)S(1)}, bf16[...) custom-call(s32[2,4]{1,0:T(2,128)} %bitcast.2, ...), custom_call_target="tpu_custom_call" | custom-call | tf_op jit(solution)/shard_map/pack/pallas_call | solution.py:479
  2.7 0.1 collective-permute-start
  2.8 0.5 %collective-permute-start.3 = (f32[64,128]{1,0:T(8,128)S(1)}, f32[64,128]{1,0:T(8,128)S(1)}, u32[]{:S(2)}, u32[]{:S(2)}) collective-permute-start(f32[64,128]{1,0:T(8,128)S(1)} %get-tuple-element.30), channel_id=1, source_target_pairs={{0,1},{1,0},{2,3},{3,2},{4,5},{5,4},{6,7},{7,6},{8,9},{9,8},{10,11... | collective-permute-start | bytes 98312 | tf_op jit(solution)/shard_map/ppermute | solution.py:457
  3.3 4.6 %collective-permute-start.4 = (f32[64,128]{1,0:T(8,128)S(1)}, f32[64,128]{1,0:T(8,128)S(1)}, u32[]{:S(2)}, u32[]{:S(2)}) collective-permute-start(f32[64,128]{1,0:T(8,128)S(1)} %get-tuple-element.31), channel_id=1, source_target_pairs={{1,2},{2,1},{5,6},{6,5},{9,10},{10,9},{13,14},{14,13},{17,18},{18,... | collective-permute-start | bytes 98312 | tf_op jit(solution)/shard_map/ppermute | solution.py:457
  7.9 1.6 %collective-permute-start.1 = (f32[24,128]{1,0:T(8,128)S(1)}, f32[24,128]{1,0:T(8,128)S(1)}, u32[]{:S(2)}, u32[]{:S(2)}) collective-permute-start(f32[24,128]{1,0:T(8,128)S(1)} %get-tuple-element.28), channel_id=1, source_target_pairs={{0,4},{4,0},{8,12},{12,8},{1,5},{5,1},{9,13},{13,9},{2,6},{6,2},{1... | collective-permute-start | bytes 36872 | tf_op jit(solution)/shard_map/ppermute | solution.py:457
  9.5 2.4 %collective-permute-start.2 = (f32[24,128]{1,0:T(8,128)S(1)}, f32[24,128]{1,0:T(8,128)S(1)}, u32[]{:S(2)}, u32[]{:S(2)}) collective-permute-start(f32[24,128]{1,0:T(8,128)S(1)} %get-tuple-element.29), channel_id=1, source_target_pairs={{4,8},{8,4},{5,9},{9,5},{6,10},{10,6},{7,11},{11,7},{20,24},{24,20... | collective-permute-start | bytes 36872 | tf_op jit(solution)/shard_map/ppermute | solution.py:457
  11.8 2.4 %local.1 = (f32[3,4,128]{2,1,0:T(4,128)S(1)}, f32[3,8,64,128]{3,2,1,0:T(8,128)S(1)}, f32[768,256]{1,0:T(8,128)S(1)}) custom-call(s32[2,4]{1,0:T(2,128)S(4)} %get-tuple-element.18.pair_ref, f32[240,128]{1,0:T(8,128)S(1)} %get-tuple-element.19.blob_ref.refs_0_, f32[3,8,64,128]{3,2,1,0:T(8,128)S(1)} %get-tuple-element.20.fluid_ref, ...), custom_call_target="tpu_custom_call" | custom-call | tf_op jit(solution)/shard_map/local/pallas_call | solution.py:511
  14.2 0.0 collective-permute-done.1.refs_2_
  14.3 1.7 %collective-permute-done.2.refs_3_ = f32[24,128]{1,0:T(8,128)S(1)} collective-permute-done((f32[24,128]{1,0:T(8,128)S(1)}, f32[24,128]{1,0:T(8,128)S(1)}, u32[]{:S(2)}, u32[]{:S(2)}) %collective-permute-start.2) | collective-permute-done | bytes 12320 | tf_op jit(solution)/shard_map/ppermute | solution.py:457
  15.9 0.0 collective-permute-done.3.refs_4_
  15.9 0.0 collective-permute-done.4.refs_5_
  15.9 0.0 collective-permute-done.refs_1_
  15.9 2.3 %finish.1 = (f32[3,4,128]{2,1,0:T(4,128)}, f32[3,8,64,128]{3,2,1,0:T(8,128)}) custom-call(f32[3,4,128]{2,1,0:T(4,128)S(1)} %get-tuple-element.25.force_ref, f32[3,8,64,128]{3,2,1,0:T(8,128)S(1)} %get-tuple-element.26.partial_ref, f32[768,256]{1,0:T(8,128)S(1)} %get-tuple-element.27.source_ref, f32[240,128]{1,0:T(8,128)S(1)} %get-tuple-element.19.blob_ref.refs_0_, ...), custom_call_target="tpu_custom_call" | custom-call | tf_op jit(solution)/shard_map/finish/pallas_call | solution.py:534
Async XLA Ops:
  2.7 13.2 %collective-permute-start = (f32[240,128]{1,0:T(8,128)S(1)}, f32[240,128]{1,0:T(8,128)S(1)}, u32[]{:S(2)}, u32[]{:S(2)}) collective-permute-start(f32[240,128]{1,0:T(8,128)S(1)} %get-tuple-element.19.blob_ref.refs_0_), channel_id=1, source_target_pairs={{0,16},{16,0},{1,17},{17,1},{2,18},{18,2},{3,19},{19,3},{4,20},{20... | collective-permute-start | bytes 368648 | tf_op jit(solution)/shard_map/ppermute | solution.py:457
  2.8 13.2 %collective-permute-start.3 = (f32[64,128]{1,0:T(8,128)S(1)}, f32[64,128]{1,0:T(8,128)S(1)}, u32[]{:S(2)}, u32[]{:S(2)}) collective-permute-start(f32[64,128]{1,0:T(8,128)S(1)} %get-tuple-element.30), channel_id=1, source_target_pairs={{0,1},{1,0},{2,3},{3,2},{4,5},{5,4},{6,7},{7,6},{8,9},{9,8},{10,11... | collective-permute-start | bytes 98312 | tf_op jit(solution)/shard_map/ppermute | solution.py:457
  3.3 12.6 %collective-permute-start.4 = (f32[64,128]{1,0:T(8,128)S(1)}, f32[64,128]{1,0:T(8,128)S(1)}, u32[]{:S(2)}, u32[]{:S(2)}) collective-permute-start(f32[64,128]{1,0:T(8,128)S(1)} %get-tuple-element.31), channel_id=1, source_target_pairs={{1,2},{2,1},{5,6},{6,5},{9,10},{10,9},{13,14},{14,13},{17,18},{18,... | collective-permute-start | bytes 98312 | tf_op jit(solution)/shard_map/ppermute | solution.py:457
  7.9 6.3 %collective-permute-start.1 = (f32[24,128]{1,0:T(8,128)S(1)}, f32[24,128]{1,0:T(8,128)S(1)}, u32[]{:S(2)}, u32[]{:S(2)}) collective-permute-start(f32[24,128]{1,0:T(8,128)S(1)} %get-tuple-element.28), channel_id=1, source_target_pairs={{0,4},{4,0},{8,12},{12,8},{1,5},{5,1},{9,13},{13,9},{2,6},{6,2},{1... | collective-permute-start | bytes 36872 | tf_op jit(solution)/shard_map/ppermute | solution.py:457
  9.5 6.5 %collective-permute-start.2 = (f32[24,128]{1,0:T(8,128)S(1)}, f32[24,128]{1,0:T(8,128)S(1)}, u32[]{:S(2)}, u32[]{:S(2)}) collective-permute-start(f32[24,128]{1,0:T(8,128)S(1)} %get-tuple-element.29), channel_id=1, source_target_pairs={{4,8},{8,4},{5,9},{9,5},{6,10},{10,6},{7,11},{11,7},{20,24},{24,20... | collective-permute-start | bytes 36872 | tf_op jit(solution)/shard_map/ppermute | solution.py:457

commit v7 on v6

--- a/solution.py
+++ b/solution.py
@@ -6,6 +6,7 @@
 from jax.experimental import pallas as pl
 from jax.experimental.pallas import tpu as pltpu
 from jax.sharding import PartitionSpec as P
+
 
 soft_core = 0.01
 damp_normal = 0.3
@@ -136,9 +137,9 @@
     for copy in small + copies:
         copy.start()
     even = parities()
-    for copy in small:
+    for copy in small + copies:
         copy.wait()
-    for n, out in enumerate(height_outs):
+    for out in height_outs:
         for b in range(blocks):
             out[bodies + 8 * b : bodies + 8 * b + 8, :] = part_ref[b]
         out[cells:shares, :] = cell_ref[...].astype(F32)
@@ -164,7 +165,6 @@
     first = jnp.zeros((across, along), F32)
     last = jnp.zeros((across, along), F32)
     for c in range(3):
-        copies[c].wait()
         for n, out in enumerate(height_outs):
             upward = even[0] if n == 0 else jnp.logical_not(even[0])
             out[c * across : (c + 1) * across, :] = fluid_ref[c, jnp.where(upward, depth - 1, 0)]

time: 18.5 us -> 18.3 us (0.989)
  no operation moved by 1% of the time
where the time goes in v7:
time: 18.3 us; the launch traced here: 18.1 us
  starting transfers between devices  9.12 us (50%)
  Pallas kernels  6.57 us (36%)
  waiting for transfers between devices  1.69 us (9%)
  between operations  0.69 us (4%)
    ppermute x5, starting transfers between devices, exchange(): results.append(lax.ppermute(payload, axis, route))  9.12 us
    pallas_call x1, Pallas kernels, body(): pl.pallas_call(functools.partial(local_kernel, blocks, pairs), out_shape=...  2.39 us
    pallas_call x1, Pallas kernels, body(): pl.pallas_call(functools.partial(finish_kernel, counts, blocks, pairs), o...  2.25 us
    pallas_call x1, Pallas kernels, body(): pl.pallas_call(functools.partial(pack_kernel, counts), out_shape=[pltpu.S...  1.92 us
    ppermute x5, waiting for transfers between devices, exchange(): results.append(lax.ppermute(payload, axis, route))  1.69 us
  transfers between devices with their start and end apart: 5, of which 1 were waited for; matrix products, arithmetic and copies ran while one was open for 0% of the time, Pallas kernels for 13%

profile of v7, /device:TPU:12, one launch (start us, length us, event | category | flops | bytes accessed | tf_op | source)
XLA Modules:
  0.0 18.1 jit_solution(4525814404397466974)
XLA Ops:
  0.6 1.9 %pack.1 = (s32[2,4]{1,0:T(2,128)S(4)}, f32[3,8,64,128]{3,2,1,0:T(8,128)S(1)}, bf16[1536,256]{1,0:T(8,128)(2,1)S(1)}, bf16[256,640]{1,0:T(8,128)(2,1)S(1)}, bf16[...) custom-call(s32[2,4]{1,0:T(2,128)} %bitcast.2, ...), custom_call_target="tpu_custom_call" | custom-call | tf_op jit(solution)/shard_map/pack/pallas_call | solution.py:479
  2.6 0.1 collective-permute-start
  2.6 0.5 %collective-permute-start.3 = (f32[64,128]{1,0:T(8,128)S(1)}, f32[64,128]{1,0:T(8,128)S(1)}, u32[]{:S(2)}, u32[]{:S(2)}) collective-permute-start(f32[64,128]{1,0:T(8,128)S(1)} %get-tuple-element.30), channel_id=1, source_target_pairs={{0,1},{1,0},{2,3},{3,2},{4,5},{5,4},{6,7},{7,6},{8,9},{9,8},{10,11... | collective-permute-start | bytes 98312 | tf_op jit(solution)/shard_map/ppermute | solution.py:457
  3.1 4.6 %collective-permute-start.4 = (f32[64,128]{1,0:T(8,128)S(1)}, f32[64,128]{1,0:T(8,128)S(1)}, u32[]{:S(2)}, u32[]{:S(2)}) collective-permute-start(f32[64,128]{1,0:T(8,128)S(1)} %get-tuple-element.31), channel_id=1, source_target_pairs={{1,2},{2,1},{5,6},{6,5},{9,10},{10,9},{13,14},{14,13},{17,18},{18,... | collective-permute-start | bytes 98312 | tf_op jit(solution)/shard_map/ppermute | solution.py:457
  7.8 1.6 %collective-permute-start.1 = (f32[24,128]{1,0:T(8,128)S(1)}, f32[24,128]{1,0:T(8,128)S(1)}, u32[]{:S(2)}, u32[]{:S(2)}) collective-permute-start(f32[24,128]{1,0:T(8,128)S(1)} %get-tuple-element.28), channel_id=1, source_target_pairs={{0,4},{4,0},{8,12},{12,8},{1,5},{5,1},{9,13},{13,9},{2,6},{6,2},{1... | collective-permute-start | bytes 36872 | tf_op jit(solution)/shard_map/ppermute | solution.py:457
  9.3 2.4 %collective-permute-start.2 = (f32[24,128]{1,0:T(8,128)S(1)}, f32[24,128]{1,0:T(8,128)S(1)}, u32[]{:S(2)}, u32[]{:S(2)}) collective-permute-start(f32[24,128]{1,0:T(8,128)S(1)} %get-tuple-element.29), channel_id=1, source_target_pairs={{4,8},{8,4},{5,9},{9,5},{6,10},{10,6},{7,11},{11,7},{20,24},{24,20... | collective-permute-start | bytes 36872 | tf_op jit(solution)/shard_map/ppermute | solution.py:457
  11.7 2.4 %local.1 = (f32[3,4,128]{2,1,0:T(4,128)S(1)}, f32[3,8,64,128]{3,2,1,0:T(8,128)S(1)}, f32[768,256]{1,0:T(8,128)S(1)}) custom-call(s32[2,4]{1,0:T(2,128)S(4)} %get-tuple-element.18.pair_ref, f32[240,128]{1,0:T(8,128)S(1)} %get-tuple-element.19.blob_ref.refs_0_, f32[3,8,64,128]{3,2,1,0:T(8,128)S(1)} %get-tuple-element.20.fluid_ref, ...), custom_call_target="tpu_custom_call" | custom-call | tf_op jit(solution)/shard_map/local/pallas_call | solution.py:511
  14.1 0.0 collective-permute-done.1.refs_2_
  14.1 1.7 %collective-permute-done.2.refs_3_ = f32[24,128]{1,0:T(8,128)S(1)} collective-permute-done((f32[24,128]{1,0:T(8,128)S(1)}, f32[24,128]{1,0:T(8,128)S(1)}, u32[]{:S(2)}, u32[]{:S(2)}) %collective-permute-start.2) | collective-permute-done | bytes 12320 | tf_op jit(solution)/shard_map/ppermute | solution.py:457
  15.8 0.0 collective-permute-done.3.refs_4_
  15.8 0.0 collective-permute-done.4.refs_5_
  15.8 0.0 collective-permute-done.refs_1_
  15.8 2.3 %finish.1 = (f32[3,4,128]{2,1,0:T(4,128)}, f32[3,8,64,128]{3,2,1,0:T(8,128)}) custom-call(f32[3,4,128]{2,1,0:T(4,128)S(1)} %get-tuple-element.25.force_ref, f32[3,8,64,128]{3,2,1,0:T(8,128)S(1)} %get-tuple-element.26.partial_ref, f32[768,256]{1,0:T(8,128)S(1)} %get-tuple-element.27.source_ref, f32[240,128]{1,0:T(8,128)S(1)} %get-tuple-element.19.blob_ref.refs_0_, ...), custom_call_target="tpu_custom_call" | custom-call | tf_op jit(solution)/shard_map/finish/pallas_call | solution.py:534
Async XLA Ops:
  2.6 13.2 %collective-permute-start = (f32[240,128]{1,0:T(8,128)S(1)}, f32[240,128]{1,0:T(8,128)S(1)}, u32[]{:S(2)}, u32[]{:S(2)}) collective-permute-start(f32[240,128]{1,0:T(8,128)S(1)} %get-tuple-element.19.blob_ref.refs_0_), channel_id=1, source_target_pairs={{0,16},{16,0},{1,17},{17,1},{2,18},{18,2},{3,19},{19,3},{4,20},{20... | collective-permute-start | bytes 368648 | tf_op jit(solution)/shard_map/ppermute | solution.py:457
  2.6 13.2 %collective-permute-start.3 = (f32[64,128]{1,0:T(8,128)S(1)}, f32[64,128]{1,0:T(8,128)S(1)}, u32[]{:S(2)}, u32[]{:S(2)}) collective-permute-start(f32[64,128]{1,0:T(8,128)S(1)} %get-tuple-element.30), channel_id=1, source_target_pairs={{0,1},{1,0},{2,3},{3,2},{4,5},{5,4},{6,7},{7,6},{8,9},{9,8},{10,11... | collective-permute-start | bytes 98312 | tf_op jit(solution)/shard_map/ppermute | solution.py:457
  3.1 12.6 %collective-permute-start.4 = (f32[64,128]{1,0:T(8,128)S(1)}, f32[64,128]{1,0:T(8,128)S(1)}, u32[]{:S(2)}, u32[]{:S(2)}) collective-permute-start(f32[64,128]{1,0:T(8,128)S(1)} %get-tuple-element.31), channel_id=1, source_target_pairs={{1,2},{2,1},{5,6},{6,5},{9,10},{10,9},{13,14},{14,13},{17,18},{18,... | collective-permute-start | bytes 98312 | tf_op jit(solution)/shard_map/ppermute | solution.py:457
  7.8 6.3 %collective-permute-start.1 = (f32[24,128]{1,0:T(8,128)S(1)}, f32[24,128]{1,0:T(8,128)S(1)}, u32[]{:S(2)}, u32[]{:S(2)}) collective-permute-start(f32[24,128]{1,0:T(8,128)S(1)} %get-tuple-element.28), channel_id=1, source_target_pairs={{0,4},{4,0},{8,12},{12,8},{1,5},{5,1},{9,13},{13,9},{2,6},{6,2},{1... | collective-permute-start | bytes 36872 | tf_op jit(solution)/shard_map/ppermute | solution.py:457
  9.3 6.5 %collective-permute-start.2 = (f32[24,128]{1,0:T(8,128)S(1)}, f32[24,128]{1,0:T(8,128)S(1)}, u32[]{:S(2)}, u32[]{:S(2)}) collective-permute-start(f32[24,128]{1,0:T(8,128)S(1)} %get-tuple-element.29), channel_id=1, source_target_pairs={{4,8},{8,4},{5,9},{9,5},{6,10},{10,6},{7,11},{11,7},{20,24},{24,20... | collective-permute-start | bytes 36872 | tf_op jit(solution)/shard_map/ppermute | solution.py:457

commit v8 on v7

v8 whole, which is shorter than its diff:
```python
import functools

import jax
import jax.numpy as jnp
from jax import lax
from jax.experimental import pallas as pl
from jax.experimental.pallas import tpu as pltpu
from jax.sharding import PartitionSpec as P


soft_core = 0.01
damp_normal = 0.3
damp_tangent = 0.2
drag_coef = 1.5
diffuse = 0.1
source_gain = 0.5

F32 = jnp.float32
BF16 = jnp.bfloat16
PARTS = 2
EXACT = 3
LANES = 128
SUBLANES = 8
GRANT = 32 * 1024 * 1024
AXES = ("gx", "gy", "gz")


def split_parts(value, count=PARTS):
    parts = []
    for _ in range(count):
        part = value.astype(BF16).astype(F32)
        parts.append(part)
        value = value - part
    return parts


def places(cell, across, along):
    layer = across * along
    if layer & (layer - 1) or along & (along - 1):
        return cell // layer, cell // along % across, cell % along
    shift = along.bit_length() - 1
    high = layer.bit_length() - 1
    return (
        lax.shift_right_logical(cell, high),
        lax.shift_right_logical(cell, shift) & (across - 1),
        cell & (along - 1),
    )


def parts_of(value):
    return jnp.concatenate([part.astype(BF16) for part in split_parts(value)], axis=1)


def spread_blocks(blocks):
    columns = []
    for block in blocks:
        rows = jnp.concatenate([block, block[7:8] * jnp.sqrt(block[6:7])], axis=0)
        parts = split_parts(rows, EXACT)
        parts.append(jnp.zeros((32 - 9 * EXACT, LANES), F32))
        columns.append(jnp.transpose(jnp.concatenate(parts, axis=0)).astype(BF16))
    lines = lax.broadcasted_iota(jnp.int32, (32, LANES), 0)
    picks = []
    for i in range(9):
        pick = lines == i
        for n in range(1, EXACT):
            pick = jnp.logical_or(pick, lines == i + 9 * n)
        picks.append(jnp.where(pick, 1.0, 0.0).astype(BF16))
    return jnp.dot(
        jnp.concatenate(columns, axis=0), jnp.concatenate(picks, axis=1), preferred_element_type=F32
    )


def pair_sum(left, spread, start, react):
    rows = [left[i : i + 1] for i in range(8)]
    rows.append((2.0 * damp_tangent) * rows[7] * jnp.sqrt(rows[6]))
    wide = [jnp.broadcast_to(row, (SUBLANES, LANES)) for row in rows]
    lanes = lax.broadcasted_iota(jnp.int32, (SUBLANES, LANES), 1)
    total = [None] * 3
    for tile in range(LANES // SUBLANES):
        place = pl.ds(pl.multiple_of(start + tile * SUBLANES, SUBLANES), SUBLANES)
        there = [spread[place, i * LANES : (i + 1) * LANES] for i in range(9)]
        ex, ey, ez, wx, wy, wz = [wide[i] - there[i] for i in range(6)]
        square = (ex * ex + ey * ey) + (ez * ez + soft_core)
        inverse = lax.rsqrt(square)
        reach = wide[6] + there[6]
        delta = jnp.maximum(reach - square * inverse, 0.0)
        mass = wide[7] + there[7]
        under = jnp.maximum((delta * reach) * (mass * mass), 1e-30)
        tangent = (wide[8] * there[8]) * (delta * lax.rsqrt(under))
        speed = ((wx * ex + wy * ey) + wz * ez) * inverse
        along = (
            (2.0 / 3.0 / damp_tangent) * delta - ((damp_normal - damp_tangent) / damp_tangent) * speed
        ) * (tangent * inverse)
        column = None
        for d, (e, w) in enumerate(((ex, wx), (ey, wy), (ez, wz))):
            force = along * e - tangent * w
            total[d] = force if total[d] is None else total[d] + force
            if react is not None:
                across_sum = jnp.broadcast_to(jnp.sum(force, axis=1, keepdims=True), (SUBLANES, LANES))
                column = across_sum if column is None else jnp.where(lanes == d, across_sum, column)
        if react is not None:
            react[tile * SUBLANES : (tile + 1) * SUBLANES, :] = column
    total = [jnp.sum(item, axis=0, keepdims=True) for item in total]
    if react is None:
        return total, None
    turned = jnp.transpose(react[...])
    return total, [-turned[d : d + 1] for d in range(3)]


def blob_layout(across, blocks, pairs):
    bodies = 3 * across
    cells = bodies + 8 * blocks
    shares = cells + blocks
    lists = shares + blocks
    rows = lists + 2 * pairs
    return bodies, cells, shares, lists, rows + -rows % 8


def parities():
    return [lax.rem(lax.axis_index(axis), 2) == 0 for axis in AXES]


def pack_kernel(counts, list_hbm, pair_hbm, part_hbm, cell_hbm, share_hbm, fluid_hbm, *refs):
    n_out = 2 + sum(counts)
    list_ref, fluid_ref = refs[:2]
    height_outs, across_outs, along_outs = by_axis(refs[2:n_out], counts)
    pair_ref, part_ref, cell_ref, share_ref, sems = refs[n_out:]
    depth, across, along = fluid_ref.shape[1:]
    blocks, pairs = part_ref.shape[0], pair_ref.shape[0]
    bodies, cells, shares, lists, rows = blob_layout(across, blocks, pairs)
    small = [(part_hbm, part_ref), (cell_hbm, cell_ref), (share_hbm, share_ref), (pair_hbm, pair_ref), (list_hbm, list_ref)]
    small = [pltpu.make_async_copy(source, target, sems.at[3 + n]) for n, (source, target) in enumerate(small)]
    copies = [pltpu.make_async_copy(fluid_hbm.at[c], fluid_ref.at[c], sems.at[c]) for c in range(3)]
    for copy in small + copies:
        copy.start()
    even = parities()
    for copy in small + copies:
        copy.wait()
    for out in height_outs:
        for b in range(blocks):
            out[bodies + 8 * b : bodies + 8 * b + 8, :] = part_ref[b]
        out[cells:shares, :] = cell_ref[...].astype(F32)
        out[shares:lists, :] = share_ref[...]
        for k in range(pairs):
            for side in range(2):
                row = lists + 2 * k + side
                out[row : row + 1, :] = jnp.full((1, LANES), pair_ref[k, side], jnp.int32).astype(F32)
        used = lists + 2 * pairs
        if used < rows:
            out[used:rows, :] = jnp.zeros((rows - used, LANES), F32)
    lanes = lax.broadcasted_iota(jnp.int32, (across, along), 1)
    first = jnp.zeros((across, along), F32)
    last = jnp.zeros((across, along), F32)
    for c in range(3):
        for n, out in enumerate(height_outs):
            upward = even[0] if n == 0 else jnp.logical_not(even[0])
            out[c * across : (c + 1) * across, :] = fluid_ref[c, jnp.where(upward, depth - 1, 0)]
        for h in range(depth):
            k = c * depth + h
            here = fluid_ref[c, h]
            for n, out in enumerate(across_outs):
                upward = even[1] if n == 0 else jnp.logical_not(even[1])
                out[k : k + 1, :] = jnp.where(upward, here[across - 1 : across], here[0:1])
            turned = pltpu.roll(here, 2 * k, 1) if k else here
            first = jnp.where(lanes == 2 * k, turned, first)
            last = jnp.where(lanes == (2 * k - 1) % along, turned, last)
    first = pltpu.roll(first, along - 1, 1)
    last = pltpu.roll(last, 1, 1)
    for n, out in enumerate(along_outs):
        upward = even[2] if n == 0 else jnp.logical_not(even[2])
        out[...] = jnp.where(upward, last, first)


def mark_cells(picks, spots, b, over, spot, half, wide):
    along = picks.shape[0] // PARTS
    sites = lax.broadcasted_iota(jnp.int32, (spots.shape[0], LANES), 0)
    one_hot = lane_one_hot(sites[:along], spot)
    for n in range(PARTS):
        picks[n * along : (n + 1) * along, b * LANES : (b + 1) * LANES] = one_hot
    one_hot = lane_one_hot(sites, jnp.where(over >= half, along, 0) + spot)
    for n in range(PARTS):
        spots[:, n * wide + b * LANES : n * wide + (b + 1) * LANES] = one_hot


def lane_one_hot(sites, target):
    return jnp.where(sites == target, 1.0, 0.0).astype(BF16)


def place_lines(ones, part, half):
    line = jnp.broadcast_to(part, (16, LANES)).astype(BF16)
    line = jnp.concatenate([line] * (half // 16), axis=0)
    return jnp.where(ones > 0, line, jnp.zeros_like(line))


def rim_kernel_part(blocks, pairs, half, fold, sent, height_ins, next_ref, scratch):
    spread, pieces, picks, seen_ref, coupled, spots = scratch
    depth, across, along = next_ref.shape[1:]
    wide = blocks * LANES
    bodies, cells, shares, lists, _ = blob_layout(across, blocks, pairs)
    even = parities()
    rows = lax.broadcasted_iota(jnp.int32, (across, LANES), 0)
    halves = lax.broadcasted_iota(jnp.int32, (half, LANES), 0)
    coupling = [[jnp.zeros((1, LANES), F32)] * blocks for _ in range(3)]
    meetings, partners = [], []
    for n, blob in enumerate(height_ins):
        own = sent[n]
        above = even[0] if n == 0 else jnp.logical_not(even[0])
        for k in range(pairs):
            ours = [own[lists + 2 * k + side : lists + 2 * k + side + 1, :] for side in range(2)]
            theirs = [blob[lists + 2 * k + side : lists + 2 * k + side + 1, :] for side in range(2)]
            to = jnp.where(above, ours[0], theirs[1])
            by = jnp.where(above, ours[1], theirs[0])
            left = own[bodies : bodies + 8, :]
            right = blob[bodies : bodies + 8, :]
            for b in range(1, blocks):
                body = slice(bodies + 8 * b, bodies + 8 * b + 8)
                left = jnp.where(to == b, own[body, :], left)
                right = jnp.where(by == b, blob[body, :], right)
            meetings.append((to, left))
            partners.append(right)
    spread[...] = spread_blocks(partners)
    for i, (to, left) in enumerate(meetings):
        force, _ = pair_sum(left, spread, i * LANES, None)
        for b in range(blocks):
            for c in range(3):
                coupling[c][b] += jnp.where(to == b, force[c], 0.0)
    for n, blob in enumerate(height_ins):
        own = sent[n]
        above = even[0] if n == 0 else jnp.logical_not(even[0])
        own_layer = jnp.where(above, depth - 1, 0)
        below = jnp.logical_not(above)
        for k in range(3):
            face = slice(k * across, (k + 1) * across)
            pieces[face, :] = parts_of(blob[face, :])
            pieces[(3 + k) * across : (4 + k) * across, :] = parts_of(own[face, :])
        lined = []
        for b in range(blocks):
            cell = jnp.where(above, own[cells + b : cells + b + 1, :], blob[cells + b : cells + b + 1, :])
            height, over, spot = places(cell.astype(jnp.int32), across, along)
            lined.append((height, over))
            mark_cells(picks, spots, b, over, spot, half, wide)
        seen_ref[...] = jnp.dot(pieces[...], picks[...], preferred_element_type=F32)
        for b in range(blocks):
            height, over = lined[b]
            share = jnp.where(above, own[shares + b : shares + b + 1, :], blob[shares + b : shares + b + 1, :])
            body = slice(bodies + 8 * b, bodies + 8 * b + 8)
            owner = jnp.where(above, own[body, :], blob[body, :])
            top = height == depth - 1
            mask = rows == over
            column = slice(b * LANES, (b + 1) * LANES)
            seen_share = jnp.where(top, jnp.where(above, share, 1.0 - share), 0.0)
            home_share = jnp.where(jnp.logical_and(top, below), share, 0.0)
            given_share = (-source_gain) * jnp.where(above, 1.0 - share, share)
            own_share = jnp.where(jnp.logical_and(top, below), 1.0, 0.0)
            ones = lane_one_hot(halves, jnp.where(over >= half, over - half, over))
            for c in range(3):
                seen = seen_ref[c * across : (c + 1) * across, column]
                home = seen_ref[(3 + c) * across : (4 + c) * across, column]
                met = jnp.where(mask, seen_share * seen + home_share * home, 0.0)
                met = jnp.sum(met, axis=0, keepdims=True)
                drag = drag_coef * owner[6:7] * (met - own_share * owner[3 + c : 4 + c])
                coupling[c][b] += jnp.where(above, drag, 0.0)
                for m, part in enumerate(split_parts(given_share * drag)):
                    coupled[c * half : (c + 1) * half, m * wide + b * LANES : m * wide + (b + 1) * LANES] = (
                        place_lines(ones, part, half)
                    )
        source = lax.dot_general(
            coupled[...], spots[...], (((1,), (1,)), ((), ())), preferred_element_type=F32
        )
        for c in range(3):
            given = [source[c * half : (c + 1) * half, f * along : (f + 1) * along] for f in range(fold)]
            next_ref[c, own_layer] += diffuse * blob[c * across : (c + 1) * across, :] + jnp.concatenate(given, axis=0)
    return coupling


def local_kernel(blocks, pairs, pair_ref, fluid_ref, *refs):
    count = (len(refs) - 18) // 2
    sent, height_ins = refs[:count], refs[count : 2 * count]
    force_ref, next_ref, source_ref = refs[2 * count : 2 * count + 3]
    spread, pieces, picks, spots, react, seen_ref, found, weights, coupled = refs[2 * count + 3 : 2 * count + 12]
    rim_refs = refs[2 * count + 12 :]
    blob_ref = sent[0]
    depth, across, along = fluid_ref.shape[1:]
    listed = pair_ref.shape[1]
    fold = spots.shape[0] // along
    half = across // fold
    wide = blocks * LANES
    bodies, cells, shares, _, _ = blob_layout(across, blocks, pairs)
    rows = lax.broadcasted_iota(jnp.int32, (across, LANES), 0)
    halves = lax.broadcasted_iota(jnp.int32, (half, LANES), 0)
    subs = lax.broadcasted_iota(jnp.int32, (SUBLANES, along), 0)
    slabs = [(c, h) for c in range(3) for h in range(depth)]

    def body_of(b):
        return blob_ref[bodies + 8 * b : bodies + 8 * b + 8, :]

    def spot_of(b):
        return places(blob_ref[cells + b : cells + b + 1, :].astype(jnp.int32), across, along)

    def stencil(c, h):
        for t in range(across // SUBLANES):
            at = t * SUBLANES
            here = fluid_ref[c, h, at : at + SUBLANES, :]
            if t > 0:
                beside = fluid_ref[c, h, at - 1 : at + SUBLANES - 1, :]
            else:
                beside = jnp.where(subs == 0, 0.0, pltpu.roll(here, 1, 0))
            if at + SUBLANES < across:
                beside += fluid_ref[c, h, at + 1 : at + SUBLANES + 1, :]
            else:
                beside += jnp.where(subs == SUBLANES - 1, 0.0, pltpu.roll(here, SUBLANES - 1, 0))
            line = (c * depth + h) * across + at
            beside += seen_ref[line : line + SUBLANES, wide : wide + along]
            if h > 0:
                beside += fluid_ref[c, h - 1, at : at + SUBLANES, :]
            if h < depth - 1:
                beside += fluid_ref[c, h + 1, at : at + SUBLANES, :]
            next_ref[c, h, at : at + SUBLANES, :] = (1.0 - 6.0 * diffuse) * here + diffuse * beside

    spread[...] = spread_blocks([body_of(b) for b in range(blocks)])
    for k, (c, h) in enumerate(slabs):
        pieces[k * across : (k + 1) * across, :] = parts_of(fluid_ref[c, h])
    for b in range(blocks):
        _, over, spot = spot_of(b)
        mark_cells(picks, spots, b, over, spot, half, wide)
    here = lax.broadcasted_iota(jnp.int32, (along, along), 0)
    there = lax.broadcasted_iota(jnp.int32, (along, along), 1)
    near = jnp.where(jnp.abs(here - there) == 1, 1.0, 0.0).astype(BF16)
    for n in range(PARTS):
        picks[n * along : (n + 1) * along, wide : wide + along] = near
    seen_ref[...] = jnp.dot(pieces[...], picks[...], preferred_element_type=F32)

    turns = blocks + listed
    share_out = [slabs[i * len(slabs) // turns : (i + 1) * len(slabs) // turns] for i in range(turns)]
    for b in range(blocks):
        for c, h in share_out[b]:
            stencil(c, h)
        force, _ = pair_sum(body_of(b), spread, b * LANES, None)
        for c in range(3):
            force_ref[c, b : b + 1, :] = force[c]

    for b in range(blocks):
        height, over, _ = spot_of(b)
        share = blob_ref[shares + b : shares + b + 1, :]
        mask = rows == over
        column = slice(b * LANES, (b + 1) * LANES)
        near = [
            jnp.where(height == h, 1.0 - share, jnp.where(height == h - 1, share, 0.0)) for h in range(depth)
        ]
        for c in range(3):
            total = jnp.zeros((SUBLANES, LANES), F32)
            for h in range(depth):
                k = c * depth + h
                seen = jnp.where(mask, seen_ref[k * across : (k + 1) * across, column], 0.0)
                total += near[h] * jnp.sum(seen.reshape(across // SUBLANES, SUBLANES, LANES), axis=0)
            met = jnp.sum(total, axis=0, keepdims=True)
            drag = drag_coef * blob_ref[bodies + 8 * b + 6 : bodies + 8 * b + 7, :] * (
                met - blob_ref[bodies + 8 * b + 3 + c : bodies + 8 * b + 4 + c, :]
            )
            force_ref[c, b : b + 1, :] += drag
            for h in range(depth):
                weights[c * depth + h : c * depth + h + 1, column] = (-source_gain) * near[h] * drag
        ones = lane_one_hot(halves, jnp.where(over >= half, over - half, over))
        for n, part in enumerate(split_parts(weights[:, column])):
            for k in range(3 * depth):
                coupled[k * half : (k + 1) * half, n * wide + b * LANES : n * wide + (b + 1) * LANES] = place_lines(
                    ones, part[k : k + 1], half
                )
    for c in range(3):
        face = slice(c * depth * half, (c + 1) * depth * half)
        source_ref[face, :] = lax.dot_general(
            coupled[face, :], spots[...], (((1,), (1,)), ((), ())), preferred_element_type=F32
        )

    for i in range(listed):
        for c, h in share_out[blocks + i]:
            stencil(c, h)
        a, c = pair_ref[0, i], pair_ref[1, i]
        left = blob_ref[pl.ds(pl.multiple_of(bodies + 8 * a, 8), 8), :]
        ahead, behind = pair_sum(left, spread, c * LANES, react.at[i])
        for side, forces in enumerate((ahead, behind)):
            for d in range(3):
                found[2 * i + side, d : d + 1, :] = forces[d]
    coupling = rim_kernel_part(blocks, pairs, half, fold, sent, height_ins, next_ref, rim_refs)
    for b in range(blocks):
        for d in range(3):
            total = force_ref[d, b : b + 1, :]
            for i in range(listed):
                for side in range(2):
                    total += jnp.where(pair_ref[side, i] == b, found[2 * i + side, d : d + 1, :], 0.0)
            force_ref[d, b : b + 1, :] = total + coupling[d][b]


def finish_kernel(counts, sizes, partial_ref, source_ref, *refs):
    n_in = sum(counts[1:])
    across_ins, along_ins = by_axis(refs[:n_in], counts[1:])
    next_hbm, next_ref, sems = refs[n_in:]
    depth, across, along = partial_ref.shape[1:]
    fold = source_ref.shape[1] // along
    half = across // fold
    even = parities()

    def second_of(arrived, axis):
        second = arrived[1][...]
        if sizes[axis] % 2:
            return second
        place = lax.axis_index(AXES[axis])
        inside = jnp.logical_and(place > 0, place < sizes[axis] - 1)
        return jnp.where(inside, second, 0.0)

    def ordered(arrived, axis):
        first = arrived[0][...]
        if len(arrived) == 1:
            return jnp.where(even[axis], 0.0, first), jnp.where(even[axis], first, 0.0)
        second = second_of(arrived, axis)
        return jnp.where(even[axis], second, first), jnp.where(even[axis], first, second)

    across_low, across_high = ordered(across_ins, 1)
    across_low = diffuse * across_low
    across_high = diffuse * across_high
    edges = along_ins[0][...]
    if len(along_ins) > 1:
        edges = edges + second_of(along_ins, 2)
    edges = diffuse * edges
    lanes = lax.broadcasted_iota(jnp.int32, (across, along), 1)
    subs = lax.broadcasted_iota(jnp.int32, (SUBLANES, along), 0)
    tail = across - SUBLANES
    rim = jnp.logical_or(lanes == 0, lanes == along - 1)
    copies = []
    for c in range(3):
        for h in range(depth):
            k = c * depth + h
            given = [
                source_ref[k * half : (k + 1) * half, f * along : (f + 1) * along] for f in range(fold)
            ]
            value = partial_ref[c, h] + jnp.concatenate(given, axis=0)
            value += jnp.where(rim, pltpu.roll(edges, (along - 2 * k) % along, 1) if k else edges, 0.0)
            next_ref[c, h] = value
            next_ref[c, h, :SUBLANES, :] += jnp.where(subs == 0, across_low[k : k + 1, :], 0.0)
            next_ref[c, h, tail:, :] += jnp.where(subs == SUBLANES - 1, across_high[k : k + 1, :], 0.0)
        copies.append(pltpu.make_async_copy(next_ref.at[c], next_hbm.at[c], sems.at[c]))
        copies[-1].start()
    for copy in copies:
        copy.wait()


def by_axis(refs, counts):
    groups, at = [], 0
    for n in counts:
        groups.append(refs[at : at + n])
        at += n
    return groups


def exchange(payloads, axis, closed):
    count = lax.axis_size(axis)
    results = []
    for n, payload in enumerate(payloads):
        route = []
        for i in range(n, count - 1, 2):
            route += [(i, i + 1), (i + 1, i)]
        if closed and n == 1 and count % 2 == 0:
            route += [(0, count - 1), (count - 1, 0)]
        results.append(lax.ppermute(payload, axis, route))
    return results


def body(particles, local_pairs, cross_pairs, drag_cell, drag_share, fluid):
    blocks = particles.shape[0]
    pairs = cross_pairs.shape[0]
    listed = local_pairs.shape[0]
    _, depth, across, along = fluid.shape
    counts = [min(2, lax.axis_size(axis) - 1) for axis in AXES]
    fold = 2 if across % 32 == 0 else 1
    half = across // fold
    wide = PARTS * blocks * LANES
    rows = blob_layout(across, blocks, pairs)[-1]
    shapes = [(rows, along), (3 * depth, along), (across, along)]
    vmem = pl.BlockSpec(memory_space=pltpu.VMEM)
    hbm = pl.BlockSpec(memory_space=pltpu.HBM)
    smem = pl.BlockSpec(memory_space=pltpu.SMEM)

    def kept(value):
        return pltpu.with_memory_space_constraint(value, pltpu.VMEM)

    listing, fluid_kept, *packed = pl.pallas_call(
        functools.partial(pack_kernel, counts),
        out_shape=[
            pltpu.SMEM((2, listed), jnp.int32),
            pltpu.VMEM(fluid.shape, F32),
        ]
        + [pltpu.VMEM(shape, F32) for shape, n in zip(shapes, counts) for _ in range(n)],
        in_specs=[hbm] * 6,
        out_specs=[smem] + [vmem] * (1 + sum(counts)),
        scratch_shapes=[
            pltpu.SMEM(cross_pairs.shape, jnp.int32),
            pltpu.VMEM(particles.shape, F32),
            pltpu.VMEM(drag_cell.shape, jnp.int32),
            pltpu.VMEM(drag_share.shape, F32),
            pltpu.SemaphoreType.DMA((8,)),
        ],
        compiler_params=pltpu.CompilerParams(vmem_limit_bytes=GRANT),
        name="pack",
    )(
        *[
            pltpu.with_memory_space_constraint(value, pltpu.HBM)
            for value in (local_pairs.T, cross_pairs, particles, drag_cell, drag_share, fluid)
        ]
    )
    received = []
    for axis, payloads in zip(AXES, by_axis(packed, counts)):
        received += exchange(payloads, axis, axis != AXES[0])

    height_count = counts[0]
    out_force, partial, source = pl.pallas_call(
        functools.partial(local_kernel, blocks, pairs),
        out_shape=[
            jax.ShapeDtypeStruct((3, blocks, LANES), F32),
            pltpu.VMEM(fluid.shape, F32),
            pltpu.VMEM((3 * depth * half, fold * along), F32),
        ],
        in_specs=[smem] + [vmem] * (1 + 2 * height_count),
        out_specs=[vmem] * 3,
        scratch_shapes=[
            pltpu.VMEM((blocks * LANES, 9 * LANES), F32),
            pltpu.VMEM((3 * depth * across, PARTS * along), BF16),
            pltpu.VMEM((PARTS * along, blocks * LANES + along), BF16),
            pltpu.VMEM((fold * along, wide), BF16),
            pltpu.VMEM((listed, LANES, LANES), F32),
            pltpu.VMEM((3 * depth * across, blocks * LANES + along), F32),
            pltpu.VMEM((2 * listed, SUBLANES, LANES), F32),
            pltpu.VMEM((3 * depth, blocks * LANES), F32),
            pltpu.VMEM((3 * depth * half, wide), BF16),
            pltpu.VMEM((height_count * pairs * LANES, 9 * LANES), F32),
            pltpu.VMEM((6 * across, PARTS * along), BF16),
            pltpu.VMEM((PARTS * along, blocks * LANES), BF16),
            pltpu.VMEM((6 * across, blocks * LANES), F32),
            pltpu.VMEM((3 * half, wide), BF16),
            pltpu.VMEM((fold * along, wide), BF16),
        ],
        compiler_params=pltpu.CompilerParams(vmem_limit_bytes=GRANT),
        name="local",
    )(
        pltpu.with_memory_space_constraint(listing, pltpu.SMEM),
        *[kept(value) for value in (fluid_kept, *packed[:height_count], *received[:height_count])],
    )

    rest = received[height_count:]
    out_next = pl.pallas_call(
        functools.partial(finish_kernel, counts, [lax.axis_size(axis) for axis in AXES]),
        out_shape=jax.ShapeDtypeStruct(fluid.shape, F32),
        in_specs=[vmem] * (2 + len(rest)),
        out_specs=hbm,
        scratch_shapes=[pltpu.VMEM(fluid.shape, F32), pltpu.SemaphoreType.DMA((3,))],
        compiler_params=pltpu.CompilerParams(vmem_limit_bytes=GRANT),
        name="finish",
    )(*[kept(value) for value in [partial, source, *rest]])
    return jnp.transpose(out_force, (1, 0, 2)), out_next


def solution(mesh):
    in_specs = (
        P(("gx", "gy", "gz"), None, None),
        P(("gx", "gy", "gz"), None),
        P(("gx", "gy", "gz"), None),
        P(("gx", "gy", "gz"), None),
        P(("gx", "gy", "gz"), None),
        P(None, "gx", "gy", "gz"),
    )
    out_specs = (P(("gx", "gy", "gz"), None, None), P(None, "gx", "gy", "gz"))
    return jax.shard_map(body, mesh=mesh, in_specs=in_specs, out_specs=out_specs, check_vma=False)
```

time: 18.3 us -> 16.3 us (0.89)
  the two profiles are of different devices: /device:TPU:12 before, /device:TPU:0 now
where the time goes in v8:
time: 16.3 us; the launch traced here: 16.1 us
  starting transfers between devices  8.65 us (53%)
  Pallas kernels  6.77 us (42%)
  between operations  0.66 us (4%)
    ppermute x5, starting transfers between devices, exchange(): results.append(lax.ppermute(payload, axis, route))  8.65 us
    pallas_call x1, Pallas kernels, body(): pl.pallas_call(functools.partial(local_kernel, blocks, pairs), out_shape=...  4.15 us
    pallas_call x1, Pallas kernels, body(): pl.pallas_call(functools.partial(pack_kernel, counts), out_shape=[pltpu.S...  1.58 us
    pallas_call x1, Pallas kernels, body(): pl.pallas_call(functools.partial(finish_kernel, counts, [lax.axis_size(ax...  1.05 us
  transfers between devices with their start and end apart: 5, of which 0 were waited for; matrix products, arithmetic and copies ran while one was open for 0% of the time, Pallas kernels for 26%

profile of v8, /device:TPU:0, one launch (start us, length us, event | category | flops | bytes accessed | tf_op | source)
XLA Modules:
  0.0 16.1 jit_solution(7199649506516499526)
XLA Ops:
  0.6 1.6 %pack.1 = (s32[2,4]{1,0:T(2,128)S(4)}, f32[3,8,64,128]{3,2,1,0:T(8,128)S(1)}, f32[240,128]{1,0:T(8,128)S(1)}, f32[24,128]{1,0:T(8,128)S(1)}, f32[24,128]{1,0:T(8...) custom-call(s32[2,4]{1,0:T(2,128)} %bitcast.2, s32[2,2]{1,0:T(2,128)} %pair_hbm.1, f32[4,8,128]{2,1,0:T(8,128)} %part_hbm.1, ...), custom_call_target="tpu_custom_call" | custom-call | tf_op jit(solution)/shard_map/pack/pallas_call | solution.py:486
  2.2 0.6 %collective-permute-start = (f32[240,128]{1,0:T(8,128)S(1)}, f32[240,128]{1,0:T(8,128)S(1)}, u32[]{:S(2)}, u32[]{:S(2)}) collective-permute-start(f32[240,128]{1,0:T(8,128)S(1)} %get-tuple-element.14.refs_0_), channel_id=1, source_target_pairs={{0,16},{16,0},{1,17},{17,1},{2,18},{18,2},{3,19},{19,3},{4,20},{20... | collective-permute-start | bytes 368648 | tf_op jit(solution)/shard_map/ppermute | solution.py:464
  2.8 2.6 %collective-permute-start.3 = (f32[64,128]{1,0:T(8,128)S(1)}, f32[64,128]{1,0:T(8,128)S(1)}, u32[]{:S(2)}, u32[]{:S(2)}) collective-permute-start(f32[64,128]{1,0:T(8,128)S(1)} %get-tuple-element.20), channel_id=1, source_target_pairs={{0,1},{1,0},{2,3},{3,2},{4,5},{5,4},{6,7},{7,6},{8,9},{9,8},{10,11... | collective-permute-start | bytes 98312 | tf_op jit(solution)/shard_map/ppermute | solution.py:464
  5.4 2.5 %collective-permute-start.4 = (f32[64,128]{1,0:T(8,128)S(1)}, f32[64,128]{1,0:T(8,128)S(1)}, u32[]{:S(2)}, u32[]{:S(2)}) collective-permute-start(f32[64,128]{1,0:T(8,128)S(1)} %get-tuple-element.21), channel_id=1, source_target_pairs={{1,2},{2,1},{0,3},{3,0},{5,6},{6,5},{4,7},{7,4},{9,10},{10,9},{8,1... | collective-permute-start | bytes 98312 | tf_op jit(solution)/shard_map/ppermute | solution.py:464
  7.9 1.5 %collective-permute-start.1 = (f32[24,128]{1,0:T(8,128)S(1)}, f32[24,128]{1,0:T(8,128)S(1)}, u32[]{:S(2)}, u32[]{:S(2)}) collective-permute-start(f32[24,128]{1,0:T(8,128)S(1)} %get-tuple-element.18), channel_id=1, source_target_pairs={{0,4},{4,0},{8,12},{12,8},{1,5},{5,1},{9,13},{13,9},{2,6},{6,2},{1... | collective-permute-start | bytes 36872 | tf_op jit(solution)/shard_map/ppermute | solution.py:464
  9.4 1.5 %collective-permute-start.2 = (f32[24,128]{1,0:T(8,128)S(1)}, f32[24,128]{1,0:T(8,128)S(1)}, u32[]{:S(2)}, u32[]{:S(2)}) collective-permute-start(f32[24,128]{1,0:T(8,128)S(1)} %get-tuple-element.19), channel_id=1, source_target_pairs={{4,8},{8,4},{0,12},{12,0},{5,9},{9,5},{1,13},{13,1},{6,10},{10,6},... | collective-permute-start | bytes 36872 | tf_op jit(solution)/shard_map/ppermute | solution.py:464
  10.9 0.0 collective-permute-done.refs_1_
  10.9 4.2 %local.1 = (f32[3,4,128]{2,1,0:T(4,128)}, f32[3,8,64,128]{3,2,1,0:T(8,128)S(1)}, f32[768,256]{1,0:T(8,128)S(1)}) custom-call(s32[2,4]{1,0:T(2,128)S(4)} %get-tuple-element.12.pair_ref, f32[3,8,64,128]{3,2,1,0:T(8,128)S(1)} %get-tuple-element.13.fluid_ref, f32[240,128]{1,0:T(8,128)S(1)} %get-tuple-element.14.refs_0_, f32[240,128]{1,0:T(8,128)S(1)} %collective-permute-done.refs_1_), custom_call_target="tpu_custom_call" | custom-call | tf_op jit(solution)/shard_map/local/pallas_call | solution.py:515
  15.0 0.0 collective-permute-done.1.refs_0_
  15.0 0.0 collective-permute-done.2.refs_1_
  15.0 0.0 collective-permute-done.3.refs_2_
  15.0 0.0 collective-permute-done.4.refs_3_
  15.0 1.0 %finish.1 = f32[3,8,64,128]{3,2,1,0:T(8,128)} custom-call(f32[3,8,64,128]{3,2,1,0:T(8,128)S(1)} %get-tuple-element.16.partial_ref, f32[768,256]{1,0:T(8,128)S(1)} %get-tuple-element.17.source_ref, f32[24,128]{1,0:T(8,128)S(1)} %collective-permute-done.1.refs_0_, f32[24,128]{1,0:T(8,128)S(1)} %collective-permute-done.2.refs_1_, ...), custom_call_target="tpu_custom_call" | custom-call | tf_op jit(solution)/shard_map/finish/pallas_call | solution.py:549
Async XLA Ops:
  2.2 8.7 %collective-permute-start = (f32[240,128]{1,0:T(8,128)S(1)}, f32[240,128]{1,0:T(8,128)S(1)}, u32[]{:S(2)}, u32[]{:S(2)}) collective-permute-start(f32[240,128]{1,0:T(8,128)S(1)} %get-tuple-element.14.refs_0_), channel_id=1, source_target_pairs={{0,16},{16,0},{1,17},{17,1},{2,18},{18,2},{3,19},{19,3},{4,20},{20... | collective-permute-start | bytes 368648 | tf_op jit(solution)/shard_map/ppermute | solution.py:464
  2.8 12.3 %collective-permute-start.3 = (f32[64,128]{1,0:T(8,128)S(1)}, f32[64,128]{1,0:T(8,128)S(1)}, u32[]{:S(2)}, u32[]{:S(2)}) collective-permute-start(f32[64,128]{1,0:T(8,128)S(1)} %get-tuple-element.20), channel_id=1, source_target_pairs={{0,1},{1,0},{2,3},{3,2},{4,5},{5,4},{6,7},{7,6},{8,9},{9,8},{10,11... | collective-permute-start | bytes 98312 | tf_op jit(solution)/shard_map/ppermute | solution.py:464
  5.4 9.6 %collective-permute-start.4 = (f32[64,128]{1,0:T(8,128)S(1)}, f32[64,128]{1,0:T(8,128)S(1)}, u32[]{:S(2)}, u32[]{:S(2)}) collective-permute-start(f32[64,128]{1,0:T(8,128)S(1)} %get-tuple-element.21), channel_id=1, source_target_pairs={{1,2},{2,1},{0,3},{3,0},{5,6},{6,5},{4,7},{7,4},{9,10},{10,9},{8,1... | collective-permute-start | bytes 98312 | tf_op jit(solution)/shard_map/ppermute | solution.py:464
  7.9 7.1 %collective-permute-start.1 = (f32[24,128]{1,0:T(8,128)S(1)}, f32[24,128]{1,0:T(8,128)S(1)}, u32[]{:S(2)}, u32[]{:S(2)}) collective-permute-start(f32[24,128]{1,0:T(8,128)S(1)} %get-tuple-element.18), channel_id=1, source_target_pairs={{0,4},{4,0},{8,12},{12,8},{1,5},{5,1},{9,13},{13,9},{2,6},{6,2},{1... | collective-permute-start | bytes 36872 | tf_op jit(solution)/shard_map/ppermute | solution.py:464
  9.4 5.7 %collective-permute-start.2 = (f32[24,128]{1,0:T(8,128)S(1)}, f32[24,128]{1,0:T(8,128)S(1)}, u32[]{:S(2)}, u32[]{:S(2)}) collective-permute-start(f32[24,128]{1,0:T(8,128)S(1)} %get-tuple-element.19), channel_id=1, source_target_pairs={{4,8},{8,4},{0,12},{12,0},{5,9},{9,5},{1,13},{13,1},{6,10},{10,6},... | collective-permute-start | bytes 36872 | tf_op jit(solution)/shard_map/ppermute | solution.py:464

commit v9 on v8

--- a/solution.py
+++ b/solution.py
@@ -391,10 +391,12 @@
             force_ref[d, b : b + 1, :] = total + coupling[d][b]
 
 
-def finish_kernel(counts, sizes, partial_ref, source_ref, *refs):
+def finish_kernel(counts, sizes, force_ref, partial_ref, source_ref, *refs):
     n_in = sum(counts[1:])
     across_ins, along_ins = by_axis(refs[:n_in], counts[1:])
-    next_hbm, next_ref, sems = refs[n_in:]
+    force_hbm, next_hbm, next_ref, sems = refs[n_in:]
+    copies = [pltpu.make_async_copy(force_ref, force_hbm, sems.at[3])]
+    copies[0].start()
     depth, across, along = partial_ref.shape[1:]
     fold = source_ref.shape[1] // along
     half = across // fold
@@ -426,7 +428,6 @@
     subs = lax.broadcasted_iota(jnp.int32, (SUBLANES, along), 0)
     tail = across - SUBLANES
     rim = jnp.logical_or(lanes == 0, lanes == along - 1)
-    copies = []
     for c in range(3):
         for h in range(depth):
             k = c * depth + h
@@ -512,10 +513,10 @@
         received += exchange(payloads, axis, axis != AXES[0])
 
     height_count = counts[0]
-    out_force, partial, source = pl.pallas_call(
+    force, partial, source = pl.pallas_call(
         functools.partial(local_kernel, blocks, pairs),
         out_shape=[
-            jax.ShapeDtypeStruct((3, blocks, LANES), F32),
+            pltpu.VMEM((3, blocks, LANES), F32),
             pltpu.VMEM(fluid.shape, F32),
             pltpu.VMEM((3 * depth * half, fold * along), F32),
         ],
@@ -546,15 +547,18 @@
     )
 
     rest = received[height_count:]
-    out_next = pl.pallas_call(
+    out_force, out_next = pl.pallas_call(
         functools.partial(finish_kernel, counts, [lax.axis_size(axis) for axis in AXES]),
-        out_shape=jax.ShapeDtypeStruct(fluid.shape, F32),
-        in_specs=[vmem] * (2 + len(rest)),
-        out_specs=hbm,
-        scratch_shapes=[pltpu.VMEM(fluid.shape, F32), pltpu.SemaphoreType.DMA((3,))],
+        out_shape=[
+            jax.ShapeDtypeStruct((3, blocks, LANES), F32),
+            jax.ShapeDtypeStruct(fluid.shape, F32),
+        ],
+        in_specs=[vmem] * (3 + len(rest)),
+        out_specs=[hbm, hbm],
+        scratch_shapes=[pltpu.VMEM(fluid.shape, F32), pltpu.SemaphoreType.DMA((4,))],
         compiler_params=pltpu.CompilerParams(vmem_limit_bytes=GRANT),
         name="finish",
-    )(*[kept(value) for value in [partial, source, *rest]])
+    )(*[kept(value) for value in [force, partial, source, *rest]])
     return jnp.transpose(out_force, (1, 0, 2)), out_next
 
 

time: 16.3 us -> 16 us (0.982)
  Pallas kernels: 6.77 us -> 6.4 us
    pallas_call x1, Pallas kernels: 4.15 us -> 3.76 us  [body(): pl.pallas_call(functools.partial(local_kernel, blocks, pairs), out_shape=...]
  transfers between devices with their start and end apart: 5 -> 5, of which waited for: 0 -> 0; matrix products, arithmetic and copies ran while one was open for 0% -> 0% of each run, Pallas kernels for 26% -> 24%
where the time goes in v9:
time: 16 us; the launch traced here: 15.7 us
  starting transfers between devices  8.65 us (54%)
  Pallas kernels  6.4 us (40%)
  between operations  0.68 us (4%)
    ppermute x5, starting transfers between devices, exchange(): results.append(lax.ppermute(payload, axis, route))  8.65 us
    pallas_call x1, Pallas kernels, body(): pl.pallas_call(functools.partial(local_kernel, blocks, pairs), out_shape=...  3.76 us
    pallas_call x1, Pallas kernels, body(): pl.pallas_call(functools.partial(pack_kernel, counts), out_shape=[pltpu.S...  1.58 us
    pallas_call x1, Pallas kernels, body(): pl.pallas_call(functools.partial(finish_kernel, counts, [lax.axis_size(ax...  1.06 us
  transfers between devices with their start and end apart: 5, of which 0 were waited for; matrix products, arithmetic and copies ran while one was open for 0% of the time, Pallas kernels for 24%

profile of v9, /device:TPU:0, one launch (start us, length us, event | category | flops | bytes accessed | tf_op | source)
XLA Modules:
  0.0 15.7 jit_solution(3248806203490075423)
XLA Ops:
  0.6 1.6 %pack.1 = (s32[2,4]{1,0:T(2,128)S(4)}, f32[3,8,64,128]{3,2,1,0:T(8,128)S(1)}, f32[240,128]{1,0:T(8,128)S(1)}, f32[24,128]{1,0:T(8,128)S(1)}, f32[24,128]{1,0:T(8...) custom-call(s32[2,4]{1,0:T(2,128)} %bitcast.2, s32[2,2]{1,0:T(2,128)} %pair_hbm.1, f32[4,8,128]{2,1,0:T(8,128)} %part_hbm.1, ...), custom_call_target="tpu_custom_call" | custom-call | tf_op jit(solution)/shard_map/pack/pallas_call | solution.py:487
  2.2 0.6 %collective-permute-start = (f32[240,128]{1,0:T(8,128)S(1)}, f32[240,128]{1,0:T(8,128)S(1)}, u32[]{:S(2)}, u32[]{:S(2)}) collective-permute-start(f32[240,128]{1,0:T(8,128)S(1)} %get-tuple-element.16.refs_0_), channel_id=1, source_target_pairs={{0,16},{16,0},{1,17},{17,1},{2,18},{18,2},{3,19},{19,3},{4,20},{20... | collective-permute-start | bytes 368648 | tf_op jit(solution)/shard_map/ppermute | solution.py:465
  2.8 2.6 %collective-permute-start.3 = (f32[64,128]{1,0:T(8,128)S(1)}, f32[64,128]{1,0:T(8,128)S(1)}, u32[]{:S(2)}, u32[]{:S(2)}) collective-permute-start(f32[64,128]{1,0:T(8,128)S(1)} %get-tuple-element.22), channel_id=1, source_target_pairs={{0,1},{1,0},{2,3},{3,2},{4,5},{5,4},{6,7},{7,6},{8,9},{9,8},{10,11... | collective-permute-start | bytes 98312 | tf_op jit(solution)/shard_map/ppermute | solution.py:465
  5.4 2.5 %collective-permute-start.4 = (f32[64,128]{1,0:T(8,128)S(1)}, f32[64,128]{1,0:T(8,128)S(1)}, u32[]{:S(2)}, u32[]{:S(2)}) collective-permute-start(f32[64,128]{1,0:T(8,128)S(1)} %get-tuple-element.23), channel_id=1, source_target_pairs={{1,2},{2,1},{0,3},{3,0},{5,6},{6,5},{4,7},{7,4},{9,10},{10,9},{8,1... | collective-permute-start | bytes 98312 | tf_op jit(solution)/shard_map/ppermute | solution.py:465
  7.9 1.5 %collective-permute-start.1 = (f32[24,128]{1,0:T(8,128)S(1)}, f32[24,128]{1,0:T(8,128)S(1)}, u32[]{:S(2)}, u32[]{:S(2)}) collective-permute-start(f32[24,128]{1,0:T(8,128)S(1)} %get-tuple-element.20), channel_id=1, source_target_pairs={{0,4},{4,0},{8,12},{12,8},{1,5},{5,1},{9,13},{13,9},{2,6},{6,2},{1... | collective-permute-start | bytes 36872 | tf_op jit(solution)/shard_map/ppermute | solution.py:465
  9.4 1.5 %collective-permute-start.2 = (f32[24,128]{1,0:T(8,128)S(1)}, f32[24,128]{1,0:T(8,128)S(1)}, u32[]{:S(2)}, u32[]{:S(2)}) collective-permute-start(f32[24,128]{1,0:T(8,128)S(1)} %get-tuple-element.21), channel_id=1, source_target_pairs={{4,8},{8,4},{0,12},{12,0},{5,9},{9,5},{1,13},{13,1},{6,10},{10,6},... | collective-permute-start | bytes 36872 | tf_op jit(solution)/shard_map/ppermute | solution.py:465
  10.9 0.0 collective-permute-done.refs_1_
  10.9 3.8 %local.1 = (f32[3,4,128]{2,1,0:T(4,128)S(1)}, f32[3,8,64,128]{3,2,1,0:T(8,128)S(1)}, f32[768,256]{1,0:T(8,128)S(1)}) custom-call(s32[2,4]{1,0:T(2,128)S(4)} %get-tuple-element.14.pair_ref, f32[3,8,64,128]{3,2,1,0:T(8,128)S(1)} %get-tuple-element.15.fluid_ref, f32[240,128]{1,0:T(8,128)S(1)} %get-tuple-element.16.refs_0_, ...), custom_call_target="tpu_custom_call" | custom-call | tf_op jit(solution)/shard_map/local/pallas_call | solution.py:516
  14.6 0.0 collective-permute-done.1.refs_0_
  14.7 0.0 collective-permute-done.2.refs_1_
  14.7 0.0 collective-permute-done.3.refs_2_
  14.7 0.0 collective-permute-done.4.refs_3_
  14.7 1.1 %finish.1 = (f32[3,4,128]{2,1,0:T(4,128)}, f32[3,8,64,128]{3,2,1,0:T(8,128)}) custom-call(f32[3,4,128]{2,1,0:T(4,128)S(1)} %get-tuple-element.17.force_ref, f32[3,8,64,128]{3,2,1,0:T(8,128)S(1)} %get-tuple-element.18.partial_ref, f32[768,256]{1,0:T(8,128)S(1)} %get-tuple-element.19.source_ref, f32[24,128]{1,0:T(8,128)S(1)} %collective-permute-done.1.refs_0_, ...), custom_call_target="tpu_custom_call" | custom-call | tf_op jit(solution)/shard_map/finish/pallas_call | solution.py:550
Async XLA Ops:
  2.2 8.7 %collective-permute-start = (f32[240,128]{1,0:T(8,128)S(1)}, f32[240,128]{1,0:T(8,128)S(1)}, u32[]{:S(2)}, u32[]{:S(2)}) collective-permute-start(f32[240,128]{1,0:T(8,128)S(1)} %get-tuple-element.16.refs_0_), channel_id=1, source_target_pairs={{0,16},{16,0},{1,17},{17,1},{2,18},{18,2},{3,19},{19,3},{4,20},{20... | collective-permute-start | bytes 368648 | tf_op jit(solution)/shard_map/ppermute | solution.py:465
  2.8 11.9 %collective-permute-start.3 = (f32[64,128]{1,0:T(8,128)S(1)}, f32[64,128]{1,0:T(8,128)S(1)}, u32[]{:S(2)}, u32[]{:S(2)}) collective-permute-start(f32[64,128]{1,0:T(8,128)S(1)} %get-tuple-element.22), channel_id=1, source_target_pairs={{0,1},{1,0},{2,3},{3,2},{4,5},{5,4},{6,7},{7,6},{8,9},{9,8},{10,11... | collective-permute-start | bytes 98312 | tf_op jit(solution)/shard_map/ppermute | solution.py:465
  5.4 9.3 %collective-permute-start.4 = (f32[64,128]{1,0:T(8,128)S(1)}, f32[64,128]{1,0:T(8,128)S(1)}, u32[]{:S(2)}, u32[]{:S(2)}) collective-permute-start(f32[64,128]{1,0:T(8,128)S(1)} %get-tuple-element.23), channel_id=1, source_target_pairs={{1,2},{2,1},{0,3},{3,0},{5,6},{6,5},{4,7},{7,4},{9,10},{10,9},{8,1... | collective-permute-start | bytes 98312 | tf_op jit(solution)/shard_map/ppermute | solution.py:465
  7.9 6.8 %collective-permute-start.1 = (f32[24,128]{1,0:T(8,128)S(1)}, f32[24,128]{1,0:T(8,128)S(1)}, u32[]{:S(2)}, u32[]{:S(2)}) collective-permute-start(f32[24,128]{1,0:T(8,128)S(1)} %get-tuple-element.20), channel_id=1, source_target_pairs={{0,4},{4,0},{8,12},{12,8},{1,5},{5,1},{9,13},{13,9},{2,6},{6,2},{1... | collective-permute-start | bytes 36872 | tf_op jit(solution)/shard_map/ppermute | solution.py:465
  9.4 5.3 %collective-permute-start.2 = (f32[24,128]{1,0:T(8,128)S(1)}, f32[24,128]{1,0:T(8,128)S(1)}, u32[]{:S(2)}, u32[]{:S(2)}) collective-permute-start(f32[24,128]{1,0:T(8,128)S(1)} %get-tuple-element.21), channel_id=1, source_target_pairs={{4,8},{8,4},{0,12},{12,0},{5,9},{9,5},{1,13},{13,1},{6,10},{10,6},... | collective-permute-start | bytes 36872 | tf_op jit(solution)/shard_map/ppermute | solution.py:465

commit v10 on v9

--- a/solution.py
+++ b/solution.py
@@ -395,9 +395,10 @@
     n_in = sum(counts[1:])
     across_ins, along_ins = by_axis(refs[:n_in], counts[1:])
     force_hbm, next_hbm, next_ref, sems = refs[n_in:]
-    copies = [pltpu.make_async_copy(force_ref, force_hbm, sems.at[3])]
+    copies = [pltpu.make_async_copy(force_ref, force_hbm, sems.at[0])]
     copies[0].start()
     depth, across, along = partial_ref.shape[1:]
+    ends = sorted({(depth + 1) // 2, depth})
     fold = source_ref.shape[1] // along
     half = across // fold
     even = parities()
@@ -439,8 +440,13 @@
             next_ref[c, h] = value
             next_ref[c, h, :SUBLANES, :] += jnp.where(subs == 0, across_low[k : k + 1, :], 0.0)
             next_ref[c, h, tail:, :] += jnp.where(subs == SUBLANES - 1, across_high[k : k + 1, :], 0.0)
-        copies.append(pltpu.make_async_copy(next_ref.at[c], next_hbm.at[c], sems.at[c]))
-        copies[-1].start()
+            if h + 1 in ends:
+                n = ends.index(h + 1)
+                done = pl.ds(ends[n - 1] if n else 0, ends[n] - (ends[n - 1] if n else 0))
+                copies.append(
+                    pltpu.make_async_copy(next_ref.at[c, done], next_hbm.at[c, done], sems.at[1 + 2 * c + n])
+                )
+                copies[-1].start()
     for copy in copies:
         copy.wait()
 
@@ -555,7 +561,7 @@
         ],
         in_specs=[vmem] * (3 + len(rest)),
         out_specs=[hbm, hbm],
-        scratch_shapes=[pltpu.VMEM(fluid.shape, F32), pltpu.SemaphoreType.DMA((4,))],
+        scratch_shapes=[pltpu.VMEM(fluid.shape, F32), pltpu.SemaphoreType.DMA((7,))],
         compiler_params=pltpu.CompilerParams(vmem_limit_bytes=GRANT),
         name="finish",
     )(*[kept(value) for value in [force, partial, source, *rest]])

time: 16 us -> 16 us (level)
  no operation moved by 1% of the time
where the time goes in v10:
time: 16 us; the launch traced here: 15.7 us
  starting transfers between devices  8.65 us (54%)
  Pallas kernels  6.38 us (40%)
  between operations  0.68 us (4%)
    ppermute x5, starting transfers between devices, exchange(): results.append(lax.ppermute(payload, axis, route))  8.65 us
    pallas_call x1, Pallas kernels, body(): pl.pallas_call(functools.partial(local_kernel, blocks, pairs), out_shape=...  3.76 us
    pallas_call x1, Pallas kernels, body(): pl.pallas_call(functools.partial(pack_kernel, counts), out_shape=[pltpu.S...  1.58 us
    pallas_call x1, Pallas kernels, body(): pl.pallas_call(functools.partial(finish_kernel, counts, [lax.axis_size(ax...  1.04 us
  transfers between devices with their start and end apart: 5, of which 0 were waited for; matrix products, arithmetic and copies ran while one was open for 0% of the time, Pallas kernels for 24%

profile of v10, /device:TPU:0, one launch (start us, length us, event | category | flops | bytes accessed | tf_op | source)
XLA Modules:
  0.0 15.7 jit_solution(8838434455009334627)
XLA Ops:
  0.6 1.6 %pack.1 = (s32[2,4]{1,0:T(2,128)S(4)}, f32[3,8,64,128]{3,2,1,0:T(8,128)S(1)}, f32[240,128]{1,0:T(8,128)S(1)}, f32[24,128]{1,0:T(8,128)S(1)}, f32[24,128]{1,0:T(8...) custom-call(s32[2,4]{1,0:T(2,128)} %bitcast.2, s32[2,2]{1,0:T(2,128)} %pair_hbm.1, f32[4,8,128]{2,1,0:T(8,128)} %part_hbm.1, ...), custom_call_target="tpu_custom_call" | custom-call | tf_op jit(solution)/shard_map/pack/pallas_call | solution.py:493
  2.2 0.6 %collective-permute-start = (f32[240,128]{1,0:T(8,128)S(1)}, f32[240,128]{1,0:T(8,128)S(1)}, u32[]{:S(2)}, u32[]{:S(2)}) collective-permute-start(f32[240,128]{1,0:T(8,128)S(1)} %get-tuple-element.16.refs_0_), channel_id=1, source_target_pairs={{0,16},{16,0},{1,17},{17,1},{2,18},{18,2},{3,19},{19,3},{4,20},{20... | collective-permute-start | bytes 368648 | tf_op jit(solution)/shard_map/ppermute | solution.py:471
  2.8 2.6 %collective-permute-start.3 = (f32[64,128]{1,0:T(8,128)S(1)}, f32[64,128]{1,0:T(8,128)S(1)}, u32[]{:S(2)}, u32[]{:S(2)}) collective-permute-start(f32[64,128]{1,0:T(8,128)S(1)} %get-tuple-element.22), channel_id=1, source_target_pairs={{0,1},{1,0},{2,3},{3,2},{4,5},{5,4},{6,7},{7,6},{8,9},{9,8},{10,11... | collective-permute-start | bytes 98312 | tf_op jit(solution)/shard_map/ppermute | solution.py:471
  5.4 2.5 %collective-permute-start.4 = (f32[64,128]{1,0:T(8,128)S(1)}, f32[64,128]{1,0:T(8,128)S(1)}, u32[]{:S(2)}, u32[]{:S(2)}) collective-permute-start(f32[64,128]{1,0:T(8,128)S(1)} %get-tuple-element.23), channel_id=1, source_target_pairs={{1,2},{2,1},{0,3},{3,0},{5,6},{6,5},{4,7},{7,4},{9,10},{10,9},{8,1... | collective-permute-start | bytes 98312 | tf_op jit(solution)/shard_map/ppermute | solution.py:471
  7.9 1.5 %collective-permute-start.1 = (f32[24,128]{1,0:T(8,128)S(1)}, f32[24,128]{1,0:T(8,128)S(1)}, u32[]{:S(2)}, u32[]{:S(2)}) collective-permute-start(f32[24,128]{1,0:T(8,128)S(1)} %get-tuple-element.20), channel_id=1, source_target_pairs={{0,4},{4,0},{8,12},{12,8},{1,5},{5,1},{9,13},{13,9},{2,6},{6,2},{1... | collective-permute-start | bytes 36872 | tf_op jit(solution)/shard_map/ppermute | solution.py:471
  9.4 1.5 %collective-permute-start.2 = (f32[24,128]{1,0:T(8,128)S(1)}, f32[24,128]{1,0:T(8,128)S(1)}, u32[]{:S(2)}, u32[]{:S(2)}) collective-permute-start(f32[24,128]{1,0:T(8,128)S(1)} %get-tuple-element.21), channel_id=1, source_target_pairs={{4,8},{8,4},{0,12},{12,0},{5,9},{9,5},{1,13},{13,1},{6,10},{10,6},... | collective-permute-start | bytes 36872 | tf_op jit(solution)/shard_map/ppermute | solution.py:471
  10.9 0.0 collective-permute-done.refs_1_
  10.9 3.8 %local.1 = (f32[3,4,128]{2,1,0:T(4,128)S(1)}, f32[3,8,64,128]{3,2,1,0:T(8,128)S(1)}, f32[768,256]{1,0:T(8,128)S(1)}) custom-call(s32[2,4]{1,0:T(2,128)S(4)} %get-tuple-element.14.pair_ref, f32[3,8,64,128]{3,2,1,0:T(8,128)S(1)} %get-tuple-element.15.fluid_ref, f32[240,128]{1,0:T(8,128)S(1)} %get-tuple-element.16.refs_0_, ...), custom_call_target="tpu_custom_call" | custom-call | tf_op jit(solution)/shard_map/local/pallas_call | solution.py:522
  14.6 0.0 collective-permute-done.1.refs_0_
  14.7 0.0 collective-permute-done.2.refs_1_
  14.7 0.0 collective-permute-done.3.refs_2_
  14.7 0.0 collective-permute-done.4.refs_3_
  14.7 1.0 %finish.1 = (f32[3,4,128]{2,1,0:T(4,128)}, f32[3,8,64,128]{3,2,1,0:T(8,128)}) custom-call(f32[3,4,128]{2,1,0:T(4,128)S(1)} %get-tuple-element.17.force_ref, f32[3,8,64,128]{3,2,1,0:T(8,128)S(1)} %get-tuple-element.18.partial_ref, f32[768,256]{1,0:T(8,128)S(1)} %get-tuple-element.19.source_ref, f32[24,128]{1,0:T(8,128)S(1)} %collective-permute-done.1.refs_0_, ...), custom_call_target="tpu_custom_call" | custom-call | tf_op jit(solution)/shard_map/finish/pallas_call | solution.py:556
Async XLA Ops:
  2.2 8.7 %collective-permute-start = (f32[240,128]{1,0:T(8,128)S(1)}, f32[240,128]{1,0:T(8,128)S(1)}, u32[]{:S(2)}, u32[]{:S(2)}) collective-permute-start(f32[240,128]{1,0:T(8,128)S(1)} %get-tuple-element.16.refs_0_), channel_id=1, source_target_pairs={{0,16},{16,0},{1,17},{17,1},{2,18},{18,2},{3,19},{19,3},{4,20},{20... | collective-permute-start | bytes 368648 | tf_op jit(solution)/shard_map/ppermute | solution.py:471
  2.8 11.9 %collective-permute-start.3 = (f32[64,128]{1,0:T(8,128)S(1)}, f32[64,128]{1,0:T(8,128)S(1)}, u32[]{:S(2)}, u32[]{:S(2)}) collective-permute-start(f32[64,128]{1,0:T(8,128)S(1)} %get-tuple-element.22), channel_id=1, source_target_pairs={{0,1},{1,0},{2,3},{3,2},{4,5},{5,4},{6,7},{7,6},{8,9},{9,8},{10,11... | collective-permute-start | bytes 98312 | tf_op jit(solution)/shard_map/ppermute | solution.py:471
  5.4 9.3 %collective-permute-start.4 = (f32[64,128]{1,0:T(8,128)S(1)}, f32[64,128]{1,0:T(8,128)S(1)}, u32[]{:S(2)}, u32[]{:S(2)}) collective-permute-start(f32[64,128]{1,0:T(8,128)S(1)} %get-tuple-element.23), channel_id=1, source_target_pairs={{1,2},{2,1},{0,3},{3,0},{5,6},{6,5},{4,7},{7,4},{9,10},{10,9},{8,1... | collective-permute-start | bytes 98312 | tf_op jit(solution)/shard_map/ppermute | solution.py:471
  7.9 6.8 %collective-permute-start.1 = (f32[24,128]{1,0:T(8,128)S(1)}, f32[24,128]{1,0:T(8,128)S(1)}, u32[]{:S(2)}, u32[]{:S(2)}) collective-permute-start(f32[24,128]{1,0:T(8,128)S(1)} %get-tuple-element.20), channel_id=1, source_target_pairs={{0,4},{4,0},{8,12},{12,8},{1,5},{5,1},{9,13},{13,9},{2,6},{6,2},{1... | collective-permute-start | bytes 36872 | tf_op jit(solution)/shard_map/ppermute | solution.py:471
  9.4 5.3 %collective-permute-start.2 = (f32[24,128]{1,0:T(8,128)S(1)}, f32[24,128]{1,0:T(8,128)S(1)}, u32[]{:S(2)}, u32[]{:S(2)}) collective-permute-start(f32[24,128]{1,0:T(8,128)S(1)} %get-tuple-element.21), channel_id=1, source_target_pairs={{4,8},{8,4},{0,12},{12,0},{5,9},{9,5},{1,13},{13,1},{6,10},{10,6},... | collective-permute-start | bytes 36872 | tf_op jit(solution)/shard_map/ppermute | solution.py:471
